TPU v7x, 32 devices: a whole 2x2x4 slice. The times are simulated.
32 devices in a mesh: grp: 2 (over x), row: 8 (over z, y), col: 2 (over core).
Axes of the slice: x: 2, y: 2, z: 4, core: 2. Of those that a mesh axis runs over, the one named last changes fastest.
Arguments:
- tokens: int32 [1024, 256], P(('grp', 'row', 'col')), parts along dimension 0, may hold values from 0 to 20
- gap_mask: int32 [1024, 256], P(('grp', 'row', 'col')), parts along dimension 0, may hold values 0 or 1
- dilations: int32 [4], replicated, may hold values from 1 to 4, as said below
- embedding: float32 [21, 64], replicated, may hold values from -6 to 6
- residue_filters: float32 [2, 3, 64, 64], replicated, may hold values from -0.4375 to 0.4375
- projection: bfloat16 [4096, 128], replicated, may hold values from -0.09375 to 0.09375
- pair_filters: bfloat16 [2, 3, 3, 128, 128], replicated, may hold values from -0.1875 to 0.1875
Outputs:
- pair_map: bfloat16 [512, 256, 128], P(('grp', 'row'), 'col'), parts along dimension 0
There are 2 independent parts, one for each index of `grp`. A program takes and returns all parts, laid end to end along the dimension named above; an argument that names none is the same for every part. Nothing has to cross between parts.
Inputs may be any that keep to these rules, and one draw needn't show every extreme that they name: `dilations`: at least one layer has dilation 4.
All inputs are finite; a program needn't handle non-finite values. No bound on the sum of `gap_mask` on one device may be relied on, other than what follows from the above.
Results may differ from a plain program's by a relative error of at most 0.0066.
Values may be sent and summed in bfloat16 or wider, within the bound.
No kernel may reach another device: no remote copies, remote signals or barrier semaphores. Data moves between devices by JAX's collectives and lax.ppermute only.
A program may use at most 128 MiB of HBM per device.

v0:
```python
import functools

import jax
import jax.numpy as jnp
from jax import lax
from jax.experimental import pallas as pl
from jax.experimental.pallas import tpu as pltpu
from jax.sharding import PartitionSpec as P


NL1 = 2
DMAX = 4
HALO = 2 * DMAX
BLOCK = 16
VMEM_LIMIT = 62 << 20


def elu(x):
    return jnp.maximum(x, jnp.exp(jnp.minimum(x, 0.0)) - 1.0)


def contract_last(left, right):
    return lax.dot_general(
        left, right, (((1,), (1,)), ((), ())), preferred_element_type=jnp.float32
    )


def exchange(block, axis, bit):
    count = lax.axis_size(axis)
    return lax.ppermute(block, axis, [(i, i ^ bit) for i in range(count)])


def first_sequences(tokens, gap_mask):
    half = jnp.stack([tokens, gap_mask]).astype(jnp.bfloat16)[None]
    bit = lax.axis_size("row") // 4
    while bit >= 1:
        half = jnp.concatenate([half, exchange(half, "row", bit)])
        bit //= 2
    return half


def feature_tables(embedding, filters):
    letters, channels = embedding.shape
    kinds = -(-letters // 32) * 32
    padded = jnp.pad(embedding, ((0, kinds - letters), (0, 0)))
    mixed = jnp.einsum("koc,tc->okt", filters[0], padded, precision=lax.Precision.HIGHEST)
    plain = jnp.zeros_like(mixed).at[:, 1, :].set(padded.T)
    table = jnp.concatenate([mixed, plain], axis=0).reshape(2 * channels, 3 * kinds)
    high = table.astype(jnp.bfloat16)
    low = (table - high.astype(jnp.float32)).astype(jnp.bfloat16)
    second = filters[1].transpose(1, 0, 2).reshape(channels, 3 * channels).astype(jnp.bfloat16)
    return jnp.concatenate([high, low], axis=1), second


def feature_kernel(
    scalars, here_ref, there_ref, table_ref, second_ref, row_ref, col_ref, row_mark_ref, col_mark_ref,
    token_s, mark_s, onehot_s, hidden_s, narrow_s, turn_s, stage_s, sems, *, pitch,
):
    first_spread, second_spread, row_first, col_first = scalars[0], scalars[1], scalars[2], scalars[3]
    blocks, _, each, length = here_ref.shape
    part = blocks * each
    width = 2 * part
    channels = second_ref.shape[0]
    kinds = onehot_s.shape[1]
    rows, cols = row_ref.shape[0], col_ref.shape[1]
    lanes = 128
    for side, ref in enumerate((here_ref, there_ref)):
        at = slice(side * part, (side + 1) * part)
        token_s[HALO : HALO + length, at] = ref[:, 0].reshape(part, length).astype(jnp.float32).T
        mark_s[:, at] = ref[:, 1].reshape(part, length).astype(jnp.float32).T
    edge = jnp.full((HALO, width), -1.0, jnp.float32)
    token_s[0:HALO, :] = edge
    token_s[HALO + length : 2 * HALO + length, :] = edge
    row_mark_ref[...] = mark_s[pl.ds(pl.multiple_of(row_first, 8), rows), :].astype(row_mark_ref.dtype)
    col_mark_ref[...] = mark_s[pl.ds(pl.multiple_of(col_first, 8), cols), :].astype(col_mark_ref.dtype)
    letters = lax.broadcasted_iota(jnp.int32, (kinds, width), 0).astype(jnp.float32)
    table = table_ref[...]
    second = second_ref[...]

    def layer_one(start, count):
        for k in range(count):
            at = start + k
            taps = jnp.concatenate([onehot_s[at - first_spread], onehot_s[at], onehot_s[at + first_spread]], axis=0)
            mixing = jnp.dot(table, jnp.concatenate([taps, taps], axis=0), preferred_element_type=jnp.float32)
            hidden = mixing[channels:] + elu(mixing[:channels])
            hidden_s[at] = hidden
            narrow_s[at] = hidden.astype(narrow_s.dtype)

    def run(first, count, emit, finish):
        def hot(step, carry):
            block = token_s[pl.ds(pl.multiple_of(first + step * 8, 8), 8), :]
            for k in range(8):
                onehot_s[step * 8 + k] = jnp.where(block[k : k + 1, :] == letters, 1.0, 0.0).astype(onehot_s.dtype)
            return carry

        lax.fori_loop(0, (count + 2 * HALO) // 8, hot, 0)

        def layer_two(step):
            marks = mark_s[pl.ds(pl.multiple_of(first + step * BLOCK, 8), BLOCK), :]
            for k in range(BLOCK):
                at = HALO + step * BLOCK + k
                taps = jnp.concatenate(
                    [narrow_s[at - second_spread], narrow_s[at], narrow_s[at + second_spread]], axis=0
                )
                mixing = jnp.dot(second, taps, preferred_element_type=jnp.float32)
                emit(step, k, (hidden_s[at] + elu(mixing)) * marks[k : k + 1, :])
            finish(step)

        def clear(starts):
            for start in starts:
                for k in range(DMAX):
                    place = first - HALO + start + k

                    @pl.when((place < 0) | (place >= length))
                    def _():
                        narrow_s[start + k] = jnp.zeros((channels, width), narrow_s.dtype)

        ahead = BLOCK + 2 * DMAX
        layer_one(DMAX, ahead)
        clear((DMAX,))

        def trip(step, carry):
            layer_two(step)
            layer_one(DMAX + ahead + step * BLOCK, BLOCK)
            return carry

        lax.fori_loop(0, count // BLOCK - 1, trip, 0)
        clear((count + HALO,))
        layer_two(count // BLOCK - 1)

    def emit_row(step, k, value):
        row_ref[step * BLOCK + k] = value.astype(row_ref.dtype)

    def emit_col(step, k, value):
        for piece in range(width // lanes):
            turn_s[pl.ds(piece * channels * pitch + k, channels, stride=pitch), :] = value[
                :, piece * lanes : (piece + 1) * lanes
            ]

    def leave(step):
        slot = lax.rem(step, 2)
        start = pl.multiple_of(step * BLOCK, BLOCK)
        return pltpu.make_async_copy(stage_s.at[slot], col_ref.at[:, pl.ds(start, BLOCK), :], sems.at[slot])

    def finish_col(step):
        @pl.when(step >= 2)
        def _():
            leave(step - 2).wait()

        slot = lax.rem(step, 2)
        for channel in range(channels):
            for piece in range(width // lanes):
                start = (piece * channels + channel) * pitch
                stage_s[slot, channel, :, piece * lanes : (piece + 1) * lanes] = turn_s[
                    start : start + BLOCK, :
                ].astype(stage_s.dtype)
        leave(step).start()

    run(row_first, rows, emit_row, lambda step: None)
    run(col_first, cols, emit_col, finish_col)
    steps = cols // BLOCK
    for step in range(max(steps - 2, 0), steps):
        leave(step).wait()


def features(scalars, here, there, table, second, rows, cols):
    blocks, _, each, length = here.shape
    width = 2 * blocks * each
    channels = second.shape[0]
    kinds = table.shape[1] // 6
    span = max(rows, cols) + 2 * HALO
    pitch = BLOCK + 8
    bf16, f32 = jnp.bfloat16, jnp.float32
    full = lambda shape: pl.BlockSpec(shape, functools.partial(lambda rank, g, s: (0,) * rank, len(shape)))
    return pl.pallas_call(
        functools.partial(feature_kernel, pitch=pitch),
        grid_spec=pltpu.PrefetchScalarGridSpec(
            num_scalar_prefetch=1,
            grid=(1,),
            in_specs=[full(x.shape) for x in (here, there, table, second)],
            out_specs=[
                full((rows, channels, width)),
                pl.BlockSpec(memory_space=pl.ANY),
                full((rows, width)),
                full((cols, width)),
            ],
            scratch_shapes=[
                pltpu.VMEM((length + 2 * HALO, width), f32),
                pltpu.VMEM((length, width), f32),
                pltpu.VMEM((span, kinds, width), bf16),
                pltpu.VMEM((span, channels, width), f32),
                pltpu.VMEM((span, channels, width), bf16),
                pltpu.VMEM((width // 128 * channels * pitch, 128), f32),
                pltpu.VMEM((2, channels, BLOCK, width), bf16),
                pltpu.SemaphoreType.DMA((2,)),
            ],
        ),
        out_shape=[
            jax.ShapeDtypeStruct((rows, channels, width), bf16),
            jax.ShapeDtypeStruct((channels, cols, width), bf16),
            jax.ShapeDtypeStruct((rows, width), bf16),
            jax.ShapeDtypeStruct((cols, width), bf16),
        ],
        compiler_params=pltpu.CompilerParams(vmem_limit_bytes=VMEM_LIMIT),
        cost_estimate=pl.CostEstimate(
            flops=40 * channels * channels * width * (rows + cols),
            bytes_accessed=2 * channels * width * (rows + cols),
            transcendentals=2 * channels * width * (rows + cols),
        ),
    )(scalars, here, there, table, second)


def outer_kernel(scalars, *refs, picks, halves, swap):
    count = len(picks)
    row_refs = refs[: halves * count]
    col_refs = refs[halves * count : halves * (count + 1)]
    projection_ref = refs[halves * (count + 1)]
    marks = refs[halves * (count + 1) + 1 : -(count + 2)]
    pair_refs = refs[-(count + 2) : -2]
    edge_ref, sum_s = refs[-2:]
    step = pl.program_id(0)
    group, cols, _ = col_refs[0].shape
    channels = row_refs[0].shape[1]
    rows = count * HALO

    @pl.when(step == 0)
    def _():
        sum_s[...] = jnp.zeros_like(sum_s)

    right = jnp.concatenate([ref[...].reshape(group * cols, ref.shape[2]) for ref in col_refs], axis=1)
    left = jnp.concatenate(
        [
            jnp.concatenate([row_refs[p * halves + h][...].reshape(HALO * channels, -1) for h in range(halves)], axis=1)
            for p in range(count)
        ],
        axis=0,
    )
    projection = projection_ref[...]
    outer = contract_last(left, right).astype(jnp.bfloat16)
    for pair in range(0, rows, 2):
        sides = [
            jnp.concatenate(
                [outer[i * channels : (i + 1) * channels, b * cols : (b + 1) * cols] for b in range(group)], axis=0
            )
            for i in (pair, pair + 1)
        ]
        sum_s[pair // 2] += jnp.dot(
            projection, jnp.concatenate(sides, axis=1), preferred_element_type=jnp.float32
        )

    @pl.when(step == pl.num_programs(0) - 1)
    def _():
        row_marks, col_marks = marks[:halves], marks[halves:]
        counts = sum(contract_last(r[...], c[...]) for r, c in zip(row_marks, col_marks))
        share = 1.0 / (counts + 1.0)
        for p, pick in enumerate(picks):
            for k in range(HALO):
                i = p * HALO + k
                place = pick * HALO + k
                value = sum_s[i // 2][:, (i % 2) * cols : (i % 2 + 1) * cols] * share[place : place + 1, :]
                value = value.T
                pair_refs[p][k] = value.astype(edge_ref.dtype)
                if swap:
                    edge_ref[i] = jnp.where(scalars[0] == 0, value[cols - HALO :], value[:HALO]).astype(edge_ref.dtype)
        if not swap:
            edge_ref[...] = jnp.zeros_like(edge_ref)


def outer_products(scalars, row_feats, col_feats, projection, row_marks, col_marks, picks, swap, group=8):
    _, channels, _ = row_feats[0].shape
    cols = col_feats[0].shape[1]
    out = projection.shape[0]
    total = sum(x.shape[2] for x in row_feats)
    tall = len(picks) * HALO
    full = lambda shape: pl.BlockSpec(shape, functools.partial(lambda rank, g, s: (0,) * rank, len(shape)))
    picked = lambda pick, width: pl.BlockSpec((HALO, channels, width), lambda g, s: (pick, 0, 0))
    results = pl.pallas_call(
        functools.partial(outer_kernel, picks=picks, halves=len(row_feats), swap=swap),
        grid_spec=pltpu.PrefetchScalarGridSpec(
            num_scalar_prefetch=1,
            grid=(channels // group,),
            in_specs=[picked(pick, x.shape[2]) for pick in picks for x in row_feats]
            + [pl.BlockSpec((group, cols, x.shape[2]), lambda g, s: (g, 0, 0)) for x in col_feats]
            + [pl.BlockSpec((out, group * channels), lambda g, s: (0, g))]
            + [full(x.shape) for x in (*row_marks, *col_marks)],
            out_specs=[full((HALO, cols, out)) for _ in picks] + [full((tall, HALO, out))],
            scratch_shapes=[pltpu.VMEM((tall // 2, out, 2 * cols), jnp.float32)],
        ),
        out_shape=[jax.ShapeDtypeStruct((HALO, cols, out), jnp.bfloat16) for _ in picks]
        + [jax.ShapeDtypeStruct((tall, HALO, out), jnp.bfloat16)],
        compiler_params=pltpu.CompilerParams(vmem_limit_bytes=VMEM_LIMIT),
        cost_estimate=pl.CostEstimate(
            flops=2 * tall * cols * channels * channels * (total + out),
            bytes_accessed=2 * channels * total * (tall + cols),
            transcendentals=0,
        ),
    )(
        scalars,
        *[x for _ in picks for x in row_feats],
        *col_feats,
        projection,
        *row_marks,
        *col_marks,
    )
    return list(results[:-1]), results[-1]


def conv_kernel(scalars, *refs, length, swap):
    first_spread, second_spread, row_first, col_first = scalars[0], scalars[1], scalars[2], scalars[3]
    row_refs = refs[:-8]
    left_ref, right_ref, edge_ref, filter_ref, out_ref, wide_s, tap_s, hidden_s = refs[-8:]
    rows, cols, channels = out_ref.shape
    tall, broad = rows + 2 * DMAX, cols + 2 * DMAX
    f32, bf16 = jnp.float32, jnp.bfloat16
    for block, ref in enumerate(row_refs):
        wide_s[block * HALO : (block + 1) * HALO, HALO : HALO + cols, :] = ref[...].astype(f32)
    if swap:
        edges = edge_ref[...].astype(f32)
        wide_s[:, 0:HALO, :] = jnp.where(col_first == 0, jnp.zeros_like(edges), edges)
        wide_s[:, HALO + cols : 2 * HALO + cols, :] = jnp.where(col_first == 0, edges, jnp.zeros_like(edges))
    else:
        wide_s[:, 0:HALO, :] = left_ref[...].astype(f32)
        wide_s[:, HALO + cols : 2 * HALO + cols, :] = right_ref[...].astype(f32)

    def spread_taps(source, count, start, spread, width):
        def body(i, carry):
            for tap in range(3):
                piece = source[i, pl.ds(start + (tap - 1) * spread, width), :]
                tap_s[i, 0:width, tap * channels : (tap + 1) * channels] = piece.astype(bf16)
            return carry

        lax.fori_loop(0, count, body, 0)

    spread_taps(wide_s, rows + 2 * HALO, DMAX, first_spread, broad)
    first = filter_ref[0]
    places = col_first - DMAX + lax.broadcasted_iota(jnp.int32, (broad, channels), 0)
    col_inside = ((places >= 0) & (places < length)).astype(f32)

    def one(i, carry):
        at = i + DMAX
        taps = jnp.concatenate(
            [tap_s[at - first_spread, 0:broad], tap_s[at, 0:broad], tap_s[at + first_spread, 0:broad]], axis=1
        )
        mixing = elu(jnp.dot(taps, first, preferred_element_type=f32)).astype(bf16).astype(f32)
        place = row_first - DMAX + i
        hidden_s[i] = mixing * col_inside * jnp.where((place >= 0) & (place < length), 1.0, 0.0)
        return carry

    lax.fori_loop(0, tall, one, 0, unroll=4)
    spread_taps(hidden_s, tall, DMAX, second_spread, cols)
    second = filter_ref[1]

    def two(i, carry):
        at = i + DMAX
        taps = jnp.concatenate(
            [tap_s[at - second_spread, 0:cols], tap_s[at, 0:cols], tap_s[at + second_spread, 0:cols]], axis=1
        )
        mixing = jnp.dot(taps, second, preferred_element_type=f32)
        own = wide_s[i + HALO, HALO : HALO + cols, :]
        out_ref[i] = (own + mixing).astype(out_ref.dtype)
        return carry

    lax.fori_loop(0, rows, two, 0, unroll=4)


def pair_convolutions(scalars, blocks, left, right, edges, filters, length, swap):
    cols, channels = blocks[0].shape[1:]
    rows = (len(blocks) - 2) * HALO
    tall, broad = rows + 2 * HALO, cols + 2 * HALO
    operands = (*blocks, left, right, edges, filters)
    full = lambda shape: pl.BlockSpec(shape, functools.partial(lambda rank, g, s: (0,) * rank, len(shape)))
    return pl.pallas_call(
        functools.partial(conv_kernel, length=length, swap=swap),
        grid_spec=pltpu.PrefetchScalarGridSpec(
            num_scalar_prefetch=1,
            grid=(1,),
            in_specs=[full(x.shape) for x in operands],
            out_specs=full((rows, cols, channels)),
            scratch_shapes=[
                pltpu.VMEM((tall, broad, channels), jnp.float32),
                pltpu.VMEM((tall, broad - 2 * DMAX, 3 * channels), jnp.bfloat16),
                pltpu.VMEM((tall - 2 * DMAX, broad - 2 * DMAX, channels), jnp.float32),
            ],
        ),
        out_shape=jax.ShapeDtypeStruct((rows, cols, channels), jnp.bfloat16),
        compiler_params=pltpu.CompilerParams(vmem_limit_bytes=VMEM_LIMIT),
    )(scalars, *operands)


def col_margins(tall):
    steps = range(lax.axis_size("col") - 1)
    head, tail = tall[:, :HALO], tall[:, tall.shape[1] - HALO :]
    return (
        lax.ppermute(tail, "col", [(i, i + 1) for i in steps]),
        lax.ppermute(head, "col", [(i + 1, i) for i in steps]),
    )


def per_device(tokens, gap_mask, dilations, embedding, residue_filters, projection, pair_filters):
    length = tokens.shape[1]
    channels = embedding.shape[1]
    out = projection.shape[1]
    row_count, col_count = lax.axis_size("row"), lax.axis_size("col")
    rows, cols = length // row_count, length // col_count
    col_index = lax.axis_index("col")
    starts = jnp.stack([lax.axis_index("row") * rows, col_index * cols]).astype(jnp.int32)
    col_scalar = col_index.astype(jnp.int32).reshape(1)
    swap = col_count == 2
    near = first_sequences(tokens, gap_mask)
    near_there = exchange(near, "col", 1)
    far = exchange(near, "row", row_count // 2)
    far_there = exchange(far, "col", 1)
    table, second = feature_tables(embedding, residue_filters)
    turned = projection.reshape(channels, channels, out).transpose(2, 1, 0).reshape(out, channels * channels)
    scalars = jnp.concatenate([dilations[:NL1], starts])
    near_parts = features(scalars, near, near_there, table, second, rows, cols)
    far_parts = features(scalars, far, far_there, table, second, rows, cols)
    row_feats, col_feats, row_marks, col_marks = zip(near_parts, far_parts)
    last = rows // HALO - 1
    run = functools.partial(outer_products, col_scalar, row_feats, col_feats, turned, row_marks, col_marks, swap=swap)
    ends, end_edges = run(picks=(0, last))
    steps = range(row_count - 1)
    above = lax.ppermute(ends[1], "row", [(i, i + 1) for i in steps])
    below = lax.ppermute(ends[0], "row", [(i + 1, i) for i in steps])
    if last > 1:
        middle, middle_edges = run(picks=tuple(range(1, last)))
    else:
        middle, middle_edges = [], end_edges[:0]
    blocks = [above, ends[0], *middle, ends[1], below]
    if swap:
        pick = lambda block: jnp.where(col_index == 0, block[:, cols - HALO :], block[:, :HALO])
        edges = jnp.concatenate([pick(above), end_edges[:HALO], middle_edges, end_edges[HALO:], pick(below)])
        edges = exchange(edges, "col", 1)
        left = right = edges[:1]
    else:
        left, right = col_margins(jnp.concatenate(blocks))
        edges = left[:1]
    return pair_convolutions(
        jnp.concatenate([dilations[NL1:], starts]),
        blocks, left, right, edges,
        pair_filters.reshape(2, 9 * pair_filters.shape[3], pair_filters.shape[4]),
        length,
        swap,
    )


def solution(mesh):
    in_specs = (
        P(("grp", "row", "col"), None),
        P(("grp", "row", "col"), None),
        P(),
        P(),
        P(),
        P(),
        P(),
    )
    out_specs = P(("grp", "row"), "col", None)
    return jax.shard_map(per_device, mesh=mesh, in_specs=in_specs, out_specs=out_specs, check_vma=False)
```

profile of v0, /device:TPU:0, one launch (start us, length us, event | category | flops | bytes accessed | tf_op | source)
XLA Modules:
  0.0 113.8 jit_solution(5219193769593072156)
XLA Ops:
  0.0 0.8 convert_bitcast_fusion
  0.8 3.1 %collective-permute-start = (bf16[1,2,32,256]{3,2,1,0:T(8,128)(2,1)S(1)}, bf16[1,2,32,256]{3,2,1,0:T(8,128)(2,1)S(1)}, u32[]{:S(2)}, u32[]{:S(2)}) collective-permute-start(bf16[1,2,32,256]{3,2,1,0:T(8,128)(2,1)S(1)} %pad_maximum_fusion.3), channel_id=1, source_target_pairs={{0,4},{2,6},{4,0},{6,2},{8,12},{10,14},{12,8},{14,10},{1,5},{3,7},... | collective-permute-start | bytes 98312 | tf_op jit(solution)/shard_map/ppermute | solution.py:30
  3.9 0.7 pad_bitcast_fusion
  4.6 1.2 %convolution_bitcast_fusion = f32[64,3,32]{0,2,1:T(8,128)S(1)} fusion(f32[2,3,64,64]{3,2,1,0:T(8,128)} %param.13, f32[21,64]{1,0:T(8,128)} %param.12), kind=kOutput, calls=%fused_computation | convolution fusion | flops 4718592 | bytes 135168 | tf_op jit(solution)/shard_map/koc,tc->okt/dot_general | solution.py:46
  5.9 0.9 fusion.2
  7.1 1.6 %collective-permute-start.1 = (bf16[2,2,32,256]{3,2,1,0:T(8,128)(2,1)S(1)}, bf16[2,2,32,256]{3,2,1,0:T(8,128)(2,1)S(1)}, u32[]{:S(2)}, u32[]{:S(2)}) collective-permute-start(bf16[2,2,32,256]{3,2,1,0:T(8,128)(2,1)S(1)} %pad_maximum_fusion.1), channel_id=1, source_target_pairs={{0,2},{2,0},{4,6},{6,4},{8,10},{10,8},{12,14},{14,12},{1,3},{3,1},... | collective-permute-start | bytes 196616 | tf_op jit(solution)/shard_map/ppermute | solution.py:30
  8.7 0.8 fusion.6
  9.5 1.9 %collective-permute-done.1 = bf16[2,2,32,256]{3,2,1,0:T(8,128)(2,1)S(1)} collective-permute-done((bf16[2,2,32,256]{3,2,1,0:T(8,128)(2,1)S(1)}, bf16[2,2,32,256]{3,2,1,0:T(8,128)(2,1)S(1)}, u32[]{:S(2)}, u32[]{:S(2)}) %collective-permute-start.1) | collective-permute-done | bytes 65568 | tf_op jit(solution)/shard_map/ppermute | solution.py:30
  11.5 2.7 %collective-permute-start.3 = (bf16[4,2,32,256]{3,2,1,0:T(8,128)(2,1)S(1)}, bf16[4,2,32,256]{3,2,1,0:T(8,128)(2,1)S(1)}, u32[]{:S(2)}, u32[]{:S(2)}) collective-permute-start(bf16[4,2,32,256]{3,2,1,0:T(8,128)(2,1)S(1)} %pad_maximum_fusion.here_ref), channel_id=1, source_target_pairs={{0,8},{2,10},{4,12},{6,14},{8,0},{10,2},{12,4},{14,6},{1,9},{3,11}... | collective-permute-start | bytes 393224 | tf_op jit(solution)/shard_map/ppermute | solution.py:30
  14.9 0.7 copy.30.second_ref
  15.6 1.9 %copy.32 = bf16[128,64,64]{0,2,1:T(8,128)(2,1)S(1)} copy(bf16[128,64,64]{0,1,2:T(8,128)(2,1)} %bitcast.32) | data formatting | bytes 2097152 | tf_op jit(solution)/shard_map/transpose | solution.py:414
  17.5 1.4 %copy.33.refs_6_ = bf16[128,4096]{1,0:T(8,128)(2,1)} copy(bf16[128,4096]{0,1:T(8,128)(2,1)S(1)} %bitcast.31) | data formatting | bytes 2097152 | tf_op jit(solution)/shard_map/reshape | solution.py:414
  18.9 0.7 pad_maximum_fusion.2.table_ref
  20.1 0.7 copy-done.7
  20.8 14.5 %shard_map.73 = (bf16[32,64,256]{2,1,0:T(8,128)(2,1)}, bf16[64,128,256]{2,1,0:T(8,128)(2,1)}, bf16[32,256]{1,0:T(8,128)(2,1)}, bf16[128,256]{1,0:T(8,128)(2,1)}) custom-call(s32[4]{0:T(128)} %add_add_fusion.1.scalars, bf16[4,2,32,256]{3,2,1,0:T(8,128)(2,1)} %copy-done.3, bf16[4,2,32,256]{3,2,1,0:T(8,128)(2,1)} %copy-done.7, ...), custom_call_target="tpu_custom_call" | custom-call | flops 6710886400 | bytes 5242880 | tf_op jit(solution)/shard_map/pallas_call | solution.py:175
  36.0 14.5 %shard_map.74 = (bf16[32,64,256]{2,1,0:T(8,128)(2,1)}, bf16[64,128,256]{2,1,0:T(8,128)(2,1)}, bf16[32,256]{1,0:T(8,128)(2,1)}, bf16[128,256]{1,0:T(8,128)(2,1)}) custom-call(s32[4]{0:T(128)} %add_add_fusion.1.scalars, bf16[4,2,32,256]{3,2,1,0:T(8,128)(2,1)} %copy-done.6, bf16[4,2,32,256]{3,2,1,0:T(8,128)(2,1)} %copy-done.8, ...), custom_call_target="tpu_custom_call" | custom-call | flops 6710886400 | bytes 5242880 | tf_op jit(solution)/shard_map/pallas_call | solution.py:175
  50.5 16.5 %shard_map.75 = (bf16[8,128,128]{2,1,0:T(8,128)(2,1)}, bf16[8,128,128]{2,1,0:T(8,128)(2,1)}, bf16[16,8,128]{2,1,0:T(8,128)(2,1)}) custom-call(s32[1]{0:T(128)} %bitcast.2.scalars, bf16[32,64,256]{2,1,0:T(8,128)(2,1)} %get-tuple-element.31.refs_0_.refs_2_, bf16[32,64,256]{2,1,0:T(8,128)(2,1)} %get-tuple-element.32.refs_1_.refs_3_, ...), custom_call_target="tpu_custom_call" | custom-call | flops 10737418240 | bytes 9437184 | tf_op jit(solution)/shard_map/pallas_call | solution.py:277
  67.0 3.8 %collective-permute-start.5 = (bf16[8,128,128]{2,1,0:T(8,128)(2,1)}, bf16[8,128,128]{2,1,0:T(8,128)(2,1)S(1)}, u32[]{:S(2)}, u32[]{:S(2)}) collective-permute-start(bf16[8,128,128]{2,1,0:T(8,128)(2,1)} %get-tuple-element.39.refs_4_), channel_id=1, source_target_pairs={{0,2},{2,4},{4,6},{6,8},{8,10},{10,12},{12,14},{1,3},{3,5},{5,7},{... | collective-permute-start | bytes 786440 | tf_op jit(solution)/shard_map/ppermute | solution.py:423
  70.8 16.5 %shard_map.76 = (bf16[8,128,128]{2,1,0:T(8,128)(2,1)}, bf16[8,128,128]{2,1,0:T(8,128)(2,1)}, bf16[16,8,128]{2,1,0:T(8,128)(2,1)}) custom-call(s32[1]{0:T(128)} %bitcast.2.scalars, bf16[32,64,256]{2,1,0:T(8,128)(2,1)} %get-tuple-element.31.refs_0_.refs_2_, bf16[32,64,256]{2,1,0:T(8,128)(2,1)} %get-tuple-element.32.refs_1_.refs_3_, ...), custom_call_target="tpu_custom_call" | custom-call | flops 10737418240 | bytes 9437184 | tf_op jit(solution)/shard_map/pallas_call | solution.py:277
  87.3 1.3 %collective-permute-start.6 = (bf16[8,128,128]{2,1,0:T(8,128)(2,1)S(1)}, bf16[8,128,128]{2,1,0:T(8,128)(2,1)S(1)}, u32[]{:S(2)}, u32[]{:S(2)}) collective-permute-start(bf16[8,128,128]{2,1,0:T(8,128)(2,1)S(1)} %copy-done.2), channel_id=1, source_target_pairs={{2,0},{4,2},{6,4},{8,6},{10,8},{12,10},{14,12},{3,1},{5,3},{7,5},{... | collective-permute-start | bytes 786440 | tf_op jit(solution)/shard_map/ppermute | solution.py:424
  88.6 0.8 constant_dynamic-update-slice_fusion
  89.4 7.7 %collective-permute-done.6.refs_5_ = bf16[8,128,128]{2,1,0:T(8,128)(2,1)S(1)} collective-permute-done((bf16[8,128,128]{2,1,0:T(8,128)(2,1)S(1)}, bf16[8,128,128]{2,1,0:T(8,128)(2,1)S(1)}, u32[]{:S(2)}, u32[]{:S(2)}) %collective-permute-start.6) | collective-permute-done | bytes 262176 | tf_op jit(solution)/shard_map/ppermute | solution.py:424
  97.8 0.7 collective-permute-done.7.refs_8_
  99.2 14.6 %shard_map.77 = bf16[32,128,128]{2,1,0:T(8,128)(2,1)} custom-call(s32[4]{0:T(128)} %add_add_fusion.scalars, bf16[8,128,128]{2,1,0:T(8,128)(2,1)} %copy-done, bf16[8,128,128]{2,1,0:T(8,128)(2,1)} %get-tuple-element.40.refs_1_, bf16[8,128,128]{2,1,0:T(8,128)(2,1)} %get-tuple-element.41.refs_2_, bf16[8,128,128]{2,1,0:T(8,128)(2,1)} %get-tuple-element.42.refs_3_, ...), custom_call_target="tpu_custom_call" | custom-call | tf_op jit(solution)/shard_map/pallas_call | solution.py:372
  (41 shorter events, 3.6 us)
Async XLA Ops:
  0.8 6.3 %collective-permute-start = (bf16[1,2,32,256]{3,2,1,0:T(8,128)(2,1)S(1)}, bf16[1,2,32,256]{3,2,1,0:T(8,128)(2,1)S(1)}, u32[]{:S(2)}, u32[]{:S(2)}) collective-permute-start(bf16[1,2,32,256]{3,2,1,0:T(8,128)(2,1)S(1)} %pad_maximum_fusion.3), channel_id=1, source_target_pairs={{0,4},{2,6},{4,0},{6,2},{8,12},{10,14},{12,8},{14,10},{1,5},{3,7},... | collective-permute-start | bytes 98312 | tf_op jit(solution)/shard_map/ppermute | solution.py:30
  7.1 4.3 %collective-permute-start.1 = (bf16[2,2,32,256]{3,2,1,0:T(8,128)(2,1)S(1)}, bf16[2,2,32,256]{3,2,1,0:T(8,128)(2,1)S(1)}, u32[]{:S(2)}, u32[]{:S(2)}) collective-permute-start(bf16[2,2,32,256]{3,2,1,0:T(8,128)(2,1)S(1)} %pad_maximum_fusion.1), channel_id=1, source_target_pairs={{0,2},{2,0},{4,6},{6,4},{8,10},{10,8},{12,14},{14,12},{1,3},{3,1},... | collective-permute-start | bytes 196616 | tf_op jit(solution)/shard_map/ppermute | solution.py:30
  11.5 8.7 %copy-start.3 = (bf16[4,2,32,256]{3,2,1,0:T(8,128)(2,1)}, bf16[4,2,32,256]{3,2,1,0:T(8,128)(2,1)S(1)}, u32[]{:S(2)}) copy-start(bf16[4,2,32,256]{3,2,1,0:T(8,128)(2,1)S(1)} %pad_maximum_fusion.here_ref) | copy-start | bytes 393220
  11.5 8.1 %collective-permute-start.3 = (bf16[4,2,32,256]{3,2,1,0:T(8,128)(2,1)S(1)}, bf16[4,2,32,256]{3,2,1,0:T(8,128)(2,1)S(1)}, u32[]{:S(2)}, u32[]{:S(2)}) collective-permute-start(bf16[4,2,32,256]{3,2,1,0:T(8,128)(2,1)S(1)} %pad_maximum_fusion.here_ref), channel_id=1, source_target_pairs={{0,8},{2,10},{4,12},{6,14},{8,0},{10,2},{12,4},{14,6},{1,9},{3,11}... | collective-permute-start | bytes 393224 | tf_op jit(solution)/shard_map/ppermute | solution.py:30
  14.1 6.0 %collective-permute-start.2 = (bf16[4,2,32,256]{3,2,1,0:T(8,128)(2,1)S(1)}, bf16[4,2,32,256]{3,2,1,0:T(8,128)(2,1)S(1)}, u32[]{:S(2)}, u32[]{:S(2)}) collective-permute-start(bf16[4,2,32,256]{3,2,1,0:T(8,128)(2,1)S(1)} %pad_maximum_fusion.here_ref), channel_id=1, source_target_pairs={{0,1},{1,0},{2,3},{3,2},{4,5},{5,4},{6,7},{7,6},{8,9},{9,8},{10,11... | collective-permute-start | bytes 393224 | tf_op jit(solution)/shard_map/ppermute | solution.py:30
  19.6 15.7 %copy-start.6 = (bf16[4,2,32,256]{3,2,1,0:T(8,128)(2,1)}, bf16[4,2,32,256]{3,2,1,0:T(8,128)(2,1)S(1)}, u32[]{:S(2)}) copy-start(bf16[4,2,32,256]{3,2,1,0:T(8,128)(2,1)S(1)} %collective-permute-done.3.here_ref) | copy-start | bytes 393220
  19.6 15.7 %collective-permute-start.4 = (bf16[4,2,32,256]{3,2,1,0:T(8,128)(2,1)S(1)}, bf16[4,2,32,256]{3,2,1,0:T(8,128)(2,1)S(1)}, u32[]{:S(2)}, u32[]{:S(2)}) collective-permute-start(bf16[4,2,32,256]{3,2,1,0:T(8,128)(2,1)S(1)} %collective-permute-done.3.here_ref), channel_id=1, source_target_pairs={{0,1},{1,0},{2,3},{3,2},{4,5},{5,4},{6,7},{7,6},{8,9},{9,8},{10,11... | collective-permute-start | bytes 393224 | tf_op jit(solution)/shard_map/ppermute | solution.py:30
  20.1 0.7 copy-start.7
  35.3 0.7 copy-start.8
  67.0 20.2 %copy-start.2 = (bf16[8,128,128]{2,1,0:T(8,128)(2,1)S(1)}, bf16[8,128,128]{2,1,0:T(8,128)(2,1)}, u32[]{:S(2)}) copy-start(bf16[8,128,128]{2,1,0:T(8,128)(2,1)} %get-tuple-element.40.refs_1_) | copy-start | bytes 786436
  67.0 21.6 %copy-start.5 = (bf16[16,8,128]{2,1,0:T(8,128)(2,1)S(1)}, bf16[16,8,128]{2,1,0:T(8,128)(2,1)}, u32[]{:S(2)}) copy-start(bf16[16,8,128]{2,1,0:T(8,128)(2,1)} %get-tuple-element.43) | copy-start | bytes 98308
  67.0 21.5 %collective-permute-start.5 = (bf16[8,128,128]{2,1,0:T(8,128)(2,1)}, bf16[8,128,128]{2,1,0:T(8,128)(2,1)S(1)}, u32[]{:S(2)}, u32[]{:S(2)}) collective-permute-start(bf16[8,128,128]{2,1,0:T(8,128)(2,1)} %get-tuple-element.39.refs_4_), channel_id=1, source_target_pairs={{0,2},{2,4},{4,6},{6,8},{8,10},{10,12},{12,14},{1,3},{3,5},{5,7},{... | collective-permute-start | bytes 786440 | tf_op jit(solution)/shard_map/ppermute | solution.py:423
  87.3 9.9 %collective-permute-start.6 = (bf16[8,128,128]{2,1,0:T(8,128)(2,1)S(1)}, bf16[8,128,128]{2,1,0:T(8,128)(2,1)S(1)}, u32[]{:S(2)}, u32[]{:S(2)}) collective-permute-start(bf16[8,128,128]{2,1,0:T(8,128)(2,1)S(1)} %copy-done.2), channel_id=1, source_target_pairs={{2,0},{4,2},{6,4},{8,6},{10,8},{12,10},{14,12},{3,1},{5,3},{7,5},{... | collective-permute-start | bytes 786440 | tf_op jit(solution)/shard_map/ppermute | solution.py:424
  88.6 10.6 %copy-start = (bf16[8,128,128]{2,1,0:T(8,128)(2,1)}, bf16[8,128,128]{2,1,0:T(8,128)(2,1)S(1)}, u32[]{:S(2)}) copy-start(bf16[8,128,128]{2,1,0:T(8,128)(2,1)S(1)} %collective-permute-done.5.refs_0_) | copy-start | bytes 786436
  97.1 2.0 %copy-start.1 = (bf16[8,128,128]{2,1,0:T(8,128)(2,1)}, bf16[8,128,128]{2,1,0:T(8,128)(2,1)S(1)}, u32[]{:S(2)}) copy-start(bf16[8,128,128]{2,1,0:T(8,128)(2,1)S(1)} %collective-permute-done.6.refs_5_) | copy-start | bytes 786436
  97.2 1.4 %collective-permute-start.7 = (bf16[48,8,128]{2,1,0:T(8,128)(2,1)S(1)}, bf16[48,8,128]{2,1,0:T(8,128)(2,1)S(1)}, u32[]{:S(2)}, u32[]{:S(2)}) collective-permute-start(bf16[48,8,128]{2,1,0:T(8,128)(2,1)S(1)} %fusion.3), channel_id=1, source_target_pairs={{0,1},{1,0},{2,3},{3,2},{4,5},{5,4},{6,7},{7,6},{8,9},{9,8},{10,11... | collective-permute-start | bytes 294920 | tf_op jit(solution)/shard_map/ppermute | solution.py:30
  98.5 0.6 copy-start.4
where the time goes:
time: 114 us
  Pallas kernels  76.7 us (67%)
  starting transfers between devices  13 us (11%)
  waiting for transfers between devices  10.4 us (9%)
  local copies, waits for them, and re-layouts  9.49 us (8%)
  other arithmetic  2.89 us (3%)
  matrix products  1.24 us (1%)
    pallas_call x2, Pallas kernels, outer_products(): pl.pallas_call(functools.partial(outer_kernel, picks=picks, halves=len(ro...  33 us
    pallas_call x2, Pallas kernels, features(): pl.pallas_call(functools.partial(feature_kernel, pitch=pitch), grid_spec=...  29 us
    pallas_call x1, Pallas kernels, pair_convolutions(): pl.pallas_call(functools.partial(conv_kernel, length=length, swap=swap),...  14.6 us
    ppermute x6, starting transfers between devices, exchange(): return lax.ppermute(block, axis, [(i, i ^ bit) for i in range(count)])  7.94 us
    ppermute x1, waiting for transfers between devices, per_device(): below = lax.ppermute(ends[0], 'row', [(i + 1, i) for i in steps])  7.69 us
    ppermute x1, starting transfers between devices, per_device(): above = lax.ppermute(ends[1], 'row', [(i, i + 1) for i in steps])  3.75 us
    ppermute x6, waiting for transfers between devices, exchange(): return lax.ppermute(block, axis, [(i, i ^ bit) for i in range(count)])  2.66 us
  transfers between devices with their start and end apart: 8, of which 3 were waited for; matrix products, arithmetic and copies ran while one was open for 10% of the time, Pallas kernels for 27%

commit v1 on v0

v1 whole, which is shorter than its diff:
```python
import functools
import math

import jax
import jax.numpy as jnp
from jax import lax
from jax.experimental import pallas as pl
from jax.experimental.pallas import tpu as pltpu
from jax.sharding import PartitionSpec as P


NL1 = 2
DMAX = 4
HALO = 2 * DMAX
BLOCK = 16
LANES = 128
TILE = 256
LOG2E = 1.4426950408889634
SHIFT = math.log2(LOG2E)
VMEM_LIMIT = 62 << 20


def elu(x):
    return jnp.maximum(x, jnp.exp(jnp.minimum(x, 0.0)) - 1.0)


def contract_last(left, right):
    return lax.dot_general(
        left, right, (((1,), (1,)), ((), ())), preferred_element_type=jnp.float32
    )


def exchange(block, axis, bit):
    count = lax.axis_size(axis)
    return lax.ppermute(block, axis, [(i, i ^ bit) for i in range(count)])


def first_sequences(tokens, gap_mask):
    half = jnp.stack([tokens, gap_mask]).astype(jnp.bfloat16)[None]
    bit = lax.axis_size("row") // 4
    while bit >= 1:
        half = jnp.concatenate([half, exchange(half, "row", bit)])
        bit //= 2
    return half


def prepare_kernel(embedding_ref, filters_ref, projection_ref, table_ref, second_ref, turned_ref, letter_s, turn_s):
    letters, channels = embedding_ref.shape
    kinds = letter_s.shape[0]
    f32, bf16 = jnp.float32, jnp.bfloat16
    letter_s[...] = jnp.zeros_like(letter_s)
    letter_s[0:letters, :] = embedding_ref[...]
    letter = letter_s[...]
    for tap in range(3):
        mixed = LOG2E * lax.dot_general(
            filters_ref[0, tap], letter, (((1,), (1,)), ((), ())),
            precision=lax.Precision.HIGHEST, preferred_element_type=f32,
        )
        plain = jnp.zeros((channels, kinds), f32)
        if tap == 1:
            mixed = mixed + SHIFT
            plain = LOG2E * letter.T - SHIFT
        for first, value in ((0, mixed), (channels, plain)):
            high = value.astype(bf16)
            low = (value - high.astype(f32)).astype(bf16)
            for part, piece in enumerate((high, low)):
                start = (part * 3 + tap) * kinds
                table_ref[first : first + channels, start : start + kinds] = piece
        second_ref[:, tap * channels : (tap + 1) * channels] = filters_ref[1, tap].astype(bf16)
    pitch = turn_s.shape[0] // channels

    def widen(a, carry):
        start = pl.multiple_of(a * channels, channels)
        turn_s[pl.ds(pl.multiple_of(a * pitch, 8), channels), :] = projection_ref[pl.ds(start, channels), :].astype(f32)
        return carry

    lax.fori_loop(0, channels, widen, 0, unroll=4)

    def turn(step, carry):
        pair = jnp.concatenate([turn_s[pl.ds(2 * step + k, channels, stride=pitch), :] for k in range(2)], axis=0)
        start = pl.multiple_of(step * 2 * channels, 2 * channels)
        turned_ref[:, pl.ds(start, 2 * channels)] = pair.T.astype(bf16)
        return carry

    lax.fori_loop(0, channels // 2, turn, 0, unroll=2)


def prepare(embedding, filters, projection):
    letters, channels = embedding.shape
    kinds = -(-letters // 32) * 32
    out = projection.shape[1]
    bf16 = jnp.bfloat16
    return pl.pallas_call(
        prepare_kernel,
        out_shape=[
            jax.ShapeDtypeStruct((2 * channels, 6 * kinds), bf16),
            jax.ShapeDtypeStruct((channels, 3 * channels), bf16),
            jax.ShapeDtypeStruct((out, channels * channels), bf16),
        ],
        scratch_shapes=[
            pltpu.VMEM((kinds, channels), jnp.float32),
            pltpu.VMEM((channels * (channels + 8), out), jnp.float32),
        ],
        compiler_params=pltpu.CompilerParams(vmem_limit_bytes=16 << 20),
        cost_estimate=pl.CostEstimate(flops=10**6, bytes_accessed=4 << 20, transcendentals=0),
    )(embedding, filters, projection)


def feature_kernel(
    dilations, here_ref, there_ref, table_ref, second_ref, row_ref, col_ref, row_mark_ref, col_mark_ref,
    token_s, mark_s, onehot_s, hidden_s, narrow_s, turn_s, stage_s, sems, *, pitch,
):
    first_spread, second_spread = dilations[0], dilations[1]
    blocks, _, each, length = here_ref.shape
    part = blocks * each
    width = 2 * part
    channels = second_ref.shape[0]
    kinds = onehot_s.shape[1]
    rows, cols = row_ref.shape[0], col_ref.shape[1]
    row_first, col_first = lax.axis_index("row") * rows, lax.axis_index("col") * cols
    lanes = LANES
    for side, ref in enumerate((here_ref, there_ref)):
        at = slice(side * part, (side + 1) * part)
        token_s[HALO : HALO + length, at] = ref[:, 0].reshape(part, length).astype(jnp.float32).T
        mark_s[:, at] = ref[:, 1].reshape(part, length).astype(jnp.float32).T
    edge = jnp.full((HALO, width), -1.0, jnp.float32)
    token_s[0:HALO, :] = edge
    token_s[HALO + length : 2 * HALO + length, :] = edge
    row_mark_ref[...] = mark_s[pl.ds(pl.multiple_of(row_first, 8), rows), :].astype(row_mark_ref.dtype)
    col_mark_ref[...] = mark_s[pl.ds(pl.multiple_of(col_first, 8), cols), :].astype(col_mark_ref.dtype)
    letters = lax.broadcasted_iota(jnp.int32, (kinds, width), 0).astype(jnp.float32)
    table = table_ref[...]
    second = second_ref[...]

    def layer_one(at):
        taps = jnp.concatenate([onehot_s[at - first_spread], onehot_s[at], onehot_s[at + first_spread]], axis=0)
        mixing = jnp.dot(table, jnp.concatenate([taps, taps], axis=0), preferred_element_type=jnp.float32)
        shifted = mixing[:channels]
        hidden = mixing[channels:] + jnp.maximum(shifted, jnp.exp2(jnp.minimum(shifted, SHIFT)) + (SHIFT - LOG2E))
        hidden_s[at] = hidden
        narrow_s[at] = hidden.astype(narrow_s.dtype)

    def layer_two(at):
        taps = jnp.concatenate([narrow_s[at - second_spread], narrow_s[at], narrow_s[at + second_spread]], axis=0)
        mixing = jnp.dot(second, taps, preferred_element_type=jnp.float32)
        return hidden_s[at] + jnp.maximum(mixing, LOG2E * jnp.exp2(jnp.minimum(mixing, 0.0)) - LOG2E)

    def run(first, count, emit, before, between, after):
        def hot(step, carry):
            block = token_s[pl.ds(pl.multiple_of(first + step * 8, 8), 8), :]
            for k in range(8):
                onehot_s[step * 8 + k] = jnp.where(block[k : k + 1, :] == letters, 1.0, 0.0).astype(onehot_s.dtype)
            return carry

        lax.fori_loop(0, (count + 2 * HALO) // 8, hot, 0)

        def clear(start):
            for k in range(DMAX):
                place = first - HALO + start + k

                @pl.when((place < 0) | (place >= length))
                def _():
                    narrow_s[start + k] = jnp.zeros((channels, width), narrow_s.dtype)

        ahead = BLOCK + 2 * DMAX
        for k in range(ahead):
            layer_one(DMAX + k)
        clear(DMAX)

        def trip(step, carry):
            before(step)
            between(step)
            for k in range(BLOCK):
                emit(step, k, layer_two(HALO + step * BLOCK + k))
                layer_one(DMAX + ahead + step * BLOCK + k)
            after(step)
            return carry

        last = count // BLOCK - 1
        lax.fori_loop(0, last, trip, 0)
        clear(count + HALO)
        before(last)
        between(last)
        for k in range(BLOCK):
            emit(last, k, layer_two(HALO + last * BLOCK + k))
        after(last)

    def emit_row(step, k, value):
        marks = mark_s[pl.ds(row_first + step * BLOCK + k, 1), :]
        row_ref[step * BLOCK + k] = (value * marks).astype(row_ref.dtype)

    def emit_col(step, k, value):
        for piece in range(width // lanes):
            turn_s[pl.ds(piece * channels * pitch + k, channels, stride=pitch), :] = value[
                :, piece * lanes : (piece + 1) * lanes
            ]

    def leave(step):
        slot = lax.rem(step, 2)
        start = pl.multiple_of(step * BLOCK, BLOCK)
        return pltpu.make_async_copy(stage_s.at[slot], col_ref.at[:, pl.ds(start, BLOCK), :], sems.at[slot])

    def await_stage(step):
        @pl.when(step >= 3)
        def _():
            leave(step - 3).wait()

    def turn_block(step):
        slot = lax.rem(step + 1, 2)
        start = pl.multiple_of(jnp.maximum(step - 1, 0) * BLOCK, BLOCK)
        marks = col_mark_ref[pl.ds(start, BLOCK), :]
        for channel in range(channels):
            for piece in range(width // lanes):
                part = slice(piece * lanes, (piece + 1) * lanes)
                place = (piece * channels + channel) * pitch
                stage_s[slot, channel, :, part] = turn_s[place : place + BLOCK, :].astype(stage_s.dtype) * marks[:, part]

    def send_block(step):
        @pl.when(step >= 1)
        def _():
            leave(step - 1).start()

    nothing = lambda step: None
    run(row_first, rows, emit_row, nothing, nothing, nothing)
    run(col_first, cols, emit_col, await_stage, turn_block, send_block)
    steps = cols // BLOCK
    if steps >= 3:
        leave(steps - 3).wait()
    turn_block(steps)
    leave(steps - 1).start()
    for step in range(max(steps - 2, 0), steps):
        leave(step).wait()


def features(dilations, here, there, table, second, rows, cols):
    blocks, _, each, length = here.shape
    width = 2 * blocks * each
    channels = second.shape[0]
    kinds = table.shape[1] // 6
    span = max(rows, cols) + 2 * HALO
    pitch = BLOCK + 8
    bf16, f32 = jnp.bfloat16, jnp.float32
    full = lambda shape: pl.BlockSpec(shape, functools.partial(lambda rank, g, s: (0,) * rank, len(shape)))
    return pl.pallas_call(
        functools.partial(feature_kernel, pitch=pitch),
        grid_spec=pltpu.PrefetchScalarGridSpec(
            num_scalar_prefetch=1,
            grid=(1,),
            in_specs=[full(x.shape) for x in (here, there, table, second)],
            out_specs=[
                full((rows, channels, width)),
                pl.BlockSpec(memory_space=pl.ANY),
                full((rows, width)),
                full((cols, width)),
            ],
            scratch_shapes=[
                pltpu.VMEM((length + 2 * HALO, width), f32),
                pltpu.VMEM((length, width), f32),
                pltpu.VMEM((span, kinds, width), bf16),
                pltpu.VMEM((span, channels, width), f32),
                pltpu.VMEM((span, channels, width), bf16),
                pltpu.VMEM((width // 128 * channels * pitch, 128), f32),
                pltpu.VMEM((2, channels, BLOCK, width), bf16),
                pltpu.SemaphoreType.DMA((2,)),
            ],
        ),
        out_shape=[
            jax.ShapeDtypeStruct((rows, channels, width), bf16),
            jax.ShapeDtypeStruct((channels, cols, width), bf16),
            jax.ShapeDtypeStruct((rows, width), bf16),
            jax.ShapeDtypeStruct((cols, width), bf16),
        ],
        compiler_params=pltpu.CompilerParams(vmem_limit_bytes=VMEM_LIMIT),
        cost_estimate=pl.CostEstimate(
            flops=40 * channels * channels * width * (rows + cols),
            bytes_accessed=2 * channels * width * (rows + cols),
            transcendentals=2 * channels * width * (rows + cols),
        ),
    )(dilations, here, there, table, second)


def outer_kernel(*refs, picks, halves, swap):
    count = len(picks)
    row_refs = refs[: halves * count]
    col_refs = refs[halves * count : halves * (count + 1)]
    projection_ref = refs[halves * (count + 1)]
    marks = refs[halves * (count + 1) + 1 : -(count + 2)]
    pair_refs = refs[-(count + 2) : -2]
    edge_ref, sum_s = refs[-2:]
    step = pl.program_id(0)
    group, cols, _ = col_refs[0].shape
    channels = row_refs[0].shape[1]
    rows = count * HALO

    @pl.when(step == 0)
    def _():
        sum_s[...] = jnp.zeros_like(sum_s)

    right = jnp.concatenate([ref[...].reshape(group * cols, ref.shape[2]) for ref in col_refs], axis=1)
    left = jnp.concatenate(
        [
            jnp.concatenate([row_refs[p * halves + h][...].reshape(HALO * channels, -1) for h in range(halves)], axis=1)
            for p in range(count)
        ],
        axis=0,
    )
    projection = projection_ref[...]
    outer = contract_last(left, right).astype(jnp.bfloat16)
    for pair in range(0, rows, 2):
        sides = [
            jnp.concatenate(
                [outer[i * channels : (i + 1) * channels, b * cols : (b + 1) * cols] for b in range(group)], axis=0
            )
            for i in (pair, pair + 1)
        ]
        sum_s[pair // 2] += jnp.dot(
            projection, jnp.concatenate(sides, axis=1), preferred_element_type=jnp.float32
        )

    @pl.when(step == pl.num_programs(0) - 1)
    def _():
        row_marks, col_marks = marks[:halves], marks[halves:]
        counts = sum(contract_last(r[...], c[...]) for r, c in zip(row_marks, col_marks))
        share = 1.0 / ((counts + 1.0) * (LOG2E * LOG2E))
        for p, pick in enumerate(picks):
            for k in range(HALO):
                i = p * HALO + k
                place = pick * HALO + k
                value = sum_s[i // 2][:, (i % 2) * cols : (i % 2 + 1) * cols] * share[place : place + 1, :]
                value = value.T
                pair_refs[p][k] = value.astype(edge_ref.dtype)
                if swap:
                    edge_ref[i] = jnp.where(lax.axis_index("col") == 0, value[cols - HALO :], value[:HALO]).astype(edge_ref.dtype)
        if not swap:
            edge_ref[...] = jnp.zeros_like(edge_ref)


def outer_products(row_feats, col_feats, projection, row_marks, col_marks, picks, swap, group=8):
    _, channels, _ = row_feats[0].shape
    cols = col_feats[0].shape[1]
    out = projection.shape[0]
    total = sum(x.shape[2] for x in row_feats)
    tall = len(picks) * HALO
    full = lambda shape: pl.BlockSpec(shape, functools.partial(lambda rank, g: (0,) * rank, len(shape)))
    picked = lambda pick, width: pl.BlockSpec((HALO, channels, width), lambda g: (pick, 0, 0))
    results = pl.pallas_call(
        functools.partial(outer_kernel, picks=picks, halves=len(row_feats), swap=swap),
        grid_spec=pl.GridSpec(
            grid=(channels // group,),
            in_specs=[picked(pick, x.shape[2]) for pick in picks for x in row_feats]
            + [pl.BlockSpec((group, cols, x.shape[2]), lambda g: (g, 0, 0)) for x in col_feats]
            + [pl.BlockSpec((out, group * channels), lambda g: (0, g))]
            + [full(x.shape) for x in (*row_marks, *col_marks)],
            out_specs=[full((HALO, cols, out)) for _ in picks] + [full((tall, HALO, out))],
            scratch_shapes=[pltpu.VMEM((tall // 2, out, 2 * cols), jnp.float32)],
        ),
        out_shape=[jax.ShapeDtypeStruct((HALO, cols, out), jnp.bfloat16) for _ in picks]
        + [jax.ShapeDtypeStruct((tall, HALO, out), jnp.bfloat16)],
        compiler_params=pltpu.CompilerParams(vmem_limit_bytes=VMEM_LIMIT),
        cost_estimate=pl.CostEstimate(
            flops=2 * tall * cols * channels * channels * (total + out),
            bytes_accessed=2 * channels * total * (tall + cols),
            transcendentals=0,
        ),
    )(
        *[x for _ in picks for x in row_feats],
        *col_feats,
        projection,
        *row_marks,
        *col_marks,
    )
    return list(results[:-1]), results[-1]


def conv_kernel(dilations, *refs, length, swap, rows, cols):
    first_spread, second_spread = dilations[NL1], dilations[NL1 + 1]
    row_first, col_first = lax.axis_index("row") * rows, lax.axis_index("col") * cols
    blocks = rows // HALO + 2
    row_refs = refs[:blocks]
    margin_refs = refs[blocks:-6]
    filter_ref, out_ref, wide_s, first_s, hidden_s, second_s = refs[-6:]
    channels = out_ref.shape[2]
    tall, pitch = rows + 2 * DMAX, cols + 2 * HALO
    f32, bf16 = jnp.float32, jnp.bfloat16
    for block, ref in enumerate(row_refs):
        for k in range(HALO):
            start = (block * HALO + k) * pitch + HALO
            wide_s[start : start + cols, :] = ref[k].astype(f32)
    for i in range(rows + 2 * HALO):
        if swap:
            edge = margin_refs[0][i].astype(f32)
            left = jnp.where(col_first == 0, jnp.zeros_like(edge), edge)
            right = jnp.where(col_first == 0, edge, jnp.zeros_like(edge))
        else:
            left, right = margin_refs[0][i].astype(f32), margin_refs[1][i].astype(f32)
        wide_s[i * pitch : i * pitch + HALO, :] = left
        wide_s[i * pitch + HALO + cols : (i + 1) * pitch, :] = right
    weights = [
        jnp.concatenate(
            [filter_ref[layer, k * channels : (k + 1) * channels, :].astype(f32).T for k in range(9)], axis=1
        ).astype(bf16)
        for layer in range(2)
    ]

    def spread_taps(source, target, count, spread, width, span):
        def body(i, carry):
            for tap in range(3):
                start = i * pitch + DMAX + (tap - 1) * spread
                for at in range(0, width, 16):
                    piece = source[pl.ds(start + at, 16), :].astype(bf16)
                    target[pl.ds(pl.multiple_of(i * span + at, 16), 16), tap * channels : (tap + 1) * channels] = piece
            return carry

        lax.fori_loop(0, count, body, 0, unroll=2)

    def mix(source, layer, start, spread, span):
        taps = jnp.concatenate(
            [
                source[pl.ds(pl.multiple_of(start + (DMAX + (tap - 1) * spread) * span, 16), TILE), :]
                for tap in range(3)
            ],
            axis=1,
        )
        return contract_last(weights[layer], taps)

    spread_taps(wide_s, first_s, rows + 2 * HALO, first_spread, pitch, pitch)

    def one(step, carry):
        start = pl.multiple_of(step * TILE, TILE)
        hidden_s[pl.ds(start, TILE), :] = elu(mix(first_s, 0, start, first_spread, pitch)).T
        return carry

    lax.fori_loop(0, -(-tall * pitch // TILE), one, 0, unroll=2)
    for i in range(tall):
        place = row_first - DMAX + i
        if i < DMAX or i >= tall - DMAX:

            @pl.when((place < 0) | (place >= length))
            def _():
                hidden_s[i * pitch : (i + 1) * pitch, :] = jnp.zeros((pitch, channels), f32)

    @pl.when(col_first == 0)
    def _():
        for i in range(tall):
            hidden_s[i * pitch : i * pitch + DMAX, :] = jnp.zeros((DMAX, channels), f32)

    @pl.when(col_first + cols == length)
    def _():
        for i in range(tall):
            start = i * pitch + DMAX + cols
            hidden_s[start : start + DMAX, :] = jnp.zeros((DMAX, channels), f32)

    spread_taps(hidden_s, second_s, tall, second_spread, cols, cols)

    def two(step, carry):
        start = pl.multiple_of(step * TILE, TILE)
        mixing = mix(second_s, 1, start, second_spread, cols).T
        for k in range(TILE // cols):
            i = step * (TILE // cols) + k
            own = wide_s[pl.ds(pl.multiple_of((i + HALO) * pitch + HALO, 8), cols), :]
            out_ref[i] = (own + mixing[k * cols : (k + 1) * cols]).astype(out_ref.dtype)
        return carry

    lax.fori_loop(0, rows * cols // TILE, two, 0, unroll=2)


def pair_convolutions(dilations, blocks, margins, filters, length, swap):
    cols, channels = blocks[0].shape[1:]
    rows = (len(blocks) - 2) * HALO
    pitch = cols + 2 * HALO
    padded = -(-(rows + 2 * DMAX) * pitch // TILE) * TILE
    operands = (*blocks, *margins, filters)
    full = lambda shape: pl.BlockSpec(shape, functools.partial(lambda rank, g, s: (0,) * rank, len(shape)))
    return pl.pallas_call(
        functools.partial(conv_kernel, length=length, swap=swap, rows=rows, cols=cols),
        grid_spec=pltpu.PrefetchScalarGridSpec(
            num_scalar_prefetch=1,
            grid=(1,),
            in_specs=[full(x.shape) for x in operands],
            out_specs=full((rows, cols, channels)),
            scratch_shapes=[
                pltpu.VMEM(((rows + 2 * HALO) * pitch + HALO, channels), jnp.float32),
                pltpu.VMEM((padded + 2 * DMAX * pitch, 3 * channels), jnp.bfloat16),
                pltpu.VMEM((padded, channels), jnp.float32),
                pltpu.VMEM(((rows + 2 * DMAX) * cols, 3 * channels), jnp.bfloat16),
            ],
        ),
        out_shape=jax.ShapeDtypeStruct((rows, cols, channels), jnp.bfloat16),
        compiler_params=pltpu.CompilerParams(vmem_limit_bytes=40 << 20),
    )(dilations, *operands)


def col_margins(tall):
    steps = range(lax.axis_size("col") - 1)
    head, tail = tall[:, :HALO], tall[:, tall.shape[1] - HALO :]
    return (
        lax.ppermute(tail, "col", [(i, i + 1) for i in steps]),
        lax.ppermute(head, "col", [(i + 1, i) for i in steps]),
    )


def per_device(tokens, gap_mask, dilations, embedding, residue_filters, projection, pair_filters):
    length = tokens.shape[1]
    row_count, col_count = lax.axis_size("row"), lax.axis_size("col")
    rows, cols = length // row_count, length // col_count
    col_index = lax.axis_index("col")
    swap = col_count == 2
    near = first_sequences(tokens, gap_mask)
    near_there = exchange(near, "col", 1)
    far = exchange(near, "row", row_count // 2)
    far_there = exchange(far, "col", 1)
    table, second, turned = prepare(embedding, residue_filters, projection)
    near_parts = features(dilations, near, near_there, table, second, rows, cols)
    far_parts = features(dilations, far, far_there, table, second, rows, cols)
    row_feats, col_feats, row_marks, col_marks = zip(near_parts, far_parts)
    last = rows // HALO - 1
    run = functools.partial(outer_products, row_feats, col_feats, turned, row_marks, col_marks, swap=swap)
    ends, end_edges = run(picks=(0, last))
    steps = range(row_count - 1)
    above = lax.ppermute(ends[1], "row", [(i, i + 1) for i in steps])
    below = lax.ppermute(ends[0], "row", [(i + 1, i) for i in steps])
    if last > 1:
        middle, middle_edges = run(picks=tuple(range(1, last)))
    else:
        middle, middle_edges = [], end_edges[:0]
    blocks = [above, ends[0], *middle, ends[1], below]
    if swap:
        pick = lambda block: jnp.where(col_index == 0, block[:, cols - HALO :], block[:, :HALO])
        edges = jnp.concatenate([pick(above), end_edges[:HALO], middle_edges, end_edges[HALO:], pick(below)])
        edges = exchange(edges, "col", 1)
        margins = [edges]
    else:
        margins = col_margins(jnp.concatenate(blocks))
    filters = pair_filters.reshape(2, 9 * pair_filters.shape[3], pair_filters.shape[4])
    return pair_convolutions(dilations, blocks, margins, filters, length, swap)


def solution(mesh):
    in_specs = (
        P(("grp", "row", "col"), None),
        P(("grp", "row", "col"), None),
        P(),
        P(),
        P(),
        P(),
        P(),
    )
    out_specs = P(("grp", "row"), "col", None)
    return jax.shard_map(per_device, mesh=mesh, in_specs=in_specs, out_specs=out_specs, check_vma=False)
```

time: 114 us -> 149 us (1.31)
  Pallas kernels: 76.7 us -> 111 us
  waiting for transfers between devices: 10.4 us -> 13.2 us
  other arithmetic: 2.89 us -> 0.84 us
    pallas_call x2, Pallas kernels: 29 us -> 59.8 us  [features(): pl.pallas_call(functools.partial(feature_kernel, pitch=pitch), grid_spec=...]
    unnamed x21 -> x37, local copies, waits for them, and re-layouts: 2.15 us -> 9.14 us
    pallas_call x1 -> x2, Pallas kernels: 14.6 us -> 18.4 us  [the longest x1 16.1 us: pair_convolutions(): pl.pallas_call(functools.partial(conv_kernel, length=length, swap=swap, r...]
    ppermute x6, waiting for transfers between devices: 2.66 us -> 5.49 us  [exchange(): return lax.ppermute(block, axis, [(i, i ^ bit) for i in range(count)])]
    concatenate x4 -> x0, other arithmetic: 2.03 us -> none  [the longest x1 0.72 us: feature_tables(): return (jnp.concatenate([high, low], axis=1), second)]
    transpose x1 -> x0, local copies, waits for them, and re-layouts: 1.9 us -> none  [per_device(): projection.reshape(channels, channels, out).transpose(2, 1, 0)]
    convert_element_type x4 -> x0, local copies, waits for them, and re-layouts: 1.83 us -> none  [the longest x3 1.72 us: feature_tables(): filters[1].transpose(1, 0, 2).reshape(channels, 3 * channels)]
  transfers between devices with their start and end apart: 8 -> 8, of which waited for: 3 -> 4; matrix products, arithmetic and copies ran while one was open for 10% -> 1% of each run, Pallas kernels for 27% -> 33%
where the time goes in v1:
time: 149 us; the launch traced here: 148 us
  Pallas kernels  111 us (74%)
  starting transfers between devices  13.7 us (9%)
  waiting for transfers between devices  13.2 us (9%)
  local copies, waits for them, and re-layouts  9.14 us (6%)
    pallas_call x2, Pallas kernels, features(): pl.pallas_call(functools.partial(feature_kernel, pitch=pitch), grid_spec=...  59.8 us
    pallas_call x2, Pallas kernels, outer_products(): pl.pallas_call(functools.partial(outer_kernel, picks=picks, halves=len(ro...  33 us
    pallas_call x1, Pallas kernels, pair_convolutions(): pl.pallas_call(functools.partial(conv_kernel, length=length, swap=swap, r...  16.1 us
    unnamed x37, local copies, waits for them, and re-layouts  9.14 us
    ppermute x6, starting transfers between devices, exchange(): return lax.ppermute(block, axis, [(i, i ^ bit) for i in range(count)])  8.83 us
    ppermute x1, waiting for transfers between devices, per_device(): below = lax.ppermute(ends[0], 'row', [(i + 1, i) for i in steps])  7.75 us
    ppermute x6, waiting for transfers between devices, exchange(): return lax.ppermute(block, axis, [(i, i ^ bit) for i in range(count)])  5.49 us
    ppermute x1, starting transfers between devices, per_device(): above = lax.ppermute(ends[1], 'row', [(i, i + 1) for i in steps])  3.57 us
  transfers between devices with their start and end apart: 8, of which 4 were waited for; matrix products, arithmetic and copies ran while one was open for 1% of the time, Pallas kernels for 33%

profile of v1, /device:TPU:0, one launch (start us, length us, event | category | flops | bytes accessed | tf_op | source)
XLA Modules:
  0.0 148.3 jit_solution(4484665845495116142)
XLA Ops:
  0.0 0.8 convert_bitcast_fusion
  0.8 3.1 %collective-permute-start = (bf16[1,2,32,256]{3,2,1,0:T(8,128)(2,1)S(1)}, bf16[1,2,32,256]{3,2,1,0:T(8,128)(2,1)S(1)}, u32[]{:S(2)}, u32[]{:S(2)}) collective-permute-start(bf16[1,2,32,256]{3,2,1,0:T(8,128)(2,1)S(1)} %pad_maximum_fusion.2), channel_id=1, source_target_pairs={{0,4},{2,6},{4,0},{6,2},{8,12},{10,14},{12,8},{14,10},{1,5},{3,7},... | collective-permute-start | bytes 98312 | tf_op jit(solution)/shard_map/ppermute | solution.py:35
  3.9 1.9 %collective-permute-done = bf16[1,2,32,256]{3,2,1,0:T(8,128)(2,1)S(1)} collective-permute-done((bf16[1,2,32,256]{3,2,1,0:T(8,128)(2,1)S(1)}, bf16[1,2,32,256]{3,2,1,0:T(8,128)(2,1)S(1)}, u32[]{:S(2)}, u32[]{:S(2)}) %collective-permute-start) | collective-permute-done | bytes 32800 | tf_op jit(solution)/shard_map/ppermute | solution.py:35
  5.8 2.0 %collective-permute-start.1 = (bf16[2,2,32,256]{3,2,1,0:T(8,128)(2,1)S(1)}, bf16[2,2,32,256]{3,2,1,0:T(8,128)(2,1)S(1)}, u32[]{:S(2)}, u32[]{:S(2)}) collective-permute-start(bf16[2,2,32,256]{3,2,1,0:T(8,128)(2,1)S(1)} %pad_maximum_fusion.1), channel_id=1, source_target_pairs={{0,2},{2,0},{4,6},{6,4},{8,10},{10,8},{12,14},{14,12},{1,3},{3,1},... | collective-permute-start | bytes 196616 | tf_op jit(solution)/shard_map/ppermute | solution.py:35
  7.8 2.3 %collective-permute-done.1 = bf16[2,2,32,256]{3,2,1,0:T(8,128)(2,1)S(1)} collective-permute-done((bf16[2,2,32,256]{3,2,1,0:T(8,128)(2,1)S(1)}, bf16[2,2,32,256]{3,2,1,0:T(8,128)(2,1)S(1)}, u32[]{:S(2)}, u32[]{:S(2)}) %collective-permute-start.1) | collective-permute-done | bytes 65568 | tf_op jit(solution)/shard_map/ppermute | solution.py:35
  10.2 3.1 %collective-permute-start.3 = (bf16[4,2,32,256]{3,2,1,0:T(8,128)(2,1)S(1)}, bf16[4,2,32,256]{3,2,1,0:T(8,128)(2,1)S(1)}, u32[]{:S(2)}, u32[]{:S(2)}) collective-permute-start(bf16[4,2,32,256]{3,2,1,0:T(8,128)(2,1)S(1)} %pad_maximum_fusion.here_ref), channel_id=1, source_target_pairs={{0,8},{2,10},{4,12},{6,14},{8,0},{10,2},{12,4},{14,6},{1,9},{3,11}... | collective-permute-start | bytes 393224 | tf_op jit(solution)/shard_map/ppermute | solution.py:35
  13.3 1.2 copy-done
  14.5 0.9 copy-done.6
  15.4 0.7 copy-done.7
  16.1 2.3 %shard_map.73 = (bf16[128,192]{1,0:T(8,128)(2,1)S(1)}, bf16[64,192]{1,0:T(8,128)(2,1)S(1)}, bf16[128,4096]{1,0:T(8,128)(2,1)S(1)}) custom-call(f32[21,64]{1,0:T(8,128)S(1)} %copy-done.7, f32[2,3,64,64]{3,2,1,0:T(8,128)S(1)} %copy-done.6, bf16[4096,128]{1,0:T(8,128)(2,1)S(1)} %copy-done), custom_call_target="tpu_custom_call" | custom-call | flops 1000000 | bytes 4194304 | tf_op jit(solution)/shard_map/pallas_call | solution.py:93
  18.5 1.0 copy-done.9
  21.9 29.8 %shard_map.74 = (bf16[32,64,256]{2,1,0:T(8,128)(2,1)}, bf16[64,128,256]{2,1,0:T(8,128)(2,1)}, bf16[32,256]{1,0:T(8,128)(2,1)}, bf16[128,256]{1,0:T(8,128)(2,1)}) custom-call(s32[4]{0:T(128)} %dilations.5, bf16[4,2,32,256]{3,2,1,0:T(8,128)(2,1)} %copy-done.12, bf16[4,2,32,256]{3,2,1,0:T(8,128)(2,1)} %copy-done.15, bf16[128,192]{1,0:T(8,128)(2,1)} %copy-done.10, ...), custom_call_target="tpu_custom_call" | custom-call | flops 6710886400 | bytes 5242880 | tf_op jit(solution)/shard_map/pallas_call | solution.py:244
  51.8 0.7 copy-done.16
  52.4 30.0 %shard_map.75 = (bf16[32,64,256]{2,1,0:T(8,128)(2,1)}, bf16[64,128,256]{2,1,0:T(8,128)(2,1)}, bf16[32,256]{1,0:T(8,128)(2,1)}, bf16[128,256]{1,0:T(8,128)(2,1)}) custom-call(s32[4]{0:T(128)} %dilations.5, bf16[4,2,32,256]{3,2,1,0:T(8,128)(2,1)} %copy-done.14, bf16[4,2,32,256]{3,2,1,0:T(8,128)(2,1)} %copy-done.16, bf16[128,192]{1,0:T(8,128)(2,1)} %copy-done.10, ...), custom_call_target="tpu_custom_call" | custom-call | flops 6710886400 | bytes 5242880 | tf_op jit(solution)/shard_map/pallas_call | solution.py:244
  82.4 16.5 %shard_map.76 = (bf16[8,128,128]{2,1,0:T(8,128)(2,1)}, bf16[8,128,128]{2,1,0:T(8,128)(2,1)}, bf16[16,8,128]{2,1,0:T(8,128)(2,1)}) custom-call(bf16[32,64,256]{2,1,0:T(8,128)(2,1)} %get-tuple-element.24.refs_0_.refs_2_, bf16[32,64,256]{2,1,0:T(8,128)(2,1)} %get-tuple-element.25.refs_1_.refs_3_, bf16[32,64,256]{2,1,0:T(8,128)(2,1)} %get-tuple-element.24.refs_0_.refs_2_, ...), custom_call_target="tpu_custom_call" | custom-call | flops 10737418240 | bytes 9437184 | tf_op jit(solution)/shard_map/pallas_call | solution.py:346
  99.0 3.6 %collective-permute-start.5 = (bf16[8,128,128]{2,1,0:T(8,128)(2,1)}, bf16[8,128,128]{2,1,0:T(8,128)(2,1)S(1)}, u32[]{:S(2)}, u32[]{:S(2)}) collective-permute-start(bf16[8,128,128]{2,1,0:T(8,128)(2,1)} %get-tuple-element.33.refs_4_), channel_id=1, source_target_pairs={{0,2},{2,4},{4,6},{6,8},{8,10},{10,12},{12,14},{1,3},{3,5},{5,7},{... | collective-permute-start | bytes 786440 | tf_op jit(solution)/shard_map/ppermute | solution.py:520
  102.6 16.5 %shard_map.77 = (bf16[8,128,128]{2,1,0:T(8,128)(2,1)}, bf16[8,128,128]{2,1,0:T(8,128)(2,1)}, bf16[16,8,128]{2,1,0:T(8,128)(2,1)}) custom-call(bf16[32,64,256]{2,1,0:T(8,128)(2,1)} %get-tuple-element.24.refs_0_.refs_2_, bf16[32,64,256]{2,1,0:T(8,128)(2,1)} %get-tuple-element.25.refs_1_.refs_3_, bf16[32,64,256]{2,1,0:T(8,128)(2,1)} %get-tuple-element.24.refs_0_.refs_2_, ...), custom_call_target="tpu_custom_call" | custom-call | flops 10737418240 | bytes 9437184 | tf_op jit(solution)/shard_map/pallas_call | solution.py:346
  119.1 1.3 collective-permute-start.6
  120.4 0.8 constant_dynamic-update-slice_fusion
  121.2 7.7 %collective-permute-done.6.refs_5_ = bf16[8,128,128]{2,1,0:T(8,128)(2,1)S(1)} collective-permute-done((bf16[8,128,128]{2,1,0:T(8,128)(2,1)S(1)}, bf16[8,128,128]{2,1,0:T(8,128)(2,1)S(1)}, u32[]{:S(2)}, u32[]{:S(2)}) %collective-permute-start.6) | collective-permute-done | bytes 262176 | tf_op jit(solution)/shard_map/ppermute | solution.py:521
  129.0 1.3 collective-permute-done.7.refs_6_
  130.3 0.9 copy-done.4
  131.3 0.9 copy-done.5
  132.2 16.1 %shard_map.78 = bf16[32,128,128]{2,1,0:T(8,128)(2,1)} custom-call(s32[4]{0:T(128)S(1)} %copy-done.8, bf16[8,128,128]{2,1,0:T(8,128)(2,1)S(1)} %collective-permute-done.5.refs_0_, bf16[8,128,128]{2,1,0:T(8,128)(2,1)S(1)} %copy-done.2, bf16[8,128,128]{2,1,0:T(8,128)(2,1)S(1)} %copy-done.4, bf16[8,128,128]{2,1,0:T(8,128)(2,1)S(1)} %copy-done.5, ...), custom_call_target="tpu_custom_call" | custom-call | tf_op jit(solution)/shard_map/pallas_call | solution.py:474
  (41 shorter events, 2.6 us)
Async XLA Ops:
  0.8 5.0 %collective-permute-start = (bf16[1,2,32,256]{3,2,1,0:T(8,128)(2,1)S(1)}, bf16[1,2,32,256]{3,2,1,0:T(8,128)(2,1)S(1)}, u32[]{:S(2)}, u32[]{:S(2)}) collective-permute-start(bf16[1,2,32,256]{3,2,1,0:T(8,128)(2,1)S(1)} %pad_maximum_fusion.2), channel_id=1, source_target_pairs={{0,4},{2,6},{4,0},{6,2},{8,12},{10,14},{12,8},{14,10},{1,5},{3,7},... | collective-permute-start | bytes 98312 | tf_op jit(solution)/shard_map/ppermute | solution.py:35
  5.8 4.3 %collective-permute-start.1 = (bf16[2,2,32,256]{3,2,1,0:T(8,128)(2,1)S(1)}, bf16[2,2,32,256]{3,2,1,0:T(8,128)(2,1)S(1)}, u32[]{:S(2)}, u32[]{:S(2)}) collective-permute-start(bf16[2,2,32,256]{3,2,1,0:T(8,128)(2,1)S(1)} %pad_maximum_fusion.1), channel_id=1, source_target_pairs={{0,2},{2,0},{4,6},{6,4},{8,10},{10,8},{12,14},{14,12},{1,3},{3,1},... | collective-permute-start | bytes 196616 | tf_op jit(solution)/shard_map/ppermute | solution.py:35
  10.2 11.1 %copy-start.12 = (bf16[4,2,32,256]{3,2,1,0:T(8,128)(2,1)}, bf16[4,2,32,256]{3,2,1,0:T(8,128)(2,1)S(1)}, u32[]{:S(2)}) copy-start(bf16[4,2,32,256]{3,2,1,0:T(8,128)(2,1)S(1)} %pad_maximum_fusion.here_ref) | copy-start | bytes 393220
  10.2 10.6 %collective-permute-start.3 = (bf16[4,2,32,256]{3,2,1,0:T(8,128)(2,1)S(1)}, bf16[4,2,32,256]{3,2,1,0:T(8,128)(2,1)S(1)}, u32[]{:S(2)}, u32[]{:S(2)}) collective-permute-start(bf16[4,2,32,256]{3,2,1,0:T(8,128)(2,1)S(1)} %pad_maximum_fusion.here_ref), channel_id=1, source_target_pairs={{0,8},{2,10},{4,12},{6,14},{8,0},{10,2},{12,4},{14,6},{1,9},{3,11}... | collective-permute-start | bytes 393224 | tf_op jit(solution)/shard_map/ppermute | solution.py:35
  13.3 8.0 %collective-permute-start.2 = (bf16[4,2,32,256]{3,2,1,0:T(8,128)(2,1)S(1)}, bf16[4,2,32,256]{3,2,1,0:T(8,128)(2,1)S(1)}, u32[]{:S(2)}, u32[]{:S(2)}) collective-permute-start(bf16[4,2,32,256]{3,2,1,0:T(8,128)(2,1)S(1)} %pad_maximum_fusion.here_ref), channel_id=1, source_target_pairs={{0,1},{1,0},{2,3},{3,2},{4,5},{5,4},{6,7},{7,6},{8,9},{9,8},{10,11... | collective-permute-start | bytes 393224 | tf_op jit(solution)/shard_map/ppermute | solution.py:35
  13.3 1.2 copy-start
  14.5 0.9 copy-start.6
  15.4 0.7 copy-start.7
  18.4 1.0 copy-start.9
  19.5 0.6 copy-start.10
  20.7 31.0 %copy-start.14 = (bf16[4,2,32,256]{3,2,1,0:T(8,128)(2,1)}, bf16[4,2,32,256]{3,2,1,0:T(8,128)(2,1)S(1)}, u32[]{:S(2)}) copy-start(bf16[4,2,32,256]{3,2,1,0:T(8,128)(2,1)S(1)} %collective-permute-done.3.here_ref) | copy-start | bytes 393220
  20.7 31.0 %collective-permute-start.4 = (bf16[4,2,32,256]{3,2,1,0:T(8,128)(2,1)S(1)}, bf16[4,2,32,256]{3,2,1,0:T(8,128)(2,1)S(1)}, u32[]{:S(2)}, u32[]{:S(2)}) collective-permute-start(bf16[4,2,32,256]{3,2,1,0:T(8,128)(2,1)S(1)} %collective-permute-done.3.here_ref), channel_id=1, source_target_pairs={{0,1},{1,0},{2,3},{3,2},{4,5},{5,4},{6,7},{7,6},{8,9},{9,8},{10,11... | collective-permute-start | bytes 393224 | tf_op jit(solution)/shard_map/ppermute | solution.py:35
  21.2 0.6 copy-start.15
  51.8 0.7 copy-start.16
  98.9 20.1 %copy-start.2 = (bf16[8,128,128]{2,1,0:T(8,128)(2,1)S(1)}, bf16[8,128,128]{2,1,0:T(8,128)(2,1)}, u32[]{:S(2)}) copy-start(bf16[8,128,128]{2,1,0:T(8,128)(2,1)} %get-tuple-element.34.refs_1_) | copy-start | bytes 786436
  98.9 21.4 %copy-start.13 = (bf16[16,8,128]{2,1,0:T(8,128)(2,1)S(1)}, bf16[16,8,128]{2,1,0:T(8,128)(2,1)}, u32[]{:S(2)}) copy-start(bf16[16,8,128]{2,1,0:T(8,128)(2,1)} %get-tuple-element.37) | copy-start | bytes 98308
  98.9 31.4 %copy-start.1 = (bf16[2,3,3,128,128]{4,3,2,1,0:T(8,128)(2,1)S(1)}, bf16[2,3,3,128,128]{4,3,2,1,0:T(8,128)(2,1)}, u32[]{:S(2)}) copy-start(bf16[2,3,3,128,128]{4,3,2,1,0:T(8,128)(2,1)} %param.13) | copy-start | bytes 1769476
  99.0 31.4 %copy-start.3 = (bf16[8,128,128]{2,1,0:T(8,128)(2,1)S(1)}, bf16[8,128,128]{2,1,0:T(8,128)(2,1)}, u32[]{:S(2)}) copy-start(bf16[8,128,128]{2,1,0:T(8,128)(2,1)} %get-tuple-element.33.refs_4_) | copy-start | bytes 786436
  99.0 31.4 %copy-start.8 = (s32[4]{0:T(128)S(1)}, s32[4]{0:T(128)}, u32[]{:S(2)}) copy-start(s32[4]{0:T(128)} %dilations.5) | copy-start | bytes 52
  99.0 21.4 %collective-permute-start.5 = (bf16[8,128,128]{2,1,0:T(8,128)(2,1)}, bf16[8,128,128]{2,1,0:T(8,128)(2,1)S(1)}, u32[]{:S(2)}, u32[]{:S(2)}) collective-permute-start(bf16[8,128,128]{2,1,0:T(8,128)(2,1)} %get-tuple-element.33.refs_4_), channel_id=1, source_target_pairs={{0,2},{2,4},{4,6},{6,8},{8,10},{10,12},{12,14},{1,3},{3,5},{5,7},{... | collective-permute-start | bytes 786440 | tf_op jit(solution)/shard_map/ppermute | solution.py:520
  119.1 9.9 %collective-permute-start.6 = (bf16[8,128,128]{2,1,0:T(8,128)(2,1)S(1)}, bf16[8,128,128]{2,1,0:T(8,128)(2,1)S(1)}, u32[]{:S(2)}, u32[]{:S(2)}) collective-permute-start(bf16[8,128,128]{2,1,0:T(8,128)(2,1)S(1)} %copy-done.2), channel_id=1, source_target_pairs={{2,0},{4,2},{6,4},{8,6},{10,8},{12,10},{14,12},{3,1},{5,3},{7,5},{... | collective-permute-start | bytes 786440 | tf_op jit(solution)/shard_map/ppermute | solution.py:521
  128.9 1.4 collective-permute-start.7
  130.3 1.0 copy-start.4
  131.3 0.9 copy-start.5
  (1 other events, 0.6 us)

commit v2 on v1

--- a/solution.py
+++ b/solution.py
@@ -12,12 +12,10 @@
 NL1 = 2
 DMAX = 4
 HALO = 2 * DMAX
-BLOCK = 16
+BLOCK = 32
 LANES = 128
-TILE = 256
 LOG2E = 1.4426950408889634
 SHIFT = math.log2(LOG2E)
-VMEM_LIMIT = 62 << 20
 
 
 def elu(x):
@@ -101,7 +99,7 @@
             pltpu.VMEM((kinds, channels), jnp.float32),
             pltpu.VMEM((channels * (channels + 8), out), jnp.float32),
         ],
-        compiler_params=pltpu.CompilerParams(vmem_limit_bytes=16 << 20),
+        compiler_params=pltpu.CompilerParams(vmem_limit_bytes=62 << 20),
         cost_estimate=pl.CostEstimate(flops=10**6, bytes_accessed=4 << 20, transcendentals=0),
     )(embedding, filters, projection)
 
@@ -146,6 +144,8 @@
         return hidden_s[at] + jnp.maximum(mixing, LOG2E * jnp.exp2(jnp.minimum(mixing, 0.0)) - LOG2E)
 
     def run(first, count, emit, before, between, after):
+        block = min(BLOCK, count)
+
         def hot(step, carry):
             block = token_s[pl.ds(pl.multiple_of(first + step * 8, 8), 8), :]
             for k in range(8):
@@ -162,7 +162,7 @@
                 def _():
                     narrow_s[start + k] = jnp.zeros((channels, width), narrow_s.dtype)
 
-        ahead = BLOCK + 2 * DMAX
+        ahead = block + 2 * DMAX
         for k in range(ahead):
             layer_one(DMAX + k)
         clear(DMAX)
@@ -170,24 +170,26 @@
         def trip(step, carry):
             before(step)
             between(step)
-            for k in range(BLOCK):
-                emit(step, k, layer_two(HALO + step * BLOCK + k))
-                layer_one(DMAX + ahead + step * BLOCK + k)
+            for k in range(block):
+                emit(step, k, layer_two(HALO + step * block + k))
+            for k in range(block):
+                layer_one(DMAX + ahead + step * block + k)
             after(step)
             return carry
 
-        last = count // BLOCK - 1
+        last = count // block - 1
         lax.fori_loop(0, last, trip, 0)
         clear(count + HALO)
         before(last)
         between(last)
-        for k in range(BLOCK):
-            emit(last, k, layer_two(HALO + last * BLOCK + k))
+        for k in range(block):
+            emit(last, k, layer_two(HALO + last * block + k))
         after(last)
 
     def emit_row(step, k, value):
-        marks = mark_s[pl.ds(row_first + step * BLOCK + k, 1), :]
-        row_ref[step * BLOCK + k] = (value * marks).astype(row_ref.dtype)
+        index = step * min(BLOCK, rows) + k
+        marks = mark_s[pl.ds(row_first + index, 1), :]
+        row_ref[index] = (value * marks).astype(row_ref.dtype)
 
     def emit_col(step, k, value):
         for piece in range(width // lanes):
@@ -208,12 +210,12 @@
     def turn_block(step):
         slot = lax.rem(step + 1, 2)
         start = pl.multiple_of(jnp.maximum(step - 1, 0) * BLOCK, BLOCK)
-        marks = col_mark_ref[pl.ds(start, BLOCK), :]
+        marks = mark_s[pl.ds(pl.multiple_of(col_first + start, 8), BLOCK), :]
         for channel in range(channels):
             for piece in range(width // lanes):
                 part = slice(piece * lanes, (piece + 1) * lanes)
                 place = (piece * channels + channel) * pitch
-                stage_s[slot, channel, :, part] = turn_s[place : place + BLOCK, :].astype(stage_s.dtype) * marks[:, part]
+                stage_s[slot, channel, :, part] = (turn_s[place : place + BLOCK, :] * marks[:, part]).astype(stage_s.dtype)
 
     def send_block(step):
         @pl.when(step >= 1)
@@ -238,7 +240,7 @@
     channels = second.shape[0]
     kinds = table.shape[1] // 6
     span = max(rows, cols) + 2 * HALO
-    pitch = BLOCK + 8
+    pitch = BLOCK + 1
     bf16, f32 = jnp.bfloat16, jnp.float32
     full = lambda shape: pl.BlockSpec(shape, functools.partial(lambda rank, g, s: (0,) * rank, len(shape)))
     return pl.pallas_call(
@@ -270,7 +272,7 @@
             jax.ShapeDtypeStruct((rows, width), bf16),
             jax.ShapeDtypeStruct((cols, width), bf16),
         ],
-        compiler_params=pltpu.CompilerParams(vmem_limit_bytes=VMEM_LIMIT),
+        compiler_params=pltpu.CompilerParams(vmem_limit_bytes=40 << 20),
         cost_estimate=pl.CostEstimate(
             flops=40 * channels * channels * width * (rows + cols),
             bytes_accessed=2 * channels * width * (rows + cols),
@@ -356,7 +358,7 @@
         ),
         out_shape=[jax.ShapeDtypeStruct((HALO, cols, out), jnp.bfloat16) for _ in picks]
         + [jax.ShapeDtypeStruct((tall, HALO, out), jnp.bfloat16)],
-        compiler_params=pltpu.CompilerParams(vmem_limit_bytes=VMEM_LIMIT),
+        compiler_params=pltpu.CompilerParams(vmem_limit_bytes=32 << 20),
         cost_estimate=pl.CostEstimate(
             flops=2 * tall * cols * channels * channels * (total + out),
             bytes_accessed=2 * channels * total * (tall + cols),
@@ -377,8 +379,8 @@
     row_first, col_first = lax.axis_index("row") * rows, lax.axis_index("col") * cols
     blocks = rows // HALO + 2
     row_refs = refs[:blocks]
-    margin_refs = refs[blocks:-6]
-    filter_ref, out_ref, wide_s, first_s, hidden_s, second_s = refs[-6:]
+    margin_refs = refs[blocks:-9]
+    filter_ref, out_ref, wide_s, first_s, hidden_s, second_s, weight_s, out_s, sem = refs[-9:]
     channels = out_ref.shape[2]
     tall, pitch = rows + 2 * DMAX, cols + 2 * HALO
     f32, bf16 = jnp.float32, jnp.bfloat16
@@ -395,12 +397,12 @@
             left, right = margin_refs[0][i].astype(f32), margin_refs[1][i].astype(f32)
         wide_s[i * pitch : i * pitch + HALO, :] = left
         wide_s[i * pitch + HALO + cols : (i + 1) * pitch, :] = right
-    weights = [
-        jnp.concatenate(
-            [filter_ref[layer, k * channels : (k + 1) * channels, :].astype(f32).T for k in range(9)], axis=1
-        ).astype(bf16)
-        for layer in range(2)
-    ]
+    for layer in range(2):
+        deep = 3 * channels
+        weight_s[layer, 3 * deep :, 0:channels] = jnp.zeros((deep, channels), bf16)
+        weight_s[layer, :deep, channels:] = jnp.zeros((deep, channels), bf16)
+        weight_s[layer, : 3 * deep, 0:channels] = filter_ref[layer]
+        weight_s[layer, deep:, channels:] = filter_ref[layer]
 
     def spread_taps(source, target, count, spread, width, span):
         def body(i, carry):
@@ -413,24 +415,29 @@
 
         lax.fori_loop(0, count, body, 0, unroll=2)
 
-    def mix(source, layer, start, spread, span):
+    for target, count, span in ((first_s, rows + 2 * HALO, pitch), (second_s, tall, cols)):
+        target[count * span : (count + DMAX) * span, :] = jnp.zeros((DMAX * span, 3 * channels), bf16)
+
+    def mix(source, layer, pair, spread, span):
+        first = 2 * spread * lax.div(pair, spread) + lax.rem(pair, spread)
         taps = jnp.concatenate(
             [
-                source[pl.ds(pl.multiple_of(start + (DMAX + (tap - 1) * spread) * span, 16), TILE), :]
-                for tap in range(3)
+                source[pl.ds(pl.multiple_of((first + DMAX + (tap - 1) * spread) * span, 16), span), :]
+                for tap in range(4)
             ],
             axis=1,
         )
-        return contract_last(weights[layer], taps)
+        mixing = jnp.dot(taps, weight_s[layer], preferred_element_type=f32)
+        return (first, mixing[:, :channels]), (first + spread, mixing[:, channels:])
 
     spread_taps(wide_s, first_s, rows + 2 * HALO, first_spread, pitch, pitch)
 
-    def one(step, carry):
-        start = pl.multiple_of(step * TILE, TILE)
-        hidden_s[pl.ds(start, TILE), :] = elu(mix(first_s, 0, start, first_spread, pitch)).T
+    def one(pair, carry):
+        for i, mixing in mix(first_s, 0, pair, first_spread, pitch):
+            hidden_s[pl.ds(pl.multiple_of(i * pitch, 8), pitch), :] = elu(mixing)
         return carry
 
-    lax.fori_loop(0, -(-tall * pitch // TILE), one, 0, unroll=2)
+    lax.fori_loop(0, row_pairs(tall), one, 0, unroll=3)
     for i in range(tall):
         place = row_first - DMAX + i
         if i < DMAX or i >= tall - DMAX:
@@ -452,23 +459,27 @@
 
     spread_taps(hidden_s, second_s, tall, second_spread, cols, cols)
 
-    def two(step, carry):
-        start = pl.multiple_of(step * TILE, TILE)
-        mixing = mix(second_s, 1, start, second_spread, cols).T
-        for k in range(TILE // cols):
-            i = step * (TILE // cols) + k
-            own = wide_s[pl.ds(pl.multiple_of((i + HALO) * pitch + HALO, 8), cols), :]
-            out_ref[i] = (own + mixing[k * cols : (k + 1) * cols]).astype(out_ref.dtype)
+    def two(pair, carry):
+        for i, mixing in mix(second_s, 1, pair, second_spread, cols):
+            own = wide_s[pl.ds(pl.multiple_of(jnp.minimum(i + HALO, rows + 2 * HALO - 1) * pitch + HALO, 8), cols), :]
+            out_s[i] = (own + mixing).astype(out_s.dtype)
         return carry
 
-    lax.fori_loop(0, rows * cols // TILE, two, 0, unroll=2)
+    lax.fori_loop(0, row_pairs(rows), two, 0, unroll=3)
+    copy = pltpu.make_async_copy(out_s.at[0:rows], out_ref, sem)
+    copy.start()
+    copy.wait()
+
+
+def row_pairs(count):
+    return max(d * -(-count // (2 * d)) for d in range(1, DMAX + 1))
 
 
 def pair_convolutions(dilations, blocks, margins, filters, length, swap):
     cols, channels = blocks[0].shape[1:]
     rows = (len(blocks) - 2) * HALO
     pitch = cols + 2 * HALO
-    padded = -(-(rows + 2 * DMAX) * pitch // TILE) * TILE
+    tall = rows + 2 * DMAX
     operands = (*blocks, *margins, filters)
     full = lambda shape: pl.BlockSpec(shape, functools.partial(lambda rank, g, s: (0,) * rank, len(shape)))
     return pl.pallas_call(
@@ -477,12 +488,15 @@
             num_scalar_prefetch=1,
             grid=(1,),
             in_specs=[full(x.shape) for x in operands],
-            out_specs=full((rows, cols, channels)),
+            out_specs=pl.BlockSpec(memory_space=pl.ANY),
             scratch_shapes=[
                 pltpu.VMEM(((rows + 2 * HALO) * pitch + HALO, channels), jnp.float32),
-                pltpu.VMEM((padded + 2 * DMAX * pitch, 3 * channels), jnp.bfloat16),
-                pltpu.VMEM((padded, channels), jnp.float32),
-                pltpu.VMEM(((rows + 2 * DMAX) * cols, 3 * channels), jnp.bfloat16),
+                pltpu.VMEM(((tall + 4 * DMAX) * pitch, 3 * channels), jnp.bfloat16),
+                pltpu.VMEM(((tall + 2 * DMAX) * pitch, channels), jnp.float32),
+                pltpu.VMEM(((rows + 4 * DMAX) * cols, 3 * channels), jnp.bfloat16),
+                pltpu.VMEM((2, 12 * channels, 2 * channels), jnp.bfloat16),
+                pltpu.VMEM((rows + 2 * DMAX, cols, channels), jnp.bfloat16),
+                pltpu.SemaphoreType.DMA,
             ],
         ),
         out_shape=jax.ShapeDtypeStruct((rows, cols, channels), jnp.bfloat16),
@@ -508,7 +522,7 @@
     near = first_sequences(tokens, gap_mask)
     near_there = exchange(near, "col", 1)
     far = exchange(near, "row", row_count // 2)
-    far_there = exchange(far, "col", 1)
+    far_there = exchange(near_there, "row", row_count // 2)
     table, second, turned = prepare(embedding, residue_filters, projection)
     near_parts = features(dilations, near, near_there, table, second, rows, cols)
     far_parts = features(dilations, far, far_there, table, second, rows, cols)

time: 149 us -> 95.3 us (0.64)
  Pallas kernels: 111 us -> 64.1 us
  local copies, waits for them, and re-layouts: 9.14 us -> 2.3 us
    pallas_call x2, Pallas kernels: 59.8 us -> 21 us  [features(): pl.pallas_call(functools.partial(feature_kernel, pitch=pitch), grid_spec=...]
    unnamed x37 -> x15, local copies, waits for them, and re-layouts: 9.14 us -> 2.3 us
    pallas_call x2, Pallas kernels: 33 us -> 27.6 us  [outer_products(): pl.pallas_call(functools.partial(outer_kernel, picks=picks, halves=len(ro...]
    pallas_call x1, Pallas kernels: 16.1 us -> 10.9 us  [pair_convolutions(): pl.pallas_call(functools.partial(conv_kernel, length=length, swap=swap, r...]
    pallas_call x1, Pallas kernels: 2.3 us -> 4.64 us  [prepare(): pl.pallas_call(prepare_kernel, out_shape=[jax.ShapeDtypeStruct((2 * chann...]
  transfers between devices with their start and end apart: 8 -> 8, of which waited for: 4 -> 4; matrix products, arithmetic and copies ran while one was open for 1% -> 0% of each run, Pallas kernels for 33% -> 30%
where the time goes in v2:
time: 95.3 us; the launch traced here: 95 us
  Pallas kernels  64.1 us (67%)
  waiting for transfers between devices  13.9 us (15%)
  starting transfers between devices  13.5 us (14%)
  local copies, waits for them, and re-layouts  2.3 us (2%)
    pallas_call x2, Pallas kernels, outer_products(): pl.pallas_call(functools.partial(outer_kernel, picks=picks, halves=len(ro...  27.6 us
    pallas_call x2, Pallas kernels, features(): pl.pallas_call(functools.partial(feature_kernel, pitch=pitch), grid_spec=...  21 us
    pallas_call x1, Pallas kernels, pair_convolutions(): pl.pallas_call(functools.partial(conv_kernel, length=length, swap=swap, r...  10.9 us
    ppermute x1, waiting for transfers between devices, per_device(): below = lax.ppermute(ends[0], 'row', [(i + 1, i) for i in steps])  8.39 us
    ppermute x6, starting transfers between devices, exchange(): return lax.ppermute(block, axis, [(i, i ^ bit) for i in range(count)])  8.38 us
    ppermute x6, waiting for transfers between devices, exchange(): return lax.ppermute(block, axis, [(i, i ^ bit) for i in range(count)])  5.49 us
    pallas_call x1, Pallas kernels, prepare(): pl.pallas_call(prepare_kernel, out_shape=[jax.ShapeDtypeStruct((2 * chann...  4.64 us
    ppermute x1, starting transfers between devices, per_device(): above = lax.ppermute(ends[1], 'row', [(i, i + 1) for i in steps])  3.85 us
  transfers between devices with their start and end apart: 8, of which 4 were waited for; matrix products, arithmetic and copies ran while one was open for 0% of the time, Pallas kernels for 30%

profile of v2, /device:TPU:0, one launch (start us, length us, event | category | flops | bytes accessed | tf_op | source)
XLA Modules:
  0.0 95.0 jit_solution(17889119772574482841)
XLA Ops:
  0.0 0.8 convert_bitcast_fusion
  0.8 3.1 %collective-permute-start = (bf16[1,2,32,256]{3,2,1,0:T(8,128)(2,1)S(1)}, bf16[1,2,32,256]{3,2,1,0:T(8,128)(2,1)S(1)}, u32[]{:S(2)}, u32[]{:S(2)}) collective-permute-start(bf16[1,2,32,256]{3,2,1,0:T(8,128)(2,1)S(1)} %pad_maximum_fusion.2), channel_id=1, source_target_pairs={{0,4},{2,6},{4,0},{6,2},{8,12},{10,14},{12,8},{14,10},{1,5},{3,7},... | collective-permute-start | bytes 98312 | tf_op jit(solution)/shard_map/ppermute | solution.py:33
  3.9 1.9 %collective-permute-done = bf16[1,2,32,256]{3,2,1,0:T(8,128)(2,1)S(1)} collective-permute-done((bf16[1,2,32,256]{3,2,1,0:T(8,128)(2,1)S(1)}, bf16[1,2,32,256]{3,2,1,0:T(8,128)(2,1)S(1)}, u32[]{:S(2)}, u32[]{:S(2)}) %collective-permute-start) | collective-permute-done | bytes 32800 | tf_op jit(solution)/shard_map/ppermute | solution.py:33
  5.8 2.0 %collective-permute-start.1 = (bf16[2,2,32,256]{3,2,1,0:T(8,128)(2,1)S(1)}, bf16[2,2,32,256]{3,2,1,0:T(8,128)(2,1)S(1)}, u32[]{:S(2)}, u32[]{:S(2)}) collective-permute-start(bf16[2,2,32,256]{3,2,1,0:T(8,128)(2,1)S(1)} %pad_maximum_fusion.1), channel_id=1, source_target_pairs={{0,2},{2,0},{4,6},{6,4},{8,10},{10,8},{12,14},{14,12},{1,3},{3,1},... | collective-permute-start | bytes 196616 | tf_op jit(solution)/shard_map/ppermute | solution.py:33
  7.8 2.3 %collective-permute-done.1 = bf16[2,2,32,256]{3,2,1,0:T(8,128)(2,1)S(1)} collective-permute-done((bf16[2,2,32,256]{3,2,1,0:T(8,128)(2,1)S(1)}, bf16[2,2,32,256]{3,2,1,0:T(8,128)(2,1)S(1)}, u32[]{:S(2)}, u32[]{:S(2)}) %collective-permute-start.1) | collective-permute-done | bytes 65568 | tf_op jit(solution)/shard_map/ppermute | solution.py:33
  10.2 0.1 collective-permute-start.2
  10.3 4.6 %shard_map.73 = (bf16[128,192]{1,0:T(8,128)(2,1)}, bf16[64,192]{1,0:T(8,128)(2,1)}, bf16[128,4096]{1,0:T(8,128)(2,1)}) custom-call(f32[21,64]{1,0:T(8,128)} %embedding_ref.1, f32[2,3,64,64]{3,2,1,0:T(8,128)} %filters_ref.1, bf16[4096,128]{1,0:T(8,128)(2,1)} %projection_ref.1), custom_call_target="tpu_custom_call" | custom-call | flops 1000000 | bytes 4194304 | tf_op jit(solution)/shard_map/pallas_call | solution.py:91
  14.9 3.0 %collective-permute-start.3 = (bf16[4,2,32,256]{3,2,1,0:T(8,128)(2,1)S(1)}, bf16[4,2,32,256]{3,2,1,0:T(8,128)(2,1)S(1)}, u32[]{:S(2)}, u32[]{:S(2)}) collective-permute-start(bf16[4,2,32,256]{3,2,1,0:T(8,128)(2,1)S(1)} %pad_maximum_fusion.here_ref), channel_id=1, source_target_pairs={{0,8},{2,10},{4,12},{6,14},{8,0},{10,2},{12,4},{14,6},{1,9},{3,11}... | collective-permute-start | bytes 393224 | tf_op jit(solution)/shard_map/ppermute | solution.py:33
  17.9 0.1 collective-permute-start.4
  18.0 0.7 copy-done.1
  18.7 0.8 copy-done.4
  19.5 0.8 copy-done.5
  20.2 10.4 %shard_map.74 = (bf16[32,64,256]{2,1,0:T(8,128)(2,1)S(1)}, bf16[64,128,256]{2,1,0:T(8,128)(2,1)S(1)}, bf16[32,256]{1,0:T(8,128)(2,1)S(1)}, bf16[128,256]{1,0:T(8,128)(2,1)S(1)}) custom-call(s32[4]{0:T(128)S(1)} %copy-done.1, bf16[4,2,32,256]{3,2,1,0:T(8,128)(2,1)S(1)} %pad_maximum_fusion.here_ref, ...), custom_call_target="tpu_custom_call" | custom-call | flops 6710886400 | bytes 5242880 | tf_op jit(solution)/shard_map/pallas_call | solution.py:246
  30.7 0.0 copy-start.3
  30.7 10.6 %shard_map.75 = (bf16[32,64,256]{2,1,0:T(8,128)(2,1)S(1)}, bf16[64,128,256]{2,1,0:T(8,128)(2,1)S(1)}, bf16[32,256]{1,0:T(8,128)(2,1)S(1)}, bf16[128,256]{1,0:T(8,128)(2,1)S(1)}) custom-call(s32[4]{0:T(128)S(1)} %copy-done.1, bf16[4,2,32,256]{3,2,1,0:T(8,128)(2,1)S(1)} %collective-permute-done.3.here_ref, ...), custom_call_target="tpu_custom_call" | custom-call | flops 6710886400 | bytes 5242880 | tf_op jit(solution)/shard_map/pallas_call | solution.py:246
  41.3 13.8 %shard_map.76 = (bf16[8,128,128]{2,1,0:T(8,128)(2,1)S(1)}, bf16[8,128,128]{2,1,0:T(8,128)(2,1)S(1)}, bf16[16,8,128]{2,1,0:T(8,128)(2,1)S(1)}) custom-call(bf16[32,64,256]{2,1,0:T(8,128)(2,1)S(1)} %get-tuple-element.24.refs_0_.refs_2_, bf16[32,64,256]{2,1,0:T(8,128)(2,1)S(1)} %get-tuple-element.25.refs_1_.refs_3_, ...), custom_call_target="tpu_custom_call" | custom-call | flops 10737418240 | bytes 9437184 | tf_op jit(solution)/shard_map/pallas_call | solution.py:348
  55.1 0.0 copy-start
  55.1 3.8 %collective-permute-start.5 = (bf16[8,128,128]{2,1,0:T(8,128)(2,1)S(1)}, bf16[8,128,128]{2,1,0:T(8,128)(2,1)S(1)}, u32[]{:S(2)}, u32[]{:S(2)}) collective-permute-start(bf16[8,128,128]{2,1,0:T(8,128)(2,1)S(1)} %get-tuple-element.33.refs_4_), channel_id=1, source_target_pairs={{0,2},{2,4},{4,6},{6,8},{8,10},{10,12},{12,14},{1,3},{3,5},{5,7},{... | collective-permute-start | bytes 786440 | tf_op jit(solution)/shard_map/ppermute | solution.py:534
  59.0 13.8 %shard_map.77 = (bf16[8,128,128]{2,1,0:T(8,128)(2,1)S(1)}, bf16[8,128,128]{2,1,0:T(8,128)(2,1)S(1)}, bf16[16,8,128]{2,1,0:T(8,128)(2,1)S(1)}) custom-call(bf16[32,64,256]{2,1,0:T(8,128)(2,1)S(1)} %get-tuple-element.24.refs_0_.refs_2_, bf16[32,64,256]{2,1,0:T(8,128)(2,1)S(1)} %get-tuple-element.25.refs_1_.refs_3_, ...), custom_call_target="tpu_custom_call" | custom-call | flops 10737418240 | bytes 9437184 | tf_op jit(solution)/shard_map/pallas_call | solution.py:348
  72.8 1.3 %collective-permute-start.6 = (bf16[8,128,128]{2,1,0:T(8,128)(2,1)S(1)}, bf16[8,128,128]{2,1,0:T(8,128)(2,1)S(1)}, u32[]{:S(2)}, u32[]{:S(2)}) collective-permute-start(bf16[8,128,128]{2,1,0:T(8,128)(2,1)S(1)} %get-tuple-element.34.refs_1_), channel_id=1, source_target_pairs={{2,0},{4,2},{6,4},{8,6},{10,8},{12,10},{14,12},{3,1},{5,3},{7,5},{... | collective-permute-start | bytes 786440 | tf_op jit(solution)/shard_map/ppermute | solution.py:535
  74.2 8.4 %collective-permute-done.6.refs_5_ = bf16[8,128,128]{2,1,0:T(8,128)(2,1)S(1)} collective-permute-done((bf16[8,128,128]{2,1,0:T(8,128)(2,1)S(1)}, bf16[8,128,128]{2,1,0:T(8,128)(2,1)S(1)}, u32[]{:S(2)}, u32[]{:S(2)}) %collective-permute-start.6) | collective-permute-done | bytes 262176 | tf_op jit(solution)/shard_map/ppermute | solution.py:535
  82.6 0.1 collective-permute-start.7
  82.6 1.3 %collective-permute-done.7.refs_6_ = bf16[48,8,128]{2,1,0:T(8,128)(2,1)S(1)} collective-permute-done((bf16[48,8,128]{2,1,0:T(8,128)(2,1)S(1)}, bf16[48,8,128]{2,1,0:T(8,128)(2,1)S(1)}, u32[]{:S(2)}, u32[]{:S(2)}) %collective-permute-start.7) | collective-permute-done | bytes 98336 | tf_op jit(solution)/shard_map/ppermute | solution.py:33
  83.9 10.9 %shard_map.78 = bf16[32,128,128]{2,1,0:T(8,128)(2,1)} custom-call(s32[4]{0:T(128)S(1)} %copy-done.2, bf16[8,128,128]{2,1,0:T(8,128)(2,1)S(1)} %collective-permute-done.5.refs_0_, bf16[8,128,128]{2,1,0:T(8,128)(2,1)S(1)} %get-tuple-element.34.refs_1_, bf16[8,128,128]{2,1,0:T(8,128)(2,1)S(1)} %get-tuple-element.35.refs_2_, ...), custom_call_target="tpu_custom_call" | custom-call | tf_op jit(solution)/shard_map/pallas_call | solution.py:485
  (19 shorter events, 0.1 us)
Async XLA Ops:
  0.8 5.0 %collective-permute-start = (bf16[1,2,32,256]{3,2,1,0:T(8,128)(2,1)S(1)}, bf16[1,2,32,256]{3,2,1,0:T(8,128)(2,1)S(1)}, u32[]{:S(2)}, u32[]{:S(2)}) collective-permute-start(bf16[1,2,32,256]{3,2,1,0:T(8,128)(2,1)S(1)} %pad_maximum_fusion.2), channel_id=1, source_target_pairs={{0,4},{2,6},{4,0},{6,2},{8,12},{10,14},{12,8},{14,10},{1,5},{3,7},... | collective-permute-start | bytes 98312 | tf_op jit(solution)/shard_map/ppermute | solution.py:33
  5.8 4.3 %collective-permute-start.1 = (bf16[2,2,32,256]{3,2,1,0:T(8,128)(2,1)S(1)}, bf16[2,2,32,256]{3,2,1,0:T(8,128)(2,1)S(1)}, u32[]{:S(2)}, u32[]{:S(2)}) collective-permute-start(bf16[2,2,32,256]{3,2,1,0:T(8,128)(2,1)S(1)} %pad_maximum_fusion.1), channel_id=1, source_target_pairs={{0,2},{2,0},{4,6},{6,4},{8,10},{10,8},{12,14},{14,12},{1,3},{3,1},... | collective-permute-start | bytes 196616 | tf_op jit(solution)/shard_map/ppermute | solution.py:33
  10.2 7.8 %collective-permute-start.2 = (bf16[4,2,32,256]{3,2,1,0:T(8,128)(2,1)S(1)}, bf16[4,2,32,256]{3,2,1,0:T(8,128)(2,1)S(1)}, u32[]{:S(2)}, u32[]{:S(2)}) collective-permute-start(bf16[4,2,32,256]{3,2,1,0:T(8,128)(2,1)S(1)} %pad_maximum_fusion.here_ref), channel_id=1, source_target_pairs={{0,1},{1,0},{2,3},{3,2},{4,5},{5,4},{6,7},{7,6},{8,9},{9,8},{10,11... | collective-permute-start | bytes 393224 | tf_op jit(solution)/shard_map/ppermute | solution.py:33
  14.9 15.8 %collective-permute-start.3 = (bf16[4,2,32,256]{3,2,1,0:T(8,128)(2,1)S(1)}, bf16[4,2,32,256]{3,2,1,0:T(8,128)(2,1)S(1)}, u32[]{:S(2)}, u32[]{:S(2)}) collective-permute-start(bf16[4,2,32,256]{3,2,1,0:T(8,128)(2,1)S(1)} %pad_maximum_fusion.here_ref), channel_id=1, source_target_pairs={{0,8},{2,10},{4,12},{6,14},{8,0},{10,2},{12,4},{14,6},{1,9},{3,11}... | collective-permute-start | bytes 393224 | tf_op jit(solution)/shard_map/ppermute | solution.py:33
  17.9 12.8 %collective-permute-start.4 = (bf16[4,2,32,256]{3,2,1,0:T(8,128)(2,1)S(1)}, bf16[4,2,32,256]{3,2,1,0:T(8,128)(2,1)S(1)}, u32[]{:S(2)}, u32[]{:S(2)}) collective-permute-start(bf16[4,2,32,256]{3,2,1,0:T(8,128)(2,1)S(1)} %collective-permute-done.2.there_ref), channel_id=1, source_target_pairs={{0,8},{2,10},{4,12},{6,14},{8,0},{10,2},{12,4},{14,6},{1,9},{3,11}... | collective-permute-start | bytes 393224 | tf_op jit(solution)/shard_map/ppermute | solution.py:33
  18.0 0.7 copy-start.1
  18.6 0.8 copy-start.4
  19.5 0.8 copy-start.5
  30.7 10.6 %copy-start.3 = (bf16[128,4096]{1,0:T(8,128)(2,1)S(1)}, bf16[128,4096]{1,0:T(8,128)(2,1)}, u32[]{:S(2)}) copy-start(bf16[128,4096]{1,0:T(8,128)(2,1)} %get-tuple-element.28.refs_6_) | copy-start | bytes 3145732
  55.1 28.8 %copy-start = (bf16[2,3,3,128,128]{4,3,2,1,0:T(8,128)(2,1)S(1)}, bf16[2,3,3,128,128]{4,3,2,1,0:T(8,128)(2,1)}, u32[]{:S(2)}) copy-start(bf16[2,3,3,128,128]{4,3,2,1,0:T(8,128)(2,1)} %param.13) | copy-start | bytes 1769476
  55.1 28.8 %copy-start.2 = (s32[4]{0:T(128)S(1)}, s32[4]{0:T(128)}, u32[]{:S(2)}) copy-start(s32[4]{0:T(128)} %dilations.5) | copy-start | bytes 52
  55.1 19.0 %collective-permute-start.5 = (bf16[8,128,128]{2,1,0:T(8,128)(2,1)S(1)}, bf16[8,128,128]{2,1,0:T(8,128)(2,1)S(1)}, u32[]{:S(2)}, u32[]{:S(2)}) collective-permute-start(bf16[8,128,128]{2,1,0:T(8,128)(2,1)S(1)} %get-tuple-element.33.refs_4_), channel_id=1, source_target_pairs={{0,2},{2,4},{4,6},{6,8},{8,10},{10,12},{12,14},{1,3},{3,5},{5,7},{... | collective-permute-start | bytes 786440 | tf_op jit(solution)/shard_map/ppermute | solution.py:534
  72.8 9.8 %collective-permute-start.6 = (bf16[8,128,128]{2,1,0:T(8,128)(2,1)S(1)}, bf16[8,128,128]{2,1,0:T(8,128)(2,1)S(1)}, u32[]{:S(2)}, u32[]{:S(2)}) collective-permute-start(bf16[8,128,128]{2,1,0:T(8,128)(2,1)S(1)} %get-tuple-element.34.refs_1_), channel_id=1, source_target_pairs={{2,0},{4,2},{6,4},{8,6},{10,8},{12,10},{14,12},{3,1},{5,3},{7,5},{... | collective-permute-start | bytes 786440 | tf_op jit(solution)/shard_map/ppermute | solution.py:535
  82.6 1.4 %collective-permute-start.7 = (bf16[48,8,128]{2,1,0:T(8,128)(2,1)S(1)}, bf16[48,8,128]{2,1,0:T(8,128)(2,1)S(1)}, u32[]{:S(2)}, u32[]{:S(2)}) collective-permute-start(bf16[48,8,128]{2,1,0:T(8,128)(2,1)S(1)} %fusion), channel_id=1, source_target_pairs={{0,1},{1,0},{2,3},{3,2},{4,5},{5,4},{6,7},{7,6},{8,9},{9,8},{10,11... | collective-permute-start | bytes 294920 | tf_op jit(solution)/shard_map/ppermute | solution.py:33

commit v3 on v2

--- a/solution.py
+++ b/solution.py
@@ -22,6 +22,10 @@
     return jnp.maximum(x, jnp.exp(jnp.minimum(x, 0.0)) - 1.0)
 
 
+def in_hbm(array):
+    return pltpu.with_memory_space_constraint(array, pltpu.HBM)
+
+
 def contract_last(left, right):
     return lax.dot_general(
         left, right, (((1,), (1,)), ((), ())), preferred_element_type=jnp.float32
@@ -42,7 +46,7 @@
     return half
 
 
-def prepare_kernel(embedding_ref, filters_ref, projection_ref, table_ref, second_ref, turned_ref, letter_s, turn_s):
+def prepare_kernel(embedding_ref, filters_ref, table_ref, second_ref, letter_s):
     letters, channels = embedding_ref.shape
     kinds = letter_s.shape[0]
     f32, bf16 = jnp.float32, jnp.bfloat16
@@ -65,43 +69,24 @@
                 start = (part * 3 + tap) * kinds
                 table_ref[first : first + channels, start : start + kinds] = piece
         second_ref[:, tap * channels : (tap + 1) * channels] = filters_ref[1, tap].astype(bf16)
-    pitch = turn_s.shape[0] // channels
-
-    def widen(a, carry):
-        start = pl.multiple_of(a * channels, channels)
-        turn_s[pl.ds(pl.multiple_of(a * pitch, 8), channels), :] = projection_ref[pl.ds(start, channels), :].astype(f32)
-        return carry
-
-    lax.fori_loop(0, channels, widen, 0, unroll=4)
-
-    def turn(step, carry):
-        pair = jnp.concatenate([turn_s[pl.ds(2 * step + k, channels, stride=pitch), :] for k in range(2)], axis=0)
-        start = pl.multiple_of(step * 2 * channels, 2 * channels)
-        turned_ref[:, pl.ds(start, 2 * channels)] = pair.T.astype(bf16)
-        return carry
-
-    lax.fori_loop(0, channels // 2, turn, 0, unroll=2)
-
-
-def prepare(embedding, filters, projection):
+
+
+def prepare(embedding, filters):
     letters, channels = embedding.shape
     kinds = -(-letters // 32) * 32
-    out = projection.shape[1]
     bf16 = jnp.bfloat16
     return pl.pallas_call(
         prepare_kernel,
         out_shape=[
             jax.ShapeDtypeStruct((2 * channels, 6 * kinds), bf16),
             jax.ShapeDtypeStruct((channels, 3 * channels), bf16),
-            jax.ShapeDtypeStruct((out, channels * channels), bf16),
         ],
         scratch_shapes=[
             pltpu.VMEM((kinds, channels), jnp.float32),
-            pltpu.VMEM((channels * (channels + 8), out), jnp.float32),
         ],
         compiler_params=pltpu.CompilerParams(vmem_limit_bytes=62 << 20),
-        cost_estimate=pl.CostEstimate(flops=10**6, bytes_accessed=4 << 20, transcendentals=0),
-    )(embedding, filters, projection)
+        cost_estimate=pl.CostEstimate(flops=10**6, bytes_accessed=1 << 18, transcendentals=0),
+    )(in_hbm(embedding), in_hbm(filters))
 
 
 def feature_kernel(
@@ -278,7 +263,7 @@
             bytes_accessed=2 * channels * width * (rows + cols),
             transcendentals=2 * channels * width * (rows + cols),
         ),
-    )(dilations, here, there, table, second)
+    )(in_hbm(dilations), here, there, in_hbm(table), in_hbm(second))
 
 
 def outer_kernel(*refs, picks, halves, swap):
@@ -286,9 +271,9 @@
     row_refs = refs[: halves * count]
     col_refs = refs[halves * count : halves * (count + 1)]
     projection_ref = refs[halves * (count + 1)]
-    marks = refs[halves * (count + 1) + 1 : -(count + 2)]
-    pair_refs = refs[-(count + 2) : -2]
-    edge_ref, sum_s = refs[-2:]
+    marks = refs[halves * (count + 1) + 1 : -(count + 3)]
+    pair_refs = refs[-(count + 3) : -3]
+    edge_ref, sum_s, turn_s = refs[-3:]
     step = pl.program_id(0)
     group, cols, _ = col_refs[0].shape
     channels = row_refs[0].shape[1]
@@ -306,7 +291,14 @@
         ],
         axis=0,
     )
-    projection = projection_ref[...]
+    pitch = turn_s.shape[0] // channels
+    for a in range(channels):
+        turn_s[a * pitch : a * pitch + group, :] = projection_ref[a].astype(jnp.float32)
+    turned = []
+    for b in range(0, group, 2):
+        pair = jnp.concatenate([turn_s[pl.ds(b + k, channels, stride=pitch), :] for k in range(2)], axis=0)
+        turned.append(pair.T.astype(jnp.bfloat16))
+    projection = jnp.concatenate(turned, axis=1)
     outer = contract_last(left, right).astype(jnp.bfloat16)
     for pair in range(0, rows, 2):
         sides = [
@@ -340,7 +332,7 @@
 def outer_products(row_feats, col_feats, projection, row_marks, col_marks, picks, swap, group=8):
     _, channels, _ = row_feats[0].shape
     cols = col_feats[0].shape[1]
-    out = projection.shape[0]
+    out = projection.shape[2]
     total = sum(x.shape[2] for x in row_feats)
     tall = len(picks) * HALO
     full = lambda shape: pl.BlockSpec(shape, functools.partial(lambda rank, g: (0,) * rank, len(shape)))
@@ -351,10 +343,13 @@
             grid=(channels // group,),
             in_specs=[picked(pick, x.shape[2]) for pick in picks for x in row_feats]
             + [pl.BlockSpec((group, cols, x.shape[2]), lambda g: (g, 0, 0)) for x in col_feats]
-            + [pl.BlockSpec((out, group * channels), lambda g: (0, g))]
+            + [pl.BlockSpec((channels, group, out), lambda g: (0, g, 0))]
             + [full(x.shape) for x in (*row_marks, *col_marks)],
             out_specs=[full((HALO, cols, out)) for _ in picks] + [full((tall, HALO, out))],
-            scratch_shapes=[pltpu.VMEM((tall // 2, out, 2 * cols), jnp.float32)],
+            scratch_shapes=[
+                pltpu.VMEM((tall // 2, out, 2 * cols), jnp.float32),
+                pltpu.VMEM((channels * (group + 1), out), jnp.float32),
+            ],
         ),
         out_shape=[jax.ShapeDtypeStruct((HALO, cols, out), jnp.bfloat16) for _ in picks]
         + [jax.ShapeDtypeStruct((tall, HALO, out), jnp.bfloat16)],
@@ -501,7 +496,7 @@
         ),
         out_shape=jax.ShapeDtypeStruct((rows, cols, channels), jnp.bfloat16),
         compiler_params=pltpu.CompilerParams(vmem_limit_bytes=40 << 20),
-    )(dilations, *operands)
+    )(in_hbm(dilations), *operands)
 
 
 def col_margins(tall):
@@ -523,12 +518,14 @@
     near_there = exchange(near, "col", 1)
     far = exchange(near, "row", row_count // 2)
     far_there = exchange(near_there, "row", row_count // 2)
-    table, second, turned = prepare(embedding, residue_filters, projection)
+    table, second = prepare(embedding, residue_filters)
+    channels = embedding.shape[1]
+    blocks = projection.reshape(channels, channels, projection.shape[1])
     near_parts = features(dilations, near, near_there, table, second, rows, cols)
     far_parts = features(dilations, far, far_there, table, second, rows, cols)
     row_feats, col_feats, row_marks, col_marks = zip(near_parts, far_parts)
     last = rows // HALO - 1
-    run = functools.partial(outer_products, row_feats, col_feats, turned, row_marks, col_marks, swap=swap)
+    run = functools.partial(outer_products, row_feats, col_feats, blocks, row_marks, col_marks, swap=swap)
     ends, end_edges = run(picks=(0, last))
     steps = range(row_count - 1)
     above = lax.ppermute(ends[1], "row", [(i, i + 1) for i in steps])

time: 95.3 us -> 93.8 us (0.984)
  local copies, waits for them, and re-layouts: 2.3 us -> 0.04 us
    pallas_call x1, Pallas kernels: 4.64 us -> 1.91 us  [prepare(): pl.pallas_call(prepare_kernel, out_shape=[jax.ShapeDtypeStruct((2 * chann...]
    pallas_call x2, Pallas kernels: 21 us -> 23.3 us  [features(): pl.pallas_call(functools.partial(feature_kernel, pitch=pitch), grid_spec=...]
    unnamed x15 -> x7, local copies, waits for them, and re-layouts: 2.3 us -> 0.04 us
  transfers between devices with their start and end apart: 8 -> 8, of which waited for: 4 -> 5; matrix products, arithmetic and copies ran while one was open for 0% -> 0% of each run, Pallas kernels for 30% -> 30%
where the time goes in v3:
time: 93.8 us; the launch traced here: 93.4 us
  Pallas kernels  64.4 us (69%)
  waiting for transfers between devices  14.5 us (15%)
  starting transfers between devices  13.3 us (14%)
    pallas_call x2, Pallas kernels, outer_products(): pl.pallas_call(functools.partial(outer_kernel, picks=picks, halves=len(ro...  28.2 us
    pallas_call x2, Pallas kernels, features(): pl.pallas_call(functools.partial(feature_kernel, pitch=pitch), grid_spec=...  23.3 us
    pallas_call x1, Pallas kernels, pair_convolutions(): pl.pallas_call(functools.partial(conv_kernel, length=length, swap=swap, r...  11 us
    ppermute x6, starting transfers between devices, exchange(): return lax.ppermute(block, axis, [(i, i ^ bit) for i in range(count)])  8.39 us
    ppermute x1, waiting for transfers between devices, per_device(): below = lax.ppermute(ends[0], 'row', [(i + 1, i) for i in steps])  8.11 us
    ppermute x6, waiting for transfers between devices, exchange(): return lax.ppermute(block, axis, [(i, i ^ bit) for i in range(count)])  6.39 us
    ppermute x1, starting transfers between devices, per_device(): above = lax.ppermute(ends[1], 'row', [(i, i + 1) for i in steps])  3.6 us
    pallas_call x1, Pallas kernels, prepare(): pl.pallas_call(prepare_kernel, out_shape=[jax.ShapeDtypeStruct((2 * chann...  1.91 us
  transfers between devices with their start and end apart: 8, of which 5 were waited for; matrix products, arithmetic and copies ran while one was open for 0% of the time, Pallas kernels for 30%

profile of v3, /device:TPU:0, one launch (start us, length us, event | category | flops | bytes accessed | tf_op | source)
XLA Modules:
  0.0 93.4 jit_solution(5023798370384651724)
XLA Ops:
  0.0 0.8 convert_bitcast_fusion
  0.8 3.1 %collective-permute-start = (bf16[1,2,32,256]{3,2,1,0:T(8,128)(2,1)S(1)}, bf16[1,2,32,256]{3,2,1,0:T(8,128)(2,1)S(1)}, u32[]{:S(2)}, u32[]{:S(2)}) collective-permute-start(bf16[1,2,32,256]{3,2,1,0:T(8,128)(2,1)S(1)} %pad_maximum_fusion.2), channel_id=1, source_target_pairs={{0,4},{2,6},{4,0},{6,2},{8,12},{10,14},{12,8},{14,10},{1,5},{3,7},... | collective-permute-start | bytes 98312 | tf_op jit(solution)/shard_map/ppermute | solution.py:37
  3.9 1.9 %collective-permute-done = bf16[1,2,32,256]{3,2,1,0:T(8,128)(2,1)S(1)} collective-permute-done((bf16[1,2,32,256]{3,2,1,0:T(8,128)(2,1)S(1)}, bf16[1,2,32,256]{3,2,1,0:T(8,128)(2,1)S(1)}, u32[]{:S(2)}, u32[]{:S(2)}) %collective-permute-start) | collective-permute-done | bytes 32800 | tf_op jit(solution)/shard_map/ppermute | solution.py:37
  5.8 2.0 %collective-permute-start.1 = (bf16[2,2,32,256]{3,2,1,0:T(8,128)(2,1)S(1)}, bf16[2,2,32,256]{3,2,1,0:T(8,128)(2,1)S(1)}, u32[]{:S(2)}, u32[]{:S(2)}) collective-permute-start(bf16[2,2,32,256]{3,2,1,0:T(8,128)(2,1)S(1)} %pad_maximum_fusion.1), channel_id=1, source_target_pairs={{0,2},{2,0},{4,6},{6,4},{8,10},{10,8},{12,14},{14,12},{1,3},{3,1},... | collective-permute-start | bytes 196616 | tf_op jit(solution)/shard_map/ppermute | solution.py:37
  7.8 2.3 %collective-permute-done.1 = bf16[2,2,32,256]{3,2,1,0:T(8,128)(2,1)S(1)} collective-permute-done((bf16[2,2,32,256]{3,2,1,0:T(8,128)(2,1)S(1)}, bf16[2,2,32,256]{3,2,1,0:T(8,128)(2,1)S(1)}, u32[]{:S(2)}, u32[]{:S(2)}) %collective-permute-start.1) | collective-permute-done | bytes 65568 | tf_op jit(solution)/shard_map/ppermute | solution.py:37
  10.2 0.1 collective-permute-start.2
  10.3 1.9 %shard_map.73 = (bf16[128,192]{1,0:T(8,128)(2,1)}, bf16[64,192]{1,0:T(8,128)(2,1)}) custom-call(f32[21,64]{1,0:T(8,128)} %embedding_ref.1, f32[2,3,64,64]{3,2,1,0:T(8,128)} %filters_ref.1), custom_call_target="tpu_custom_call" | custom-call | flops 1000000 | bytes 262144 | tf_op jit(solution)/shard_map/pallas_call | solution.py:78
  12.2 3.0 %collective-permute-start.3 = (bf16[4,2,32,256]{3,2,1,0:T(8,128)(2,1)S(1)}, bf16[4,2,32,256]{3,2,1,0:T(8,128)(2,1)S(1)}, u32[]{:S(2)}, u32[]{:S(2)}) collective-permute-start(bf16[4,2,32,256]{3,2,1,0:T(8,128)(2,1)S(1)} %pad_maximum_fusion.here_ref), channel_id=1, source_target_pairs={{0,8},{2,10},{4,12},{6,14},{8,0},{10,2},{12,4},{14,6},{1,9},{3,11}... | collective-permute-start | bytes 393224 | tf_op jit(solution)/shard_map/ppermute | solution.py:37
  15.2 0.0 collective-permute-done.2.there_ref
  15.2 0.1 collective-permute-start.4
  15.3 11.6 %shard_map.74 = (bf16[32,64,256]{2,1,0:T(8,128)(2,1)S(1)}, bf16[64,128,256]{2,1,0:T(8,128)(2,1)S(1)}, bf16[32,256]{1,0:T(8,128)(2,1)S(1)}, bf16[128,256]{1,0:T(8,128)(2,1)S(1)}) custom-call(s32[4]{0:T(128)} %dilations.5, bf16[4,2,32,256]{3,2,1,0:T(8,128)(2,1)S(1)} %pad_maximum_fusion.here_ref, bf16[4,2,32,256]{3,2,1,0:T(8,128)(2,1)S(1)} %collective-permute-done.2.there_ref, ...), custom_call_target="tpu_custom_call" | custom-call | flops 6710886400 | bytes 5242880 | tf_op jit(solution)/shard_map/pallas_call | solution.py:231
  26.8 0.0 copy-start.1
  26.9 0.0 collective-permute-done.3.here_ref
  26.9 0.9 collective-permute-done.4.there_ref
  27.8 11.8 %shard_map.75 = (bf16[32,64,256]{2,1,0:T(8,128)(2,1)S(1)}, bf16[64,128,256]{2,1,0:T(8,128)(2,1)S(1)}, bf16[32,256]{1,0:T(8,128)(2,1)S(1)}, bf16[128,256]{1,0:T(8,128)(2,1)S(1)}) custom-call(s32[4]{0:T(128)} %dilations.5, bf16[4,2,32,256]{3,2,1,0:T(8,128)(2,1)S(1)} %collective-permute-done.3.here_ref, ...), custom_call_target="tpu_custom_call" | custom-call | flops 6710886400 | bytes 5242880 | tf_op jit(solution)/shard_map/pallas_call | solution.py:231
  39.5 14.1 %shard_map.76 = (bf16[8,128,128]{2,1,0:T(8,128)(2,1)S(1)}, bf16[8,128,128]{2,1,0:T(8,128)(2,1)S(1)}, bf16[16,8,128]{2,1,0:T(8,128)(2,1)S(1)}) custom-call(bf16[32,64,256]{2,1,0:T(8,128)(2,1)S(1)} %get-tuple-element.23.refs_0_.refs_2_, bf16[32,64,256]{2,1,0:T(8,128)(2,1)S(1)} %get-tuple-element.24.refs_1_.refs_3_, ...), custom_call_target="tpu_custom_call" | custom-call | flops 10737418240 | bytes 9437184 | tf_op jit(solution)/shard_map/pallas_call | solution.py:340
  53.7 0.0 copy-start
  53.7 3.6 %collective-permute-start.5 = (bf16[8,128,128]{2,1,0:T(8,128)(2,1)S(1)}, bf16[8,128,128]{2,1,0:T(8,128)(2,1)S(1)}, u32[]{:S(2)}, u32[]{:S(2)}) collective-permute-start(bf16[8,128,128]{2,1,0:T(8,128)(2,1)S(1)} %get-tuple-element.31.refs_4_), channel_id=1, source_target_pairs={{0,2},{2,4},{4,6},{6,8},{8,10},{10,12},{12,14},{1,3},{3,5},{5,7},{... | collective-permute-start | bytes 786440 | tf_op jit(solution)/shard_map/ppermute | solution.py:531
  57.3 14.1 %shard_map.77 = (bf16[8,128,128]{2,1,0:T(8,128)(2,1)S(1)}, bf16[8,128,128]{2,1,0:T(8,128)(2,1)S(1)}, bf16[16,8,128]{2,1,0:T(8,128)(2,1)S(1)}) custom-call(bf16[32,64,256]{2,1,0:T(8,128)(2,1)S(1)} %get-tuple-element.23.refs_0_.refs_2_, bf16[32,64,256]{2,1,0:T(8,128)(2,1)S(1)} %get-tuple-element.24.refs_1_.refs_3_, ...), custom_call_target="tpu_custom_call" | custom-call | flops 10737418240 | bytes 9437184 | tf_op jit(solution)/shard_map/pallas_call | solution.py:340
  71.4 1.3 %collective-permute-start.6 = (bf16[8,128,128]{2,1,0:T(8,128)(2,1)S(1)}, bf16[8,128,128]{2,1,0:T(8,128)(2,1)S(1)}, u32[]{:S(2)}, u32[]{:S(2)}) collective-permute-start(bf16[8,128,128]{2,1,0:T(8,128)(2,1)S(1)} %get-tuple-element.32.refs_1_), channel_id=1, source_target_pairs={{2,0},{4,2},{6,4},{8,6},{10,8},{12,10},{14,12},{3,1},{5,3},{7,5},{... | collective-permute-start | bytes 786440 | tf_op jit(solution)/shard_map/ppermute | solution.py:532
  72.8 8.1 %collective-permute-done.6.refs_5_ = bf16[8,128,128]{2,1,0:T(8,128)(2,1)S(1)} collective-permute-done((bf16[8,128,128]{2,1,0:T(8,128)(2,1)S(1)}, bf16[8,128,128]{2,1,0:T(8,128)(2,1)S(1)}, u32[]{:S(2)}, u32[]{:S(2)}) %collective-permute-start.6) | collective-permute-done | bytes 262176 | tf_op jit(solution)/shard_map/ppermute | solution.py:532
  80.9 0.1 collective-permute-start.7
  81.0 1.3 %collective-permute-done.7.refs_6_ = bf16[48,8,128]{2,1,0:T(8,128)(2,1)S(1)} collective-permute-done((bf16[48,8,128]{2,1,0:T(8,128)(2,1)S(1)}, bf16[48,8,128]{2,1,0:T(8,128)(2,1)S(1)}, u32[]{:S(2)}, u32[]{:S(2)}) %collective-permute-start.7) | collective-permute-done | bytes 98336 | tf_op jit(solution)/shard_map/ppermute | solution.py:37
  82.3 11.0 %shard_map.78 = bf16[32,128,128]{2,1,0:T(8,128)(2,1)} custom-call(s32[4]{0:T(128)} %dilations.5, bf16[8,128,128]{2,1,0:T(8,128)(2,1)S(1)} %collective-permute-done.5.refs_0_, bf16[8,128,128]{2,1,0:T(8,128)(2,1)S(1)} %get-tuple-element.32.refs_1_, bf16[8,128,128]{2,1,0:T(8,128)(2,1)S(1)} %get-tuple-element.33.refs_2_, ...), custom_call_target="tpu_custom_call" | custom-call | tf_op jit(solution)/shard_map/pallas_call | solution.py:480
  (11 shorter events, 0.1 us)
Async XLA Ops:
  0.8 5.0 %collective-permute-start = (bf16[1,2,32,256]{3,2,1,0:T(8,128)(2,1)S(1)}, bf16[1,2,32,256]{3,2,1,0:T(8,128)(2,1)S(1)}, u32[]{:S(2)}, u32[]{:S(2)}) collective-permute-start(bf16[1,2,32,256]{3,2,1,0:T(8,128)(2,1)S(1)} %pad_maximum_fusion.2), channel_id=1, source_target_pairs={{0,4},{2,6},{4,0},{6,2},{8,12},{10,14},{12,8},{14,10},{1,5},{3,7},... | collective-permute-start | bytes 98312 | tf_op jit(solution)/shard_map/ppermute | solution.py:37
  5.8 4.3 %collective-permute-start.1 = (bf16[2,2,32,256]{3,2,1,0:T(8,128)(2,1)S(1)}, bf16[2,2,32,256]{3,2,1,0:T(8,128)(2,1)S(1)}, u32[]{:S(2)}, u32[]{:S(2)}) collective-permute-start(bf16[2,2,32,256]{3,2,1,0:T(8,128)(2,1)S(1)} %pad_maximum_fusion.1), channel_id=1, source_target_pairs={{0,2},{2,0},{4,6},{6,4},{8,10},{10,8},{12,14},{14,12},{1,3},{3,1},... | collective-permute-start | bytes 196616 | tf_op jit(solution)/shard_map/ppermute | solution.py:37
  10.2 5.0 %collective-permute-start.2 = (bf16[4,2,32,256]{3,2,1,0:T(8,128)(2,1)S(1)}, bf16[4,2,32,256]{3,2,1,0:T(8,128)(2,1)S(1)}, u32[]{:S(2)}, u32[]{:S(2)}) collective-permute-start(bf16[4,2,32,256]{3,2,1,0:T(8,128)(2,1)S(1)} %pad_maximum_fusion.here_ref), channel_id=1, source_target_pairs={{0,1},{1,0},{2,3},{3,2},{4,5},{5,4},{6,7},{7,6},{8,9},{9,8},{10,11... | collective-permute-start | bytes 393224 | tf_op jit(solution)/shard_map/ppermute | solution.py:37
  12.2 14.7 %collective-permute-start.3 = (bf16[4,2,32,256]{3,2,1,0:T(8,128)(2,1)S(1)}, bf16[4,2,32,256]{3,2,1,0:T(8,128)(2,1)S(1)}, u32[]{:S(2)}, u32[]{:S(2)}) collective-permute-start(bf16[4,2,32,256]{3,2,1,0:T(8,128)(2,1)S(1)} %pad_maximum_fusion.here_ref), channel_id=1, source_target_pairs={{0,8},{2,10},{4,12},{6,14},{8,0},{10,2},{12,4},{14,6},{1,9},{3,11}... | collective-permute-start | bytes 393224 | tf_op jit(solution)/shard_map/ppermute | solution.py:37
  15.2 12.6 %collective-permute-start.4 = (bf16[4,2,32,256]{3,2,1,0:T(8,128)(2,1)S(1)}, bf16[4,2,32,256]{3,2,1,0:T(8,128)(2,1)S(1)}, u32[]{:S(2)}, u32[]{:S(2)}) collective-permute-start(bf16[4,2,32,256]{3,2,1,0:T(8,128)(2,1)S(1)} %collective-permute-done.2.there_ref), channel_id=1, source_target_pairs={{0,8},{2,10},{4,12},{6,14},{8,0},{10,2},{12,4},{14,6},{1,9},{3,11}... | collective-permute-start | bytes 393224 | tf_op jit(solution)/shard_map/ppermute | solution.py:37
  26.8 12.7 %copy-start.1 = (bf16[4096,128]{1,0:T(8,128)(2,1)S(1)}, bf16[4096,128]{1,0:T(8,128)(2,1)}, u32[]{:S(2)}) copy-start(bf16[4096,128]{1,0:T(8,128)(2,1)} %param.12) | copy-start | bytes 3145732
  53.7 28.6 %copy-start = (bf16[2,3,3,128,128]{4,3,2,1,0:T(8,128)(2,1)S(1)}, bf16[2,3,3,128,128]{4,3,2,1,0:T(8,128)(2,1)}, u32[]{:S(2)}) copy-start(bf16[2,3,3,128,128]{4,3,2,1,0:T(8,128)(2,1)} %param.13) | copy-start | bytes 1769476
  53.7 19.0 %collective-permute-start.5 = (bf16[8,128,128]{2,1,0:T(8,128)(2,1)S(1)}, bf16[8,128,128]{2,1,0:T(8,128)(2,1)S(1)}, u32[]{:S(2)}, u32[]{:S(2)}) collective-permute-start(bf16[8,128,128]{2,1,0:T(8,128)(2,1)S(1)} %get-tuple-element.31.refs_4_), channel_id=1, source_target_pairs={{0,2},{2,4},{4,6},{6,8},{8,10},{10,12},{12,14},{1,3},{3,5},{5,7},{... | collective-permute-start | bytes 786440 | tf_op jit(solution)/shard_map/ppermute | solution.py:531
  71.4 9.5 %collective-permute-start.6 = (bf16[8,128,128]{2,1,0:T(8,128)(2,1)S(1)}, bf16[8,128,128]{2,1,0:T(8,128)(2,1)S(1)}, u32[]{:S(2)}, u32[]{:S(2)}) collective-permute-start(bf16[8,128,128]{2,1,0:T(8,128)(2,1)S(1)} %get-tuple-element.32.refs_1_), channel_id=1, source_target_pairs={{2,0},{4,2},{6,4},{8,6},{10,8},{12,10},{14,12},{3,1},{5,3},{7,5},{... | collective-permute-start | bytes 786440 | tf_op jit(solution)/shard_map/ppermute | solution.py:532
  80.9 1.4 %collective-permute-start.7 = (bf16[48,8,128]{2,1,0:T(8,128)(2,1)S(1)}, bf16[48,8,128]{2,1,0:T(8,128)(2,1)S(1)}, u32[]{:S(2)}, u32[]{:S(2)}) collective-permute-start(bf16[48,8,128]{2,1,0:T(8,128)(2,1)S(1)} %fusion), channel_id=1, source_target_pairs={{0,1},{1,0},{2,3},{3,2},{4,5},{5,4},{6,7},{7,6},{8,9},{9,8},{10,11... | collective-permute-start | bytes 294920 | tf_op jit(solution)/shard_map/ppermute | solution.py:37

commit v4 on v3

--- a/solution.py
+++ b/solution.py
@@ -84,7 +84,7 @@
         scratch_shapes=[
             pltpu.VMEM((kinds, channels), jnp.float32),
         ],
-        compiler_params=pltpu.CompilerParams(vmem_limit_bytes=62 << 20),
+        compiler_params=pltpu.CompilerParams(vmem_limit_bytes=16 << 20),
         cost_estimate=pl.CostEstimate(flops=10**6, bytes_accessed=1 << 18, transcendentals=0),
     )(in_hbm(embedding), in_hbm(filters))
 
@@ -219,9 +219,10 @@
         leave(step).wait()
 
 
-def features(dilations, here, there, table, second, rows, cols):
-    blocks, _, each, length = here.shape
-    width = 2 * blocks * each
+def features(dilations, sequences, table, second, rows, cols):
+    blocks, _, each, length = sequences.shape
+    width = blocks * each
+    side = (blocks // 2, 2, each, length)
     channels = second.shape[0]
     kinds = table.shape[1] // 6
     span = max(rows, cols) + 2 * HALO
@@ -233,7 +234,8 @@
         grid_spec=pltpu.PrefetchScalarGridSpec(
             num_scalar_prefetch=1,
             grid=(1,),
-            in_specs=[full(x.shape) for x in (here, there, table, second)],
+            in_specs=[pl.BlockSpec(side, lambda g, s: (0, 0, 0, 0)), pl.BlockSpec(side, lambda g, s: (1, 0, 0, 0))]
+            + [full(x.shape) for x in (table, second)],
             out_specs=[
                 full((rows, channels, width)),
                 pl.BlockSpec(memory_space=pl.ANY),
@@ -263,7 +265,7 @@
             bytes_accessed=2 * channels * width * (rows + cols),
             transcendentals=2 * channels * width * (rows + cols),
         ),
-    )(in_hbm(dilations), here, there, in_hbm(table), in_hbm(second))
+    )(dilations, sequences, sequences, table, second)
 
 
 def outer_kernel(*refs, picks, halves, swap):
@@ -496,7 +498,7 @@
         ),
         out_shape=jax.ShapeDtypeStruct((rows, cols, channels), jnp.bfloat16),
         compiler_params=pltpu.CompilerParams(vmem_limit_bytes=40 << 20),
-    )(in_hbm(dilations), *operands)
+    )(dilations, *operands)
 
 
 def col_margins(tall):
@@ -516,13 +518,13 @@
     swap = col_count == 2
     near = first_sequences(tokens, gap_mask)
     near_there = exchange(near, "col", 1)
-    far = exchange(near, "row", row_count // 2)
-    far_there = exchange(near_there, "row", row_count // 2)
+    near_both = jnp.concatenate([near, near_there])
+    far_both = exchange(near_both, "row", row_count // 2)
     table, second = prepare(embedding, residue_filters)
     channels = embedding.shape[1]
     blocks = projection.reshape(channels, channels, projection.shape[1])
-    near_parts = features(dilations, near, near_there, table, second, rows, cols)
-    far_parts = features(dilations, far, far_there, table, second, rows, cols)
+    near_parts = features(dilations, near_both, table, second, rows, cols)
+    far_parts = features(dilations, far_both, table, second, rows, cols)
     row_feats, col_feats, row_marks, col_marks = zip(near_parts, far_parts)
     last = rows // HALO - 1
     run = functools.partial(outer_products, row_feats, col_feats, blocks, row_marks, col_marks, swap=swap)

time: 93.8 us -> 92 us (0.981)
  Pallas kernels: 64.4 us -> 61.4 us
    pallas_call x2, Pallas kernels: 23.3 us -> 21 us  [features(): pl.pallas_call(functools.partial(feature_kernel, pitch=pitch), grid_spec=...]
    ppermute x6 -> x5, waiting for transfers between devices: 6.39 us -> 7 us  [exchange(): return lax.ppermute(block, axis, [(i, i ^ bit) for i in range(count)])]
    ppermute x6 -> x5, starting transfers between devices: 8.39 us -> 8.39 us  [exchange(): return lax.ppermute(block, axis, [(i, i ^ bit) for i in range(count)])]
  transfers between devices with their start and end apart: 8 -> 7, of which waited for: 5 -> 6; matrix products, arithmetic and copies ran while one was open for 0% -> 0% of each run, Pallas kernels for 30% -> 28%
where the time goes in v4:
time: 92 us; the launch traced here: 91.6 us
  Pallas kernels  61.4 us (67%)
  waiting for transfers between devices  15.1 us (16%)
  starting transfers between devices  13.3 us (14%)
    pallas_call x2, Pallas kernels, outer_products(): pl.pallas_call(functools.partial(outer_kernel, picks=picks, halves=len(ro...  28.3 us
    pallas_call x2, Pallas kernels, features(): pl.pallas_call(functools.partial(feature_kernel, pitch=pitch), grid_spec=...  21 us
    pallas_call x1, Pallas kernels, pair_convolutions(): pl.pallas_call(functools.partial(conv_kernel, length=length, swap=swap, r...  10.9 us
    ppermute x5, starting transfers between devices, exchange(): return lax.ppermute(block, axis, [(i, i ^ bit) for i in range(count)])  8.39 us
    ppermute x1, waiting for transfers between devices, per_device(): below = lax.ppermute(ends[0], 'row', [(i + 1, i) for i in steps])  8.05 us
    ppermute x5, waiting for transfers between devices, exchange(): return lax.ppermute(block, axis, [(i, i ^ bit) for i in range(count)])  7 us
    ppermute x1, starting transfers between devices, per_device(): above = lax.ppermute(ends[1], 'row', [(i, i + 1) for i in steps])  3.62 us
  transfers between devices with their start and end apart: 7, of which 6 were waited for; matrix products, arithmetic and copies ran while one was open for 0% of the time, Pallas kernels for 28%

profile of v4, /device:TPU:0, one launch (start us, length us, event | category | flops | bytes accessed | tf_op | source)
XLA Modules:
  0.0 91.6 jit_solution(638583478171290917)
XLA Ops:
  0.0 0.8 convert_bitcast_fusion
  0.8 3.1 %collective-permute-start = (bf16[1,2,32,256]{3,2,1,0:T(8,128)(2,1)S(1)}, bf16[1,2,32,256]{3,2,1,0:T(8,128)(2,1)S(1)}, u32[]{:S(2)}, u32[]{:S(2)}) collective-permute-start(bf16[1,2,32,256]{3,2,1,0:T(8,128)(2,1)S(1)} %pad_maximum_fusion.3), channel_id=1, source_target_pairs={{0,4},{2,6},{4,0},{6,2},{8,12},{10,14},{12,8},{14,10},{1,5},{3,7},... | collective-permute-start | bytes 98312 | tf_op jit(solution)/shard_map/ppermute | solution.py:37
  3.9 1.9 %collective-permute-done = bf16[1,2,32,256]{3,2,1,0:T(8,128)(2,1)S(1)} collective-permute-done((bf16[1,2,32,256]{3,2,1,0:T(8,128)(2,1)S(1)}, bf16[1,2,32,256]{3,2,1,0:T(8,128)(2,1)S(1)}, u32[]{:S(2)}, u32[]{:S(2)}) %collective-permute-start) | collective-permute-done | bytes 32800 | tf_op jit(solution)/shard_map/ppermute | solution.py:37
  5.8 2.0 %collective-permute-start.1 = (bf16[2,2,32,256]{3,2,1,0:T(8,128)(2,1)S(1)}, bf16[2,2,32,256]{3,2,1,0:T(8,128)(2,1)S(1)}, u32[]{:S(2)}, u32[]{:S(2)}) collective-permute-start(bf16[2,2,32,256]{3,2,1,0:T(8,128)(2,1)S(1)} %pad_maximum_fusion.2), channel_id=1, source_target_pairs={{0,2},{2,0},{4,6},{6,4},{8,10},{10,8},{12,14},{14,12},{1,3},{3,1},... | collective-permute-start | bytes 196616 | tf_op jit(solution)/shard_map/ppermute | solution.py:37
  7.8 2.3 %collective-permute-done.1 = bf16[2,2,32,256]{3,2,1,0:T(8,128)(2,1)S(1)} collective-permute-done((bf16[2,2,32,256]{3,2,1,0:T(8,128)(2,1)S(1)}, bf16[2,2,32,256]{3,2,1,0:T(8,128)(2,1)S(1)}, u32[]{:S(2)}, u32[]{:S(2)}) %collective-permute-start.1) | collective-permute-done | bytes 65568 | tf_op jit(solution)/shard_map/ppermute | solution.py:37
  10.2 0.1 collective-permute-start.2
  10.3 1.3 %shard_map.73 = (bf16[128,192]{1,0:T(8,128)(2,1)S(1)}, bf16[64,192]{1,0:T(8,128)(2,1)S(1)}) custom-call(f32[21,64]{1,0:T(8,128)} %embedding_ref.1, f32[2,3,64,64]{3,2,1,0:T(8,128)} %filters_ref.1), custom_call_target="tpu_custom_call" | custom-call | flops 1000000 | bytes 262144 | tf_op jit(solution)/shard_map/pallas_call | solution.py:78
  11.5 0.1 collective-permute-done.2
  11.6 3.1 %collective-permute-start.3 = (bf16[8,2,32,256]{3,2,1,0:T(8,128)(2,1)S(1)}, bf16[8,2,32,256]{3,2,1,0:T(8,128)(2,1)S(1)}, u32[]{:S(2)}, u32[]{:S(2)}) collective-permute-start(bf16[8,2,32,256]{3,2,1,0:T(8,128)(2,1)S(1)} %pad_maximum_fusion.here_ref.there_ref), channel_id=1, source_target_pairs={{0,8},{2,10},{4,12},{6,14},{8,0},{10,2},{12,4},{14,6},{1,9},{3,11}... | collective-permute-start | bytes 786440 | tf_op jit(solution)/shard_map/ppermute | solution.py:37
  14.7 0.7 copy-done.1
  15.4 10.4 %shard_map.74 = (bf16[32,64,256]{2,1,0:T(8,128)(2,1)S(1)}, bf16[64,128,256]{2,1,0:T(8,128)(2,1)S(1)}, bf16[32,256]{1,0:T(8,128)(2,1)S(1)}, bf16[128,256]{1,0:T(8,128)(2,1)S(1)}) custom-call(s32[4]{0:T(128)S(1)} %copy-done.1, bf16[8,2,32,256]{3,2,1,0:T(8,128)(2,1)S(1)} %pad_maximum_fusion.here_ref.there_ref, ...), custom_call_target="tpu_custom_call" | custom-call | flops 6710886400 | bytes 5242880 | tf_op jit(solution)/shard_map/pallas_call | solution.py:232
  25.8 0.0 copy-start.3
  25.8 1.5 %collective-permute-done.3.here_ref.there_ref = bf16[8,2,32,256]{3,2,1,0:T(8,128)(2,1)S(1)} collective-permute-done((bf16[8,2,32,256]{3,2,1,0:T(8,128)(2,1)S(1)}, bf16[8,2,32,256]{3,2,1,0:T(8,128)(2,1)S(1)}, u32[]{:S(2)}, u32[]{:S(2)}) %collective-permute-start.3) | collective-permute-done | bytes 262176 | tf_op jit(solution)/shard_map/ppermute | solution.py:37
  27.2 10.6 %shard_map.75 = (bf16[32,64,256]{2,1,0:T(8,128)(2,1)S(1)}, bf16[64,128,256]{2,1,0:T(8,128)(2,1)S(1)}, bf16[32,256]{1,0:T(8,128)(2,1)S(1)}, bf16[128,256]{1,0:T(8,128)(2,1)S(1)}) custom-call(s32[4]{0:T(128)S(1)} %copy-done.1, bf16[8,2,32,256]{3,2,1,0:T(8,128)(2,1)S(1)} %collective-permute-done.3.here_ref.there_ref, ...), custom_call_target="tpu_custom_call" | custom-call | flops 6710886400 | bytes 5242880 | tf_op jit(solution)/shard_map/pallas_call | solution.py:232
  37.9 14.1 %shard_map.76 = (bf16[8,128,128]{2,1,0:T(8,128)(2,1)S(1)}, bf16[8,128,128]{2,1,0:T(8,128)(2,1)S(1)}, bf16[16,8,128]{2,1,0:T(8,128)(2,1)S(1)}) custom-call(bf16[32,64,256]{2,1,0:T(8,128)(2,1)S(1)} %get-tuple-element.23.refs_0_.refs_2_, bf16[32,64,256]{2,1,0:T(8,128)(2,1)S(1)} %get-tuple-element.24.refs_1_.refs_3_, ...), custom_call_target="tpu_custom_call" | custom-call | flops 10737418240 | bytes 9437184 | tf_op jit(solution)/shard_map/pallas_call | solution.py:342
  52.0 0.0 copy-start
  52.0 0.0 copy-start.2
  52.0 3.6 %collective-permute-start.4 = (bf16[8,128,128]{2,1,0:T(8,128)(2,1)S(1)}, bf16[8,128,128]{2,1,0:T(8,128)(2,1)S(1)}, u32[]{:S(2)}, u32[]{:S(2)}) collective-permute-start(bf16[8,128,128]{2,1,0:T(8,128)(2,1)S(1)} %get-tuple-element.31.refs_4_), channel_id=1, source_target_pairs={{0,2},{2,4},{4,6},{6,8},{8,10},{10,12},{12,14},{1,3},{3,5},{5,7},{... | collective-permute-start | bytes 786440 | tf_op jit(solution)/shard_map/ppermute | solution.py:533
  55.6 14.1 %shard_map.77 = (bf16[8,128,128]{2,1,0:T(8,128)(2,1)S(1)}, bf16[8,128,128]{2,1,0:T(8,128)(2,1)S(1)}, bf16[16,8,128]{2,1,0:T(8,128)(2,1)S(1)}) custom-call(bf16[32,64,256]{2,1,0:T(8,128)(2,1)S(1)} %get-tuple-element.23.refs_0_.refs_2_, bf16[32,64,256]{2,1,0:T(8,128)(2,1)S(1)} %get-tuple-element.24.refs_1_.refs_3_, ...), custom_call_target="tpu_custom_call" | custom-call | flops 10737418240 | bytes 9437184 | tf_op jit(solution)/shard_map/pallas_call | solution.py:342
  69.8 1.3 %collective-permute-start.5 = (bf16[8,128,128]{2,1,0:T(8,128)(2,1)S(1)}, bf16[8,128,128]{2,1,0:T(8,128)(2,1)S(1)}, u32[]{:S(2)}, u32[]{:S(2)}) collective-permute-start(bf16[8,128,128]{2,1,0:T(8,128)(2,1)S(1)} %get-tuple-element.32.refs_1_), channel_id=1, source_target_pairs={{2,0},{4,2},{6,4},{8,6},{10,8},{12,10},{14,12},{3,1},{5,3},{7,5},{... | collective-permute-start | bytes 786440 | tf_op jit(solution)/shard_map/ppermute | solution.py:534
  71.1 8.0 %collective-permute-done.5.refs_5_ = bf16[8,128,128]{2,1,0:T(8,128)(2,1)S(1)} collective-permute-done((bf16[8,128,128]{2,1,0:T(8,128)(2,1)S(1)}, bf16[8,128,128]{2,1,0:T(8,128)(2,1)S(1)}, u32[]{:S(2)}, u32[]{:S(2)}) %collective-permute-start.5) | collective-permute-done | bytes 262176 | tf_op jit(solution)/shard_map/ppermute | solution.py:534
  79.2 0.1 collective-permute-start.6
  79.3 1.3 %collective-permute-done.6.refs_6_ = bf16[48,8,128]{2,1,0:T(8,128)(2,1)S(1)} collective-permute-done((bf16[48,8,128]{2,1,0:T(8,128)(2,1)S(1)}, bf16[48,8,128]{2,1,0:T(8,128)(2,1)S(1)}, u32[]{:S(2)}, u32[]{:S(2)}) %collective-permute-start.6) | collective-permute-done | bytes 98336 | tf_op jit(solution)/shard_map/ppermute | solution.py:37
  80.6 10.9 %shard_map.78 = bf16[32,128,128]{2,1,0:T(8,128)(2,1)} custom-call(s32[4]{0:T(128)S(1)} %copy-done.2, bf16[8,128,128]{2,1,0:T(8,128)(2,1)S(1)} %collective-permute-done.4.refs_0_, bf16[8,128,128]{2,1,0:T(8,128)(2,1)S(1)} %get-tuple-element.32.refs_1_, bf16[8,128,128]{2,1,0:T(8,128)(2,1)S(1)} %get-tuple-element.33.refs_2_, ...), custom_call_target="tpu_custom_call" | custom-call | tf_op jit(solution)/shard_map/pallas_call | solution.py:482
  (14 shorter events, 0.1 us)
Async XLA Ops:
  0.8 5.0 %collective-permute-start = (bf16[1,2,32,256]{3,2,1,0:T(8,128)(2,1)S(1)}, bf16[1,2,32,256]{3,2,1,0:T(8,128)(2,1)S(1)}, u32[]{:S(2)}, u32[]{:S(2)}) collective-permute-start(bf16[1,2,32,256]{3,2,1,0:T(8,128)(2,1)S(1)} %pad_maximum_fusion.3), channel_id=1, source_target_pairs={{0,4},{2,6},{4,0},{6,2},{8,12},{10,14},{12,8},{14,10},{1,5},{3,7},... | collective-permute-start | bytes 98312 | tf_op jit(solution)/shard_map/ppermute | solution.py:37
  5.8 4.3 %collective-permute-start.1 = (bf16[2,2,32,256]{3,2,1,0:T(8,128)(2,1)S(1)}, bf16[2,2,32,256]{3,2,1,0:T(8,128)(2,1)S(1)}, u32[]{:S(2)}, u32[]{:S(2)}) collective-permute-start(bf16[2,2,32,256]{3,2,1,0:T(8,128)(2,1)S(1)} %pad_maximum_fusion.2), channel_id=1, source_target_pairs={{0,2},{2,0},{4,6},{6,4},{8,10},{10,8},{12,14},{14,12},{1,3},{3,1},... | collective-permute-start | bytes 196616 | tf_op jit(solution)/shard_map/ppermute | solution.py:37
  10.2 1.4 %collective-permute-start.2 = (bf16[4,2,32,256]{3,2,1,0:T(8,128)(2,1)S(1)}, bf16[4,2,32,256]{3,2,1,0:T(8,128)(2,1)S(1)}, u32[]{:S(2)}, u32[]{:S(2)}) collective-permute-start(bf16[4,2,32,256]{3,2,1,0:T(8,128)(2,1)S(1)} %pad_maximum_fusion.1), channel_id=1, source_target_pairs={{0,1},{1,0},{2,3},{3,2},{4,5},{5,4},{6,7},{7,6},{8,9},{9,8},{10,11... | collective-permute-start | bytes 393224 | tf_op jit(solution)/shard_map/ppermute | solution.py:37
  11.6 15.6 %collective-permute-start.3 = (bf16[8,2,32,256]{3,2,1,0:T(8,128)(2,1)S(1)}, bf16[8,2,32,256]{3,2,1,0:T(8,128)(2,1)S(1)}, u32[]{:S(2)}, u32[]{:S(2)}) collective-permute-start(bf16[8,2,32,256]{3,2,1,0:T(8,128)(2,1)S(1)} %pad_maximum_fusion.here_ref.there_ref), channel_id=1, source_target_pairs={{0,8},{2,10},{4,12},{6,14},{8,0},{10,2},{12,4},{14,6},{1,9},{3,11}... | collective-permute-start | bytes 786440 | tf_op jit(solution)/shard_map/ppermute | solution.py:37
  14.7 0.7 copy-start.1
  25.8 12.1 %copy-start.3 = (bf16[4096,128]{1,0:T(8,128)(2,1)S(1)}, bf16[4096,128]{1,0:T(8,128)(2,1)}, u32[]{:S(2)}) copy-start(bf16[4096,128]{1,0:T(8,128)(2,1)} %param.12) | copy-start | bytes 3145732
  52.0 28.6 %copy-start = (bf16[2,3,3,128,128]{4,3,2,1,0:T(8,128)(2,1)S(1)}, bf16[2,3,3,128,128]{4,3,2,1,0:T(8,128)(2,1)}, u32[]{:S(2)}) copy-start(bf16[2,3,3,128,128]{4,3,2,1,0:T(8,128)(2,1)} %param.13) | copy-start | bytes 1769476
  52.0 28.6 %copy-start.2 = (s32[4]{0:T(128)S(1)}, s32[4]{0:T(128)}, u32[]{:S(2)}) copy-start(s32[4]{0:T(128)} %dilations.5) | copy-start | bytes 52
  52.0 19.1 %collective-permute-start.4 = (bf16[8,128,128]{2,1,0:T(8,128)(2,1)S(1)}, bf16[8,128,128]{2,1,0:T(8,128)(2,1)S(1)}, u32[]{:S(2)}, u32[]{:S(2)}) collective-permute-start(bf16[8,128,128]{2,1,0:T(8,128)(2,1)S(1)} %get-tuple-element.31.refs_4_), channel_id=1, source_target_pairs={{0,2},{2,4},{4,6},{6,8},{8,10},{10,12},{12,14},{1,3},{3,5},{5,7},{... | collective-permute-start | bytes 786440 | tf_op jit(solution)/shard_map/ppermute | solution.py:533
  69.8 9.4 %collective-permute-start.5 = (bf16[8,128,128]{2,1,0:T(8,128)(2,1)S(1)}, bf16[8,128,128]{2,1,0:T(8,128)(2,1)S(1)}, u32[]{:S(2)}, u32[]{:S(2)}) collective-permute-start(bf16[8,128,128]{2,1,0:T(8,128)(2,1)S(1)} %get-tuple-element.32.refs_1_), channel_id=1, source_target_pairs={{2,0},{4,2},{6,4},{8,6},{10,8},{12,10},{14,12},{3,1},{5,3},{7,5},{... | collective-permute-start | bytes 786440 | tf_op jit(solution)/shard_map/ppermute | solution.py:534
  79.2 1.4 %collective-permute-start.6 = (bf16[48,8,128]{2,1,0:T(8,128)(2,1)S(1)}, bf16[48,8,128]{2,1,0:T(8,128)(2,1)S(1)}, u32[]{:S(2)}, u32[]{:S(2)}) collective-permute-start(bf16[48,8,128]{2,1,0:T(8,128)(2,1)S(1)} %fusion), channel_id=1, source_target_pairs={{0,1},{1,0},{2,3},{3,2},{4,5},{5,4},{6,7},{7,6},{8,9},{9,8},{10,11... | collective-permute-start | bytes 294920 | tf_op jit(solution)/shard_map/ppermute | solution.py:37

commit v5 on v3

--- a/solution.py
+++ b/solution.py
@@ -84,7 +84,7 @@
         scratch_shapes=[
             pltpu.VMEM((kinds, channels), jnp.float32),
         ],
-        compiler_params=pltpu.CompilerParams(vmem_limit_bytes=62 << 20),
+        compiler_params=pltpu.CompilerParams(vmem_limit_bytes=16 << 20),
         cost_estimate=pl.CostEstimate(flops=10**6, bytes_accessed=1 << 18, transcendentals=0),
     )(in_hbm(embedding), in_hbm(filters))
 
@@ -111,7 +111,8 @@
     token_s[HALO + length : 2 * HALO + length, :] = edge
     row_mark_ref[...] = mark_s[pl.ds(pl.multiple_of(row_first, 8), rows), :].astype(row_mark_ref.dtype)
     col_mark_ref[...] = mark_s[pl.ds(pl.multiple_of(col_first, 8), cols), :].astype(col_mark_ref.dtype)
-    letters = lax.broadcasted_iota(jnp.int32, (kinds, width), 0).astype(jnp.float32)
+    letters = lax.broadcasted_iota(jnp.int32, (kinds, width), 0).astype(jnp.float32).astype(onehot_s.dtype)
+    present, absent = jnp.ones((), onehot_s.dtype), jnp.zeros((), onehot_s.dtype)
     table = table_ref[...]
     second = second_ref[...]
 
@@ -134,7 +135,8 @@
         def hot(step, carry):
             block = token_s[pl.ds(pl.multiple_of(first + step * 8, 8), 8), :]
             for k in range(8):
-                onehot_s[step * 8 + k] = jnp.where(block[k : k + 1, :] == letters, 1.0, 0.0).astype(onehot_s.dtype)
+                letter = jnp.broadcast_to(block[k : k + 1, :], (kinds, width)).astype(onehot_s.dtype)
+                onehot_s[step * 8 + k] = jnp.where(letter == letters, present, absent)
             return carry
 
         lax.fori_loop(0, (count + 2 * HALO) // 8, hot, 0)
@@ -263,7 +265,7 @@
             bytes_accessed=2 * channels * width * (rows + cols),
             transcendentals=2 * channels * width * (rows + cols),
         ),
-    )(in_hbm(dilations), here, there, in_hbm(table), in_hbm(second))
+    )(dilations, here, there, table, second)
 
 
 def outer_kernel(*refs, picks, halves, swap):
@@ -496,7 +498,7 @@
         ),
         out_shape=jax.ShapeDtypeStruct((rows, cols, channels), jnp.bfloat16),
         compiler_params=pltpu.CompilerParams(vmem_limit_bytes=40 << 20),
-    )(in_hbm(dilations), *operands)
+    )(dilations, *operands)
 
 
 def col_margins(tall):

time: 93.8 us -> 91.8 us (0.979)
  Pallas kernels: 64.4 us -> 61.1 us
    pallas_call x2, Pallas kernels: 23.3 us -> 20.7 us  [features(): pl.pallas_call(functools.partial(feature_kernel, pitch=pitch), grid_spec=...]
  transfers between devices with their start and end apart: 8 -> 8, of which waited for: 5 -> 5; matrix products, arithmetic and copies ran while one was open for 0% -> 0% of each run, Pallas kernels for 30% -> 28%
where the time goes in v5:
time: 91.8 us; the launch traced here: 91.4 us
  Pallas kernels  61.1 us (67%)
  waiting for transfers between devices  15.1 us (16%)
  starting transfers between devices  13.4 us (15%)
    pallas_call x2, Pallas kernels, outer_products(): pl.pallas_call(functools.partial(outer_kernel, picks=picks, halves=len(ro...  28.3 us
    pallas_call x2, Pallas kernels, features(): pl.pallas_call(functools.partial(feature_kernel, pitch=pitch), grid_spec=...  20.7 us
    pallas_call x1, Pallas kernels, pair_convolutions(): pl.pallas_call(functools.partial(conv_kernel, length=length, swap=swap, r...  10.9 us
    ppermute x6, starting transfers between devices, exchange(): return lax.ppermute(block, axis, [(i, i ^ bit) for i in range(count)])  8.47 us
    ppermute x1, waiting for transfers between devices, per_device(): below = lax.ppermute(ends[0], 'row', [(i + 1, i) for i in steps])  8.07 us
    ppermute x6, waiting for transfers between devices, exchange(): return lax.ppermute(block, axis, [(i, i ^ bit) for i in range(count)])  7.05 us
    ppermute x1, starting transfers between devices, per_device(): above = lax.ppermute(ends[1], 'row', [(i, i + 1) for i in steps])  3.65 us
  transfers between devices with their start and end apart: 8, of which 5 were waited for; matrix products, arithmetic and copies ran while one was open for 0% of the time, Pallas kernels for 28%

profile of v5, /device:TPU:0, one launch (start us, length us, event | category | flops | bytes accessed | tf_op | source)
XLA Modules:
  0.0 91.4 jit_solution(6073715681775347541)
XLA Ops:
  0.0 0.8 convert_bitcast_fusion
  0.8 3.1 %collective-permute-start = (bf16[1,2,32,256]{3,2,1,0:T(8,128)(2,1)S(1)}, bf16[1,2,32,256]{3,2,1,0:T(8,128)(2,1)S(1)}, u32[]{:S(2)}, u32[]{:S(2)}) collective-permute-start(bf16[1,2,32,256]{3,2,1,0:T(8,128)(2,1)S(1)} %pad_maximum_fusion.2), channel_id=1, source_target_pairs={{0,4},{2,6},{4,0},{6,2},{8,12},{10,14},{12,8},{14,10},{1,5},{3,7},... | collective-permute-start | bytes 98312 | tf_op jit(solution)/shard_map/ppermute | solution.py:37
  3.9 1.9 %collective-permute-done = bf16[1,2,32,256]{3,2,1,0:T(8,128)(2,1)S(1)} collective-permute-done((bf16[1,2,32,256]{3,2,1,0:T(8,128)(2,1)S(1)}, bf16[1,2,32,256]{3,2,1,0:T(8,128)(2,1)S(1)}, u32[]{:S(2)}, u32[]{:S(2)}) %collective-permute-start) | collective-permute-done | bytes 32800 | tf_op jit(solution)/shard_map/ppermute | solution.py:37
  5.8 2.0 %collective-permute-start.1 = (bf16[2,2,32,256]{3,2,1,0:T(8,128)(2,1)S(1)}, bf16[2,2,32,256]{3,2,1,0:T(8,128)(2,1)S(1)}, u32[]{:S(2)}, u32[]{:S(2)}) collective-permute-start(bf16[2,2,32,256]{3,2,1,0:T(8,128)(2,1)S(1)} %pad_maximum_fusion.1), channel_id=1, source_target_pairs={{0,2},{2,0},{4,6},{6,4},{8,10},{10,8},{12,14},{14,12},{1,3},{3,1},... | collective-permute-start | bytes 196616 | tf_op jit(solution)/shard_map/ppermute | solution.py:37
  7.8 2.3 %collective-permute-done.1 = bf16[2,2,32,256]{3,2,1,0:T(8,128)(2,1)S(1)} collective-permute-done((bf16[2,2,32,256]{3,2,1,0:T(8,128)(2,1)S(1)}, bf16[2,2,32,256]{3,2,1,0:T(8,128)(2,1)S(1)}, u32[]{:S(2)}, u32[]{:S(2)}) %collective-permute-start.1) | collective-permute-done | bytes 65568 | tf_op jit(solution)/shard_map/ppermute | solution.py:37
  10.2 0.1 collective-permute-start.2
  10.3 1.3 %shard_map.73 = (bf16[128,192]{1,0:T(8,128)(2,1)S(1)}, bf16[64,192]{1,0:T(8,128)(2,1)S(1)}) custom-call(f32[21,64]{1,0:T(8,128)} %embedding_ref.1, f32[2,3,64,64]{3,2,1,0:T(8,128)} %filters_ref.1), custom_call_target="tpu_custom_call" | custom-call | flops 1000000 | bytes 262144 | tf_op jit(solution)/shard_map/pallas_call | solution.py:78
  11.5 3.1 %collective-permute-start.3 = (bf16[4,2,32,256]{3,2,1,0:T(8,128)(2,1)S(1)}, bf16[4,2,32,256]{3,2,1,0:T(8,128)(2,1)S(1)}, u32[]{:S(2)}, u32[]{:S(2)}) collective-permute-start(bf16[4,2,32,256]{3,2,1,0:T(8,128)(2,1)S(1)} %pad_maximum_fusion.here_ref), channel_id=1, source_target_pairs={{0,8},{2,10},{4,12},{6,14},{8,0},{10,2},{12,4},{14,6},{1,9},{3,11}... | collective-permute-start | bytes 393224 | tf_op jit(solution)/shard_map/ppermute | solution.py:37
  14.6 0.1 collective-permute-start.4
  14.7 0.7 copy-done.1
  15.4 10.2 %shard_map.74 = (bf16[32,64,256]{2,1,0:T(8,128)(2,1)S(1)}, bf16[64,128,256]{2,1,0:T(8,128)(2,1)S(1)}, bf16[32,256]{1,0:T(8,128)(2,1)S(1)}, bf16[128,256]{1,0:T(8,128)(2,1)S(1)}) custom-call(s32[4]{0:T(128)S(1)} %copy-done.1, bf16[4,2,32,256]{3,2,1,0:T(8,128)(2,1)S(1)} %pad_maximum_fusion.here_ref, ...), custom_call_target="tpu_custom_call" | custom-call | flops 6710886400 | bytes 5242880 | tf_op jit(solution)/shard_map/pallas_call | solution.py:233
  25.6 0.0 copy-start.3
  25.6 1.6 %collective-permute-done.4.there_ref = bf16[4,2,32,256]{3,2,1,0:T(8,128)(2,1)S(1)} collective-permute-done((bf16[4,2,32,256]{3,2,1,0:T(8,128)(2,1)S(1)}, bf16[4,2,32,256]{3,2,1,0:T(8,128)(2,1)S(1)}, u32[]{:S(2)}, u32[]{:S(2)}) %collective-permute-start.4) | collective-permute-done | bytes 131104 | tf_op jit(solution)/shard_map/ppermute | solution.py:37
  27.2 10.4 %shard_map.75 = (bf16[32,64,256]{2,1,0:T(8,128)(2,1)S(1)}, bf16[64,128,256]{2,1,0:T(8,128)(2,1)S(1)}, bf16[32,256]{1,0:T(8,128)(2,1)S(1)}, bf16[128,256]{1,0:T(8,128)(2,1)S(1)}) custom-call(s32[4]{0:T(128)S(1)} %copy-done.1, bf16[4,2,32,256]{3,2,1,0:T(8,128)(2,1)S(1)} %collective-permute-done.3.here_ref, ...), custom_call_target="tpu_custom_call" | custom-call | flops 6710886400 | bytes 5242880 | tf_op jit(solution)/shard_map/pallas_call | solution.py:233
  37.6 14.1 %shard_map.76 = (bf16[8,128,128]{2,1,0:T(8,128)(2,1)S(1)}, bf16[8,128,128]{2,1,0:T(8,128)(2,1)S(1)}, bf16[16,8,128]{2,1,0:T(8,128)(2,1)S(1)}) custom-call(bf16[32,64,256]{2,1,0:T(8,128)(2,1)S(1)} %get-tuple-element.23.refs_0_.refs_2_, bf16[32,64,256]{2,1,0:T(8,128)(2,1)S(1)} %get-tuple-element.24.refs_1_.refs_3_, ...), custom_call_target="tpu_custom_call" | custom-call | flops 10737418240 | bytes 9437184 | tf_op jit(solution)/shard_map/pallas_call | solution.py:342
  51.8 0.0 copy-start
  51.8 0.0 copy-start.2
  51.8 3.6 %collective-permute-start.5 = (bf16[8,128,128]{2,1,0:T(8,128)(2,1)S(1)}, bf16[8,128,128]{2,1,0:T(8,128)(2,1)S(1)}, u32[]{:S(2)}, u32[]{:S(2)}) collective-permute-start(bf16[8,128,128]{2,1,0:T(8,128)(2,1)S(1)} %get-tuple-element.31.refs_4_), channel_id=1, source_target_pairs={{0,2},{2,4},{4,6},{6,8},{8,10},{10,12},{12,14},{1,3},{3,5},{5,7},{... | collective-permute-start | bytes 786440 | tf_op jit(solution)/shard_map/ppermute | solution.py:533
  55.5 14.1 %shard_map.77 = (bf16[8,128,128]{2,1,0:T(8,128)(2,1)S(1)}, bf16[8,128,128]{2,1,0:T(8,128)(2,1)S(1)}, bf16[16,8,128]{2,1,0:T(8,128)(2,1)S(1)}) custom-call(bf16[32,64,256]{2,1,0:T(8,128)(2,1)S(1)} %get-tuple-element.23.refs_0_.refs_2_, bf16[32,64,256]{2,1,0:T(8,128)(2,1)S(1)} %get-tuple-element.24.refs_1_.refs_3_, ...), custom_call_target="tpu_custom_call" | custom-call | flops 10737418240 | bytes 9437184 | tf_op jit(solution)/shard_map/pallas_call | solution.py:342
  69.6 1.3 %collective-permute-start.6 = (bf16[8,128,128]{2,1,0:T(8,128)(2,1)S(1)}, bf16[8,128,128]{2,1,0:T(8,128)(2,1)S(1)}, u32[]{:S(2)}, u32[]{:S(2)}) collective-permute-start(bf16[8,128,128]{2,1,0:T(8,128)(2,1)S(1)} %get-tuple-element.32.refs_1_), channel_id=1, source_target_pairs={{2,0},{4,2},{6,4},{8,6},{10,8},{12,10},{14,12},{3,1},{5,3},{7,5},{... | collective-permute-start | bytes 786440 | tf_op jit(solution)/shard_map/ppermute | solution.py:534
  71.0 8.1 %collective-permute-done.6.refs_5_ = bf16[8,128,128]{2,1,0:T(8,128)(2,1)S(1)} collective-permute-done((bf16[8,128,128]{2,1,0:T(8,128)(2,1)S(1)}, bf16[8,128,128]{2,1,0:T(8,128)(2,1)S(1)}, u32[]{:S(2)}, u32[]{:S(2)}) %collective-permute-start.6) | collective-permute-done | bytes 262176 | tf_op jit(solution)/shard_map/ppermute | solution.py:534
  79.0 0.1 collective-permute-start.7
  79.1 1.3 %collective-permute-done.7.refs_6_ = bf16[48,8,128]{2,1,0:T(8,128)(2,1)S(1)} collective-permute-done((bf16[48,8,128]{2,1,0:T(8,128)(2,1)S(1)}, bf16[48,8,128]{2,1,0:T(8,128)(2,1)S(1)}, u32[]{:S(2)}, u32[]{:S(2)}) %collective-permute-start.7) | collective-permute-done | bytes 98336 | tf_op jit(solution)/shard_map/ppermute | solution.py:37
  80.4 10.9 %shard_map.78 = bf16[32,128,128]{2,1,0:T(8,128)(2,1)} custom-call(s32[4]{0:T(128)S(1)} %copy-done.2, bf16[8,128,128]{2,1,0:T(8,128)(2,1)S(1)} %collective-permute-done.5.refs_0_, bf16[8,128,128]{2,1,0:T(8,128)(2,1)S(1)} %get-tuple-element.32.refs_1_, bf16[8,128,128]{2,1,0:T(8,128)(2,1)S(1)} %get-tuple-element.33.refs_2_, ...), custom_call_target="tpu_custom_call" | custom-call | tf_op jit(solution)/shard_map/pallas_call | solution.py:482
  (15 shorter events, 0.1 us)
Async XLA Ops:
  0.8 5.0 %collective-permute-start = (bf16[1,2,32,256]{3,2,1,0:T(8,128)(2,1)S(1)}, bf16[1,2,32,256]{3,2,1,0:T(8,128)(2,1)S(1)}, u32[]{:S(2)}, u32[]{:S(2)}) collective-permute-start(bf16[1,2,32,256]{3,2,1,0:T(8,128)(2,1)S(1)} %pad_maximum_fusion.2), channel_id=1, source_target_pairs={{0,4},{2,6},{4,0},{6,2},{8,12},{10,14},{12,8},{14,10},{1,5},{3,7},... | collective-permute-start | bytes 98312 | tf_op jit(solution)/shard_map/ppermute | solution.py:37
  5.8 4.3 %collective-permute-start.1 = (bf16[2,2,32,256]{3,2,1,0:T(8,128)(2,1)S(1)}, bf16[2,2,32,256]{3,2,1,0:T(8,128)(2,1)S(1)}, u32[]{:S(2)}, u32[]{:S(2)}) collective-permute-start(bf16[2,2,32,256]{3,2,1,0:T(8,128)(2,1)S(1)} %pad_maximum_fusion.1), channel_id=1, source_target_pairs={{0,2},{2,0},{4,6},{6,4},{8,10},{10,8},{12,14},{14,12},{1,3},{3,1},... | collective-permute-start | bytes 196616 | tf_op jit(solution)/shard_map/ppermute | solution.py:37
  10.2 4.5 %collective-permute-start.2 = (bf16[4,2,32,256]{3,2,1,0:T(8,128)(2,1)S(1)}, bf16[4,2,32,256]{3,2,1,0:T(8,128)(2,1)S(1)}, u32[]{:S(2)}, u32[]{:S(2)}) collective-permute-start(bf16[4,2,32,256]{3,2,1,0:T(8,128)(2,1)S(1)} %pad_maximum_fusion.here_ref), channel_id=1, source_target_pairs={{0,1},{1,0},{2,3},{3,2},{4,5},{5,4},{6,7},{7,6},{8,9},{9,8},{10,11... | collective-permute-start | bytes 393224 | tf_op jit(solution)/shard_map/ppermute | solution.py:37
  11.5 14.1 %collective-permute-start.3 = (bf16[4,2,32,256]{3,2,1,0:T(8,128)(2,1)S(1)}, bf16[4,2,32,256]{3,2,1,0:T(8,128)(2,1)S(1)}, u32[]{:S(2)}, u32[]{:S(2)}) collective-permute-start(bf16[4,2,32,256]{3,2,1,0:T(8,128)(2,1)S(1)} %pad_maximum_fusion.here_ref), channel_id=1, source_target_pairs={{0,8},{2,10},{4,12},{6,14},{8,0},{10,2},{12,4},{14,6},{1,9},{3,11}... | collective-permute-start | bytes 393224 | tf_op jit(solution)/shard_map/ppermute | solution.py:37
  14.6 12.6 %collective-permute-start.4 = (bf16[4,2,32,256]{3,2,1,0:T(8,128)(2,1)S(1)}, bf16[4,2,32,256]{3,2,1,0:T(8,128)(2,1)S(1)}, u32[]{:S(2)}, u32[]{:S(2)}) collective-permute-start(bf16[4,2,32,256]{3,2,1,0:T(8,128)(2,1)S(1)} %collective-permute-done.2.there_ref), channel_id=1, source_target_pairs={{0,8},{2,10},{4,12},{6,14},{8,0},{10,2},{12,4},{14,6},{1,9},{3,11}... | collective-permute-start | bytes 393224 | tf_op jit(solution)/shard_map/ppermute | solution.py:37
  14.7 0.7 copy-start.1
  25.6 12.0 %copy-start.3 = (bf16[4096,128]{1,0:T(8,128)(2,1)S(1)}, bf16[4096,128]{1,0:T(8,128)(2,1)}, u32[]{:S(2)}) copy-start(bf16[4096,128]{1,0:T(8,128)(2,1)} %param.12) | copy-start | bytes 3145732
  51.8 28.6 %copy-start = (bf16[2,3,3,128,128]{4,3,2,1,0:T(8,128)(2,1)S(1)}, bf16[2,3,3,128,128]{4,3,2,1,0:T(8,128)(2,1)}, u32[]{:S(2)}) copy-start(bf16[2,3,3,128,128]{4,3,2,1,0:T(8,128)(2,1)} %param.13) | copy-start | bytes 1769476
  51.8 28.6 %copy-start.2 = (s32[4]{0:T(128)S(1)}, s32[4]{0:T(128)}, u32[]{:S(2)}) copy-start(s32[4]{0:T(128)} %dilations.5) | copy-start | bytes 52
  51.8 19.1 %collective-permute-start.5 = (bf16[8,128,128]{2,1,0:T(8,128)(2,1)S(1)}, bf16[8,128,128]{2,1,0:T(8,128)(2,1)S(1)}, u32[]{:S(2)}, u32[]{:S(2)}) collective-permute-start(bf16[8,128,128]{2,1,0:T(8,128)(2,1)S(1)} %get-tuple-element.31.refs_4_), channel_id=1, source_target_pairs={{0,2},{2,4},{4,6},{6,8},{8,10},{10,12},{12,14},{1,3},{3,5},{5,7},{... | collective-permute-start | bytes 786440 | tf_op jit(solution)/shard_map/ppermute | solution.py:533
  69.6 9.4 %collective-permute-start.6 = (bf16[8,128,128]{2,1,0:T(8,128)(2,1)S(1)}, bf16[8,128,128]{2,1,0:T(8,128)(2,1)S(1)}, u32[]{:S(2)}, u32[]{:S(2)}) collective-permute-start(bf16[8,128,128]{2,1,0:T(8,128)(2,1)S(1)} %get-tuple-element.32.refs_1_), channel_id=1, source_target_pairs={{2,0},{4,2},{6,4},{8,6},{10,8},{12,10},{14,12},{3,1},{5,3},{7,5},{... | collective-permute-start | bytes 786440 | tf_op jit(solution)/shard_map/ppermute | solution.py:534
  79.0 1.4 %collective-permute-start.7 = (bf16[48,8,128]{2,1,0:T(8,128)(2,1)S(1)}, bf16[48,8,128]{2,1,0:T(8,128)(2,1)S(1)}, u32[]{:S(2)}, u32[]{:S(2)}) collective-permute-start(bf16[48,8,128]{2,1,0:T(8,128)(2,1)S(1)} %fusion), channel_id=1, source_target_pairs={{0,1},{1,0},{2,3},{3,2},{4,5},{5,4},{6,7},{7,6},{8,9},{9,8},{10,11... | collective-permute-start | bytes 294920 | tf_op jit(solution)/shard_map/ppermute | solution.py:37

commit v6 on v5

--- a/solution.py
+++ b/solution.py
@@ -434,7 +434,7 @@
             hidden_s[pl.ds(pl.multiple_of(i * pitch, 8), pitch), :] = elu(mixing)
         return carry
 
-    lax.fori_loop(0, row_pairs(tall), one, 0, unroll=3)
+    lax.fori_loop(0, row_pairs(tall), one, 0, unroll=at_once(row_pairs(tall)))
     for i in range(tall):
         place = row_first - DMAX + i
         if i < DMAX or i >= tall - DMAX:
@@ -462,10 +462,14 @@
             out_s[i] = (own + mixing).astype(out_s.dtype)
         return carry
 
-    lax.fori_loop(0, row_pairs(rows), two, 0, unroll=3)
+    lax.fori_loop(0, row_pairs(rows), two, 0, unroll=at_once(row_pairs(rows)))
     copy = pltpu.make_async_copy(out_s.at[0:rows], out_ref, sem)
     copy.start()
     copy.wait()
+
+
+def at_once(count):
+    return max(k for k in range(1, 8) if count % k == 0)
 
 
 def row_pairs(count):

time: 91.8 us -> 90.5 us (0.986)
  Pallas kernels: 61.1 us -> 59.8 us
    pallas_call x1, Pallas kernels: 10.9 us -> 9.57 us  [pair_convolutions(): pl.pallas_call(functools.partial(conv_kernel, length=length, swap=swap, r...]
where the time goes in v6:
time: 90.5 us; the launch traced here: 90.1 us
  Pallas kernels  59.8 us (66%)
  waiting for transfers between devices  15.1 us (17%)
  starting transfers between devices  13.4 us (15%)
    pallas_call x2, Pallas kernels, outer_products(): pl.pallas_call(functools.partial(outer_kernel, picks=picks, halves=len(ro...  28.3 us
    pallas_call x2, Pallas kernels, features(): pl.pallas_call(functools.partial(feature_kernel, pitch=pitch), grid_spec=...  20.7 us
    pallas_call x1, Pallas kernels, pair_convolutions(): pl.pallas_call(functools.partial(conv_kernel, length=length, swap=swap, r...  9.57 us
    ppermute x6, starting transfers between devices, exchange(): return lax.ppermute(block, axis, [(i, i ^ bit) for i in range(count)])  8.47 us
    ppermute x1, waiting for transfers between devices, per_device(): below = lax.ppermute(ends[0], 'row', [(i + 1, i) for i in steps])  8.07 us
    ppermute x6, waiting for transfers between devices, exchange(): return lax.ppermute(block, axis, [(i, i ^ bit) for i in range(count)])  7.05 us
    ppermute x1, starting transfers between devices, per_device(): above = lax.ppermute(ends[1], 'row', [(i, i + 1) for i in steps])  3.65 us
  transfers between devices with their start and end apart: 8, of which 5 were waited for; matrix products, arithmetic and copies ran while one was open for 0% of the time, Pallas kernels for 28%

profile of v6, /device:TPU:0, one launch (start us, length us, event | category | flops | bytes accessed | tf_op | source)
XLA Modules:
  0.0 90.1 jit_solution(68771785375562495)
XLA Ops:
  0.0 0.8 convert_bitcast_fusion
  0.8 3.1 %collective-permute-start = (bf16[1,2,32,256]{3,2,1,0:T(8,128)(2,1)S(1)}, bf16[1,2,32,256]{3,2,1,0:T(8,128)(2,1)S(1)}, u32[]{:S(2)}, u32[]{:S(2)}) collective-permute-start(bf16[1,2,32,256]{3,2,1,0:T(8,128)(2,1)S(1)} %pad_maximum_fusion.2), channel_id=1, source_target_pairs={{0,4},{2,6},{4,0},{6,2},{8,12},{10,14},{12,8},{14,10},{1,5},{3,7},... | collective-permute-start | bytes 98312 | tf_op jit(solution)/shard_map/ppermute | solution.py:37
  3.9 1.9 %collective-permute-done = bf16[1,2,32,256]{3,2,1,0:T(8,128)(2,1)S(1)} collective-permute-done((bf16[1,2,32,256]{3,2,1,0:T(8,128)(2,1)S(1)}, bf16[1,2,32,256]{3,2,1,0:T(8,128)(2,1)S(1)}, u32[]{:S(2)}, u32[]{:S(2)}) %collective-permute-start) | collective-permute-done | bytes 32800 | tf_op jit(solution)/shard_map/ppermute | solution.py:37
  5.8 2.0 %collective-permute-start.1 = (bf16[2,2,32,256]{3,2,1,0:T(8,128)(2,1)S(1)}, bf16[2,2,32,256]{3,2,1,0:T(8,128)(2,1)S(1)}, u32[]{:S(2)}, u32[]{:S(2)}) collective-permute-start(bf16[2,2,32,256]{3,2,1,0:T(8,128)(2,1)S(1)} %pad_maximum_fusion.1), channel_id=1, source_target_pairs={{0,2},{2,0},{4,6},{6,4},{8,10},{10,8},{12,14},{14,12},{1,3},{3,1},... | collective-permute-start | bytes 196616 | tf_op jit(solution)/shard_map/ppermute | solution.py:37
  7.8 2.3 %collective-permute-done.1 = bf16[2,2,32,256]{3,2,1,0:T(8,128)(2,1)S(1)} collective-permute-done((bf16[2,2,32,256]{3,2,1,0:T(8,128)(2,1)S(1)}, bf16[2,2,32,256]{3,2,1,0:T(8,128)(2,1)S(1)}, u32[]{:S(2)}, u32[]{:S(2)}) %collective-permute-start.1) | collective-permute-done | bytes 65568 | tf_op jit(solution)/shard_map/ppermute | solution.py:37
  10.2 0.1 collective-permute-start.2
  10.3 1.3 %shard_map.73 = (bf16[128,192]{1,0:T(8,128)(2,1)S(1)}, bf16[64,192]{1,0:T(8,128)(2,1)S(1)}) custom-call(f32[21,64]{1,0:T(8,128)} %embedding_ref.1, f32[2,3,64,64]{3,2,1,0:T(8,128)} %filters_ref.1), custom_call_target="tpu_custom_call" | custom-call | flops 1000000 | bytes 262144 | tf_op jit(solution)/shard_map/pallas_call | solution.py:78
  11.5 3.1 %collective-permute-start.3 = (bf16[4,2,32,256]{3,2,1,0:T(8,128)(2,1)S(1)}, bf16[4,2,32,256]{3,2,1,0:T(8,128)(2,1)S(1)}, u32[]{:S(2)}, u32[]{:S(2)}) collective-permute-start(bf16[4,2,32,256]{3,2,1,0:T(8,128)(2,1)S(1)} %pad_maximum_fusion.here_ref), channel_id=1, source_target_pairs={{0,8},{2,10},{4,12},{6,14},{8,0},{10,2},{12,4},{14,6},{1,9},{3,11}... | collective-permute-start | bytes 393224 | tf_op jit(solution)/shard_map/ppermute | solution.py:37
  14.6 0.1 collective-permute-start.4
  14.7 0.7 copy-done.1
  15.4 10.2 %shard_map.74 = (bf16[32,64,256]{2,1,0:T(8,128)(2,1)S(1)}, bf16[64,128,256]{2,1,0:T(8,128)(2,1)S(1)}, bf16[32,256]{1,0:T(8,128)(2,1)S(1)}, bf16[128,256]{1,0:T(8,128)(2,1)S(1)}) custom-call(s32[4]{0:T(128)S(1)} %copy-done.1, bf16[4,2,32,256]{3,2,1,0:T(8,128)(2,1)S(1)} %pad_maximum_fusion.here_ref, ...), custom_call_target="tpu_custom_call" | custom-call | flops 6710886400 | bytes 5242880 | tf_op jit(solution)/shard_map/pallas_call | solution.py:233
  25.6 0.0 copy-start.3
  25.6 1.6 %collective-permute-done.4.there_ref = bf16[4,2,32,256]{3,2,1,0:T(8,128)(2,1)S(1)} collective-permute-done((bf16[4,2,32,256]{3,2,1,0:T(8,128)(2,1)S(1)}, bf16[4,2,32,256]{3,2,1,0:T(8,128)(2,1)S(1)}, u32[]{:S(2)}, u32[]{:S(2)}) %collective-permute-start.4) | collective-permute-done | bytes 131104 | tf_op jit(solution)/shard_map/ppermute | solution.py:37
  27.2 10.4 %shard_map.75 = (bf16[32,64,256]{2,1,0:T(8,128)(2,1)S(1)}, bf16[64,128,256]{2,1,0:T(8,128)(2,1)S(1)}, bf16[32,256]{1,0:T(8,128)(2,1)S(1)}, bf16[128,256]{1,0:T(8,128)(2,1)S(1)}) custom-call(s32[4]{0:T(128)S(1)} %copy-done.1, bf16[4,2,32,256]{3,2,1,0:T(8,128)(2,1)S(1)} %collective-permute-done.3.here_ref, ...), custom_call_target="tpu_custom_call" | custom-call | flops 6710886400 | bytes 5242880 | tf_op jit(solution)/shard_map/pallas_call | solution.py:233
  37.6 14.1 %shard_map.76 = (bf16[8,128,128]{2,1,0:T(8,128)(2,1)S(1)}, bf16[8,128,128]{2,1,0:T(8,128)(2,1)S(1)}, bf16[16,8,128]{2,1,0:T(8,128)(2,1)S(1)}) custom-call(bf16[32,64,256]{2,1,0:T(8,128)(2,1)S(1)} %get-tuple-element.23.refs_0_.refs_2_, bf16[32,64,256]{2,1,0:T(8,128)(2,1)S(1)} %get-tuple-element.24.refs_1_.refs_3_, ...), custom_call_target="tpu_custom_call" | custom-call | flops 10737418240 | bytes 9437184 | tf_op jit(solution)/shard_map/pallas_call | solution.py:342
  51.8 0.0 copy-start
  51.8 0.0 copy-start.2
  51.8 3.6 %collective-permute-start.5 = (bf16[8,128,128]{2,1,0:T(8,128)(2,1)S(1)}, bf16[8,128,128]{2,1,0:T(8,128)(2,1)S(1)}, u32[]{:S(2)}, u32[]{:S(2)}) collective-permute-start(bf16[8,128,128]{2,1,0:T(8,128)(2,1)S(1)} %get-tuple-element.31.refs_4_), channel_id=1, source_target_pairs={{0,2},{2,4},{4,6},{6,8},{8,10},{10,12},{12,14},{1,3},{3,5},{5,7},{... | collective-permute-start | bytes 786440 | tf_op jit(solution)/shard_map/ppermute | solution.py:537
  55.5 14.1 %shard_map.77 = (bf16[8,128,128]{2,1,0:T(8,128)(2,1)S(1)}, bf16[8,128,128]{2,1,0:T(8,128)(2,1)S(1)}, bf16[16,8,128]{2,1,0:T(8,128)(2,1)S(1)}) custom-call(bf16[32,64,256]{2,1,0:T(8,128)(2,1)S(1)} %get-tuple-element.23.refs_0_.refs_2_, bf16[32,64,256]{2,1,0:T(8,128)(2,1)S(1)} %get-tuple-element.24.refs_1_.refs_3_, ...), custom_call_target="tpu_custom_call" | custom-call | flops 10737418240 | bytes 9437184 | tf_op jit(solution)/shard_map/pallas_call | solution.py:342
  69.6 1.3 %collective-permute-start.6 = (bf16[8,128,128]{2,1,0:T(8,128)(2,1)S(1)}, bf16[8,128,128]{2,1,0:T(8,128)(2,1)S(1)}, u32[]{:S(2)}, u32[]{:S(2)}) collective-permute-start(bf16[8,128,128]{2,1,0:T(8,128)(2,1)S(1)} %get-tuple-element.32.refs_1_), channel_id=1, source_target_pairs={{2,0},{4,2},{6,4},{8,6},{10,8},{12,10},{14,12},{3,1},{5,3},{7,5},{... | collective-permute-start | bytes 786440 | tf_op jit(solution)/shard_map/ppermute | solution.py:538
  71.0 8.1 %collective-permute-done.6.refs_5_ = bf16[8,128,128]{2,1,0:T(8,128)(2,1)S(1)} collective-permute-done((bf16[8,128,128]{2,1,0:T(8,128)(2,1)S(1)}, bf16[8,128,128]{2,1,0:T(8,128)(2,1)S(1)}, u32[]{:S(2)}, u32[]{:S(2)}) %collective-permute-start.6) | collective-permute-done | bytes 262176 | tf_op jit(solution)/shard_map/ppermute | solution.py:538
  79.0 0.1 collective-permute-start.7
  79.1 1.3 %collective-permute-done.7.refs_6_ = bf16[48,8,128]{2,1,0:T(8,128)(2,1)S(1)} collective-permute-done((bf16[48,8,128]{2,1,0:T(8,128)(2,1)S(1)}, bf16[48,8,128]{2,1,0:T(8,128)(2,1)S(1)}, u32[]{:S(2)}, u32[]{:S(2)}) %collective-permute-start.7) | collective-permute-done | bytes 98336 | tf_op jit(solution)/shard_map/ppermute | solution.py:37
  80.4 9.6 %shard_map.78 = bf16[32,128,128]{2,1,0:T(8,128)(2,1)} custom-call(s32[4]{0:T(128)S(1)} %copy-done.2, bf16[8,128,128]{2,1,0:T(8,128)(2,1)S(1)} %collective-permute-done.5.refs_0_, bf16[8,128,128]{2,1,0:T(8,128)(2,1)S(1)} %get-tuple-element.32.refs_1_, bf16[8,128,128]{2,1,0:T(8,128)(2,1)S(1)} %get-tuple-element.33.refs_2_, ...), custom_call_target="tpu_custom_call" | custom-call | tf_op jit(solution)/shard_map/pallas_call | solution.py:486
  (15 shorter events, 0.1 us)
Async XLA Ops:
  0.8 5.0 %collective-permute-start = (bf16[1,2,32,256]{3,2,1,0:T(8,128)(2,1)S(1)}, bf16[1,2,32,256]{3,2,1,0:T(8,128)(2,1)S(1)}, u32[]{:S(2)}, u32[]{:S(2)}) collective-permute-start(bf16[1,2,32,256]{3,2,1,0:T(8,128)(2,1)S(1)} %pad_maximum_fusion.2), channel_id=1, source_target_pairs={{0,4},{2,6},{4,0},{6,2},{8,12},{10,14},{12,8},{14,10},{1,5},{3,7},... | collective-permute-start | bytes 98312 | tf_op jit(solution)/shard_map/ppermute | solution.py:37
  5.8 4.3 %collective-permute-start.1 = (bf16[2,2,32,256]{3,2,1,0:T(8,128)(2,1)S(1)}, bf16[2,2,32,256]{3,2,1,0:T(8,128)(2,1)S(1)}, u32[]{:S(2)}, u32[]{:S(2)}) collective-permute-start(bf16[2,2,32,256]{3,2,1,0:T(8,128)(2,1)S(1)} %pad_maximum_fusion.1), channel_id=1, source_target_pairs={{0,2},{2,0},{4,6},{6,4},{8,10},{10,8},{12,14},{14,12},{1,3},{3,1},... | collective-permute-start | bytes 196616 | tf_op jit(solution)/shard_map/ppermute | solution.py:37
  10.2 4.5 %collective-permute-start.2 = (bf16[4,2,32,256]{3,2,1,0:T(8,128)(2,1)S(1)}, bf16[4,2,32,256]{3,2,1,0:T(8,128)(2,1)S(1)}, u32[]{:S(2)}, u32[]{:S(2)}) collective-permute-start(bf16[4,2,32,256]{3,2,1,0:T(8,128)(2,1)S(1)} %pad_maximum_fusion.here_ref), channel_id=1, source_target_pairs={{0,1},{1,0},{2,3},{3,2},{4,5},{5,4},{6,7},{7,6},{8,9},{9,8},{10,11... | collective-permute-start | bytes 393224 | tf_op jit(solution)/shard_map/ppermute | solution.py:37
  11.5 14.1 %collective-permute-start.3 = (bf16[4,2,32,256]{3,2,1,0:T(8,128)(2,1)S(1)}, bf16[4,2,32,256]{3,2,1,0:T(8,128)(2,1)S(1)}, u32[]{:S(2)}, u32[]{:S(2)}) collective-permute-start(bf16[4,2,32,256]{3,2,1,0:T(8,128)(2,1)S(1)} %pad_maximum_fusion.here_ref), channel_id=1, source_target_pairs={{0,8},{2,10},{4,12},{6,14},{8,0},{10,2},{12,4},{14,6},{1,9},{3,11}... | collective-permute-start | bytes 393224 | tf_op jit(solution)/shard_map/ppermute | solution.py:37
  14.6 12.6 %collective-permute-start.4 = (bf16[4,2,32,256]{3,2,1,0:T(8,128)(2,1)S(1)}, bf16[4,2,32,256]{3,2,1,0:T(8,128)(2,1)S(1)}, u32[]{:S(2)}, u32[]{:S(2)}) collective-permute-start(bf16[4,2,32,256]{3,2,1,0:T(8,128)(2,1)S(1)} %collective-permute-done.2.there_ref), channel_id=1, source_target_pairs={{0,8},{2,10},{4,12},{6,14},{8,0},{10,2},{12,4},{14,6},{1,9},{3,11}... | collective-permute-start | bytes 393224 | tf_op jit(solution)/shard_map/ppermute | solution.py:37
  14.7 0.7 copy-start.1
  25.6 12.0 %copy-start.3 = (bf16[4096,128]{1,0:T(8,128)(2,1)S(1)}, bf16[4096,128]{1,0:T(8,128)(2,1)}, u32[]{:S(2)}) copy-start(bf16[4096,128]{1,0:T(8,128)(2,1)} %param.12) | copy-start | bytes 3145732
  51.8 28.6 %copy-start = (bf16[2,3,3,128,128]{4,3,2,1,0:T(8,128)(2,1)S(1)}, bf16[2,3,3,128,128]{4,3,2,1,0:T(8,128)(2,1)}, u32[]{:S(2)}) copy-start(bf16[2,3,3,128,128]{4,3,2,1,0:T(8,128)(2,1)} %param.13) | copy-start | bytes 1769476
  51.8 28.6 %copy-start.2 = (s32[4]{0:T(128)S(1)}, s32[4]{0:T(128)}, u32[]{:S(2)}) copy-start(s32[4]{0:T(128)} %dilations.5) | copy-start | bytes 52
  51.8 19.1 %collective-permute-start.5 = (bf16[8,128,128]{2,1,0:T(8,128)(2,1)S(1)}, bf16[8,128,128]{2,1,0:T(8,128)(2,1)S(1)}, u32[]{:S(2)}, u32[]{:S(2)}) collective-permute-start(bf16[8,128,128]{2,1,0:T(8,128)(2,1)S(1)} %get-tuple-element.31.refs_4_), channel_id=1, source_target_pairs={{0,2},{2,4},{4,6},{6,8},{8,10},{10,12},{12,14},{1,3},{3,5},{5,7},{... | collective-permute-start | bytes 786440 | tf_op jit(solution)/shard_map/ppermute | solution.py:537
  69.6 9.4 %collective-permute-start.6 = (bf16[8,128,128]{2,1,0:T(8,128)(2,1)S(1)}, bf16[8,128,128]{2,1,0:T(8,128)(2,1)S(1)}, u32[]{:S(2)}, u32[]{:S(2)}) collective-permute-start(bf16[8,128,128]{2,1,0:T(8,128)(2,1)S(1)} %get-tuple-element.32.refs_1_), channel_id=1, source_target_pairs={{2,0},{4,2},{6,4},{8,6},{10,8},{12,10},{14,12},{3,1},{5,3},{7,5},{... | collective-permute-start | bytes 786440 | tf_op jit(solution)/shard_map/ppermute | solution.py:538
  79.0 1.4 %collective-permute-start.7 = (bf16[48,8,128]{2,1,0:T(8,128)(2,1)S(1)}, bf16[48,8,128]{2,1,0:T(8,128)(2,1)S(1)}, u32[]{:S(2)}, u32[]{:S(2)}) collective-permute-start(bf16[48,8,128]{2,1,0:T(8,128)(2,1)S(1)} %fusion), channel_id=1, source_target_pairs={{0,1},{1,0},{2,3},{3,2},{4,5},{5,4},{6,7},{7,6},{8,9},{9,8},{10,11... | collective-permute-start | bytes 294920 | tf_op jit(solution)/shard_map/ppermute | solution.py:37
